TPU v7x, 256 devices: a whole 4x4x8 slice. The times are simulated.
256 devices in a mesh: half: 2 (over y_hi), row: 16 (over z, y_lo), col: 8 (over x, core).
Axes of the slice: x: 4, y: 4 (y_hi: 2, y_lo: 2; y = y_hi * 2 + y_lo), z: 8, core: 2. Of those that a mesh axis runs over, the one named last changes fastest.
Arguments:
- children: bfloat16 [2, 512, 512, 512], P('half', 'row', 'col'), may hold values from -0.01171875 to 0.01171875
- operators: bfloat16 [2, 2, 4, 512, 512], P('half'), may hold values from -1 to 1
- term_site: int32 [2, 5, 2], P('half'), may hold values from 0 to 3
- term_leg: int32 [2, 5], P('half'), may hold values from 0 to 2
- parent: bfloat16 [512, 512, 512], P(('half', 'row', 'col')), may hold values from -6 to 6
Outputs:
- updated: bfloat16 [512, 512, 512], P(('half', 'row', 'col'))
Inputs may be any that keep to these rules, and one draw needn't show every extreme that they name: `term_site`: a site index into the child's operator table of 4 entries. `term_leg`: 0: the term acts on the first leg only, 1: on the second leg only, 2: on both.
All inputs are finite; a program needn't handle non-finite values.
Results may differ from a plain program's by a relative error of at most 0.0064.
Values may be sent and summed in bfloat16 or wider, within the bound.
No kernel may reach another device: no remote copies, remote signals or barrier semaphores. Data moves between devices by JAX's collectives and lax.ppermute only.
A program may use at most 128 MiB of HBM per device.

v0:
```python
import jax
import jax.numpy as jnp
from jax import lax
from jax.experimental import pallas as pl
from jax.experimental.pallas import tpu as pltpu
from jax.sharding import Mesh
from jax.sharding import PartitionSpec as P

BF = jnp.bfloat16
F32 = jnp.float32
NZ, NY, NX, NE = 8, 2, 4, 2
COL = ("x", "e")
ROW = ("z", "y")
ROW_COL = ROW + COL
ALL = ("half",) + ROW_COL
VMEM = pl.BlockSpec(memory_space=pltpu.VMEM)
SMEM = pl.BlockSpec(memory_space=pltpu.SMEM)
LIMIT = pltpu.CompilerParams(vmem_limit_bytes=50 << 20)


def dot(a, b, ca, cb):
    return lax.dot_general(a, b, (((ca,), (cb,)), ((), ())), preferred_element_type=F32)


def swap(value, axes, offset):
    peers = lax.axis_size(axes)
    return lax.ppermute(value, axes, [(i, i ^ offset) for i in range(peers)])


def terms_kernel(me, site, leg, table, *refs):
    blocks, (out_ref, whole, inner, acc) = refs[: NX * NE], refs[NX * NE :]
    col = me[1] * NE + me[0]
    rows = whole.shape[0]
    for k, ref in enumerate(blocks):
        for a in range(rows):
            whole[a, col ^ k] = ref[a]

    def x_of(a):
        return whole[a].reshape(512, 512)

    for term in range(leg.shape[0]):
        code = leg[term]

        @pl.when(code != 0)
        def _():
            right = table[1, site[term, 1]]
            for a in range(rows):
                inner[a] = dot(x_of(a), right, 1, 1).astype(BF)

        @pl.when(code == 0)
        def _():
            for a in range(rows):
                inner[a] = x_of(a)

        @pl.when(code != 1)
        def _():
            left = table[0, site[term, 0]]
            for a in range(rows):
                part = dot(left, inner[a], 1, 0)
                acc[a] = part if term == 0 else acc[a] + part

        @pl.when(code == 1)
        def _():
            for a in range(rows):
                part = inner[a].astype(F32)
                acc[a] = part if term == 0 else acc[a] + part

    for a in range(rows):
        for x in range(NX):
            for e in range(NE):
                at = x * 128 + e * 64
                for y in range(NY):
                    block = acc[a, at : at + 64, y * 256 : (y + 1) * 256]
                    out_ref[:, y, x, a // 2, a % 2, e] = block.astype(BF).reshape(NZ, 8, 256)


def apply_terms(me, site, leg, table, arrived):
    return pl.pallas_call(
        terms_kernel,
        out_shape=jax.ShapeDtypeStruct((NZ, NY, NX, NE, 2, NE, 8, 256), BF),
        in_specs=[SMEM] * 3 + [VMEM] * (1 + NX * NE),
        out_specs=VMEM,
        scratch_shapes=[
            pltpu.VMEM((4, NX * NE, 64, 512), BF),
            pltpu.VMEM((4, 512, 512), BF),
            pltpu.VMEM((4, 512, 512), F32),
        ],
        compiler_params=LIMIT,
        name="terms",
    )(me, site, leg, table, *arrived)


def turn_kernel(in_ref, out_ref):
    out_ref[...] = jnp.swapaxes(in_ref[...], 0, 1)


def turned(value):
    rows, depth, lanes = value.shape
    step = 64
    return pl.pallas_call(
        turn_kernel,
        out_shape=jax.ShapeDtypeStruct((depth, rows, lanes), BF),
        grid=(rows // step,),
        in_specs=[pl.BlockSpec((step, depth, lanes), lambda i: (i, 0, 0))],
        out_specs=pl.BlockSpec((depth, step, lanes), lambda i: (0, i, 0)),
        compiler_params=LIMIT,
        name="turn",
    )(value)


def gram_kernel(me, s_ref, own_ref, other_ref, out_ref, acc):
    e = me[0]
    first = True
    for which, c_ref in enumerate((own_ref, other_ref)):
        block = s_ref[:, :, e if which == 0 else 1 - e]
        block = jnp.swapaxes(block.reshape(256, 8, 256), 0, 1)
        for s in range(8):
            part = dot(block[s], c_ref[s], 1, 1)
            acc[...] = part if first else acc[...] + part
            first = False
    for z in range(NZ):
        for x in range(NX):
            at = (z * NX + x) * 8
            for y in range(NY):
                out_ref[z, y, x] = acc[at : at + 8, y * 256 : (y + 1) * 256].astype(BF)


def gram(me, summed, own, other):
    return pl.pallas_call(
        gram_kernel,
        out_shape=jax.ShapeDtypeStruct((NZ, NY, NX, 8, 256), BF),
        in_specs=[SMEM, VMEM, VMEM, VMEM],
        out_specs=VMEM,
        scratch_shapes=[pltpu.VMEM((256, 512), F32)],
        compiler_params=LIMIT,
        name="gram",
    )(me, summed, own, other)


def final_kernel(me, rows_ref, cols_ref, *refs):
    pieces, (out_ref, env, acc) = refs[: NX * NE], refs[-3:]
    e, x = me[0], me[1]
    for i, ref in enumerate(pieces):
        ke, kx = i % NE, i // NE
        block = (e ^ ke) * 32 + (x ^ kx)
        for half in range(2):
            for z in range(NZ):
                for y in range(NY):
                    env[half, y, block + z * NX] = ref[(half * NZ + z) * NY + y]
    for part in range(2):
        at = slice(part * 256, part * 256 + 256)
        one = env[0, part].reshape(512, 256)
        for c in range(2):
            acc[c, at, :] = dot(one, rows_ref[c], 0, 0)
    for part in range(2):
        at = slice(part * 256, part * 256 + 256)
        two = env[1, part].reshape(512, 256)
        for c in range(2):
            out_ref[c, :, at] = (acc[c, :, at] + dot(cols_ref[c], two, 1, 0)).astype(BF)


def final(me, by_rows, by_cols, pieces):
    return pl.pallas_call(
        final_kernel,
        out_shape=jax.ShapeDtypeStruct((2, 512, 512), BF),
        in_specs=[SMEM] + [VMEM] * (2 + NX * NE),
        out_specs=VMEM,
        scratch_shapes=[
            pltpu.VMEM((2, NY, 64, 8, 256), BF),
            pltpu.VMEM((2, 512, 512), F32),
        ],
        compiler_params=LIMIT,
        name="final",
    )(me, by_rows, by_cols, *pieces)


def reordered(parent):
    wanted = jnp.arange(512).reshape(128, NE, 2).swapaxes(0, 1).reshape(512)
    pick = (jnp.arange(512)[:, None] == wanted[None, :]).astype(BF)
    by_rows = jnp.einsum("aq,cab->cqb", pick, parent, preferred_element_type=F32)
    by_cols = jnp.einsum("cab,bq->caq", parent, pick, preferred_element_type=F32)
    return by_rows.astype(BF), by_cols.astype(BF)


def on_device(children, operators, term_site, term_leg, parent):
    me = jnp.stack([lax.axis_index(a) for a in ("e", "x")]).astype(jnp.int32)
    child = children[0]
    with jax.named_scope("child_rows"):
        cut = child.reshape(32, NZ, 8, NY, 256).transpose(1, 3, 0, 2, 4)
        cut = cut.reshape(NZ * NY, 32 * 8, 256)
        child_all = lax.all_to_all(cut, ROW, 0, 0, tiled=True)
    with jax.named_scope("child_first_leg"):
        col = lax.axis_index(COL)
        blocks = child.reshape(NX * NE, 4, 64, 512)
        arrived = []
        for k in range(NX * NE):
            block = lax.dynamic_index_in_dim(blocks, col ^ k, 0, keepdims=False)
            arrived.append(swap(block, COL, k) if k else block)
    with jax.named_scope("terms"):
        summed = apply_terms(
            me, term_site[0], term_leg[0], operators[0], arrived
        )
    with jax.named_scope("summed_rows"):
        summed = lax.all_to_all(summed.reshape(128, 32, 256), ROW_COL, 0, 0, tiled=True)
    with jax.named_scope("turn"):
        own = turned(child_all.reshape(512, 8, 256))
        other = swap(own, ("e",), 1)
        by_rows, by_cols = reordered(parent)
    with jax.named_scope("gram"):
        part = gram(me, summed.reshape(128, 2, NE, 8, 256), own, other)
    with jax.named_scope("sum"):
        parts = lax.all_to_all(part.reshape(64, 8, 256), ("z", "y", "x"), 0, 0, tiled=True)
        env = jnp.sum(parts.astype(F32), axis=0).astype(BF)
    with jax.named_scope("gather_row"):
        env = jnp.broadcast_to(env, (2 * NZ * NY, 8, 256))
        env = lax.all_to_all(env, ("half",) + ROW, 0, 0, tiled=True)
    with jax.named_scope("gather_x"):
        across = [env] + [swap(env, ("x",), k) for k in range(1, NX)]
    with jax.named_scope("gather_e"):
        pieces = []
        for piece in across:
            pieces += [piece, swap(piece, ("e",), 1)]
    with jax.named_scope("final"):
        return final(me, by_rows, by_cols, pieces)


def solution(mesh):
    torus = Mesh(
        mesh.devices.reshape(2, NZ, NY, NX, NE), ("half", "z", "y", "x", "e")
    )
    in_specs = (
        P("half", ROW, COL, None),
        P("half", None, None, None, None),
        P("half", None, None),
        P("half", None),
        P(ALL, None, None),
    )
    return jax.shard_map(
        on_device, mesh=torus, in_specs=in_specs, out_specs=P(ALL, None, None), check_vma=False
    )
```

profile of v0, /device:TPU:1, one launch (start us, length us, event | category | flops | bytes accessed | tf_op | source)
XLA Modules:
  0.0 177.2 jit_solution(68537547538045620)
XLA Ops:
  0.0 3.2 %copy.11 = bf16[8,2,32,8,256]{4,3,2,1,0:T(8,128)(2,1)} copy(bf16[8,2,32,8,256]{4,3,1,0,2:T(8,128)(2,1)} %bitcast.43) | data formatting | bytes 4194304 | tf_op jit(solution)/shard_map/child_rows/transpose | solution.py:189
  3.2 10.3 %all-to-all-start.1 = ((bf16[16,256,256]{2,1,0:T(8,128)(2,1)}), bf16[16,256,256]{2,1,0:T(8,128)(2,1)}, u32[]{:S(2)}, u32[]{:S(2)}) async-start(bf16[16,256,256]{2,1,0:T(8,128)(2,1)} %bitcast.45), calls=%async_computation.1 | async-start | bytes 4194304 | tf_op jit(solution)/shard_map/child_rows/all_to_all | solution.py:191
  13.6 0.0 copy-start.3
  13.6 0.0 copy-start.1
  13.6 1.1 dynamic-slice_bitcast_fusion
  14.7 1.0 collective-permute-start
  15.6 1.2 collective-permute-start.1
  16.8 0.4 collective-permute-start.2
  17.3 2.7 %collective-permute-start.3 = (bf16[4,64,512]{2,1,0:T(8,128)(2,1)}, bf16[4,64,512]{2,1,0:T(8,128)(2,1)S(1)}, u32[]{:S(2)}, u32[]{:S(2)}) collective-permute-start(bf16[4,64,512]{2,1,0:T(8,128)(2,1)} %get-tuple-element.8), channel_id=1, source_target_pairs={{0,4},{1,5},{2,6},{3,7},{4,0},{5,1},{6,2},{7,3},{8,12},{9,13},{10,... | collective-permute-start | bytes 786440 | tf_op jit(solution)/shard_map/child_first_leg/ppermute | solution.py:27
  20.0 0.6 collective-permute-start.4
  20.6 2.5 %collective-permute-start.5 = (bf16[4,64,512]{2,1,0:T(8,128)(2,1)}, bf16[4,64,512]{2,1,0:T(8,128)(2,1)S(1)}, u32[]{:S(2)}, u32[]{:S(2)}) collective-permute-start(bf16[4,64,512]{2,1,0:T(8,128)(2,1)} %get-tuple-element.6), channel_id=1, source_target_pairs={{0,6},{1,7},{2,4},{3,5},{4,2},{5,3},{6,0},{7,1},{8,14},{9,15},{10,... | collective-permute-start | bytes 786440 | tf_op jit(solution)/shard_map/child_first_leg/ppermute | solution.py:27
  23.1 0.6 collective-permute-done.1.refs_2_
  23.7 3.4 %collective-permute-start.6 = (bf16[4,64,512]{2,1,0:T(8,128)(2,1)}, bf16[4,64,512]{2,1,0:T(8,128)(2,1)S(1)}, u32[]{:S(2)}, u32[]{:S(2)}) collective-permute-start(bf16[4,64,512]{2,1,0:T(8,128)(2,1)} %get-tuple-element.5), channel_id=1, source_target_pairs={{0,7},{1,6},{2,5},{3,4},{4,3},{5,2},{6,1},{7,0},{8,15},{9,14},{10,... | collective-permute-start | bytes 786440 | tf_op jit(solution)/shard_map/child_first_leg/ppermute | solution.py:27
  27.1 0.1 copy.10.site
  27.2 0.1 pad_add_fusion.me
  27.3 2.8 %collective-permute-done.2.refs_3_ = bf16[4,64,512]{2,1,0:T(8,128)(2,1)S(1)} collective-permute-done((bf16[4,64,512]{2,1,0:T(8,128)(2,1)}, bf16[4,64,512]{2,1,0:T(8,128)(2,1)S(1)}, u32[]{:S(2)}, u32[]{:S(2)}) %collective-permute-start.2) | collective-permute-done | bytes 262176 | tf_op jit(solution)/shard_map/child_first_leg/ppermute | solution.py:27
  30.1 7.1 %collective-permute-done.3.refs_4_ = bf16[4,64,512]{2,1,0:T(8,128)(2,1)S(1)} collective-permute-done((bf16[4,64,512]{2,1,0:T(8,128)(2,1)}, bf16[4,64,512]{2,1,0:T(8,128)(2,1)S(1)}, u32[]{:S(2)}, u32[]{:S(2)}) %collective-permute-start.3) | collective-permute-done | bytes 262176 | tf_op jit(solution)/shard_map/child_first_leg/ppermute | solution.py:27
  37.1 5.7 %collective-permute-done.4.refs_5_ = bf16[4,64,512]{2,1,0:T(8,128)(2,1)S(1)} collective-permute-done((bf16[4,64,512]{2,1,0:T(8,128)(2,1)}, bf16[4,64,512]{2,1,0:T(8,128)(2,1)S(1)}, u32[]{:S(2)}, u32[]{:S(2)}) %collective-permute-start.4) | collective-permute-done | bytes 262176 | tf_op jit(solution)/shard_map/child_first_leg/ppermute | solution.py:27
  42.8 4.5 %collective-permute-done.6.refs_7_ = bf16[4,64,512]{2,1,0:T(8,128)(2,1)S(1)} collective-permute-done((bf16[4,64,512]{2,1,0:T(8,128)(2,1)}, bf16[4,64,512]{2,1,0:T(8,128)(2,1)S(1)}, u32[]{:S(2)}, u32[]{:S(2)}) %collective-permute-start.6) | collective-permute-done | bytes 262176 | tf_op jit(solution)/shard_map/child_first_leg/ppermute | solution.py:27
  47.3 13.4 %terms.1 = bf16[8,2,4,2,2,2,8,256]{7,6,5,4,3,2,1,0:T(8,128)(2,1)} custom-call(s32[2]{0:T(128)S(1)} %pad_add_fusion.me, s32[5,2]{1,0:T(8,128)S(1)} %copy.10.site, s32[5]{0:T(128)S(1)} %bitcast.42, bf16[2,4,512,512]{3,2,1,0:T(8,128)(2,1)} %bitcast.47, bf16[4,64,512]{2,1,0:T(8,128)(2,1)S(1)} %get-tuple-element.12.refs_0_, ...), custom_call_target="tpu_custom_call" | custom-call | tf_op jit(solution)/shard_map/terms/terms/pallas_call | solution.py:78
  60.8 1.1 all-to-all-done.1
  61.8 10.5 %all-to-all-start = ((bf16[128,32,256]{2,1,0:T(8,128)(2,1)}), bf16[128,32,256]{2,1,0:T(8,128)(2,1)S(1)}, u32[]{:S(2)}, u32[]{:S(2)}) async-start(bf16[128,32,256]{2,1,0:T(8,128)(2,1)} %bitcast.46), calls=%async_computation | async-start | bytes 4194304 | tf_op jit(solution)/shard_map/summed_rows/all_to_all | solution.py:204
  72.3 5.8 %turn.1.own_ref = bf16[8,512,256]{2,1,0:T(8,128)(2,1)} custom-call(bf16[512,8,256]{2,1,0:T(8,128)(2,1)} %bitcast.22.in_ref), custom_call_target="tpu_custom_call" | custom-call | tf_op jit(solution)/shard_map/turn/turn/pallas_call | solution.py:100
  78.2 0.9 collective-permute-start.7
  79.1 44.6 %all-to-all-done = bf16[128,32,256]{2,1,0:T(8,128)(2,1)S(1)} async-done(((bf16[128,32,256]{2,1,0:T(8,128)(2,1)}), bf16[128,32,256]{2,1,0:T(8,128)(2,1)S(1)}, u32[]{:S(2)}, u32[]{:S(2)}) %all-to-all-start) | async-done | bytes 2097184 | tf_op jit(solution)/shard_map/summed_rows/all_to_all | solution.py:204
  123.7 0.0 collective-permute-done.7.other_ref
  123.7 3.6 %gram.1 = bf16[8,2,4,8,256]{4,3,2,1,0:T(8,128)(2,1)S(1)} custom-call(s32[2]{0:T(128)S(1)} %pad_add_fusion.me, bf16[128,2,2,8,256]{4,3,2,1,0:T(8,128)(2,1)S(1)} %bitcast.40, bf16[8,512,256]{2,1,0:T(8,128)(2,1)} %turn.1.own_ref, bf16[8,512,256]{2,1,0:T(8,128)(2,1)} %collective-permute-done.7.other_ref), custom_call_target="tpu_custom_call" | custom-call | tf_op jit(solution)/shard_map/gram/gram/pallas_call | solution.py:129
  127.3 16.8 %all_to_all.20 = bf16[64,8,256]{2,1,0:T(8,128)(2,1)S(1)} all-to-all(bf16[64,8,256]{2,1,0:T(8,128)(2,1)S(1)} %bitcast.41), channel_id=1, replica_groups=mesh['half'=2,'z'=8,'y'=2,'x'=4,'e'=2] {'z','y','x'}, dimensions={0} | all-to-all | bytes 524288 | tf_op jit(solution)/shard_map/sum/all_to_all | solution.py:212
  144.1 0.1 reduce_sum.12
  144.2 0.7 broadcast_in_dim.4
  144.8 6.6 %all-to-all-start.3 = ((bf16[32,8,256]{2,1,0:T(8,128)(2,1)}), bf16[32,8,256]{2,1,0:T(8,128)(2,1)S(1)}, u32[]{:S(2)}, u32[]{:S(2)}) async-start(bf16[32,8,256]{2,1,0:T(8,128)(2,1)} %broadcast_in_dim.4), calls=%async_computation.3 | async-start | bytes 262144 | tf_op jit(solution)/shard_map/gather_row/all_to_all | solution.py:216
  151.4 0.1 reshape.75
  151.6 9.8 %all-to-all-done.3.refs_0_ = bf16[32,8,256]{2,1,0:T(8,128)(2,1)S(1)} async-done(((bf16[32,8,256]{2,1,0:T(8,128)(2,1)}), bf16[32,8,256]{2,1,0:T(8,128)(2,1)S(1)}, u32[]{:S(2)}, u32[]{:S(2)}) %all-to-all-start.3) | async-done | bytes 131104 | tf_op jit(solution)/shard_map/gather_row/all_to_all | solution.py:216
  161.4 0.4 collective-permute-start.9
  161.7 1.3 collective-permute-start.11
  163.0 2.2 %collective-permute-start.13 = (bf16[32,8,256]{2,1,0:T(8,128)(2,1)S(1)}, bf16[32,8,256]{2,1,0:T(8,128)(2,1)S(1)}, u32[]{:S(2)}, u32[]{:S(2)}) collective-permute-start(bf16[32,8,256]{2,1,0:T(8,128)(2,1)S(1)} %all-to-all-done.3.refs_0_), channel_id=1, source_target_pairs={{0,6},{2,4},{4,2},{6,0},{1,7},{3,5},{5,3},{7,1},{8,14},{10,12},{12... | collective-permute-start | bytes 393224 | tf_op jit(solution)/shard_map/gather_x/ppermute | solution.py:27
  165.2 0.7 fusion.rows_ref
  166.0 3.9 %collective-permute-start.8 = (bf16[32,8,256]{2,1,0:T(8,128)(2,1)S(1)}, bf16[32,8,256]{2,1,0:T(8,128)(2,1)S(1)}, u32[]{:S(2)}, u32[]{:S(2)}) collective-permute-start(bf16[32,8,256]{2,1,0:T(8,128)(2,1)S(1)} %all-to-all-done.3.refs_0_), channel_id=1, source_target_pairs={{0,1},{1,0},{2,3},{3,2},{4,5},{5,4},{6,7},{7,6},{8,9},{9,8},{10,11... | collective-permute-start | bytes 393224 | tf_op jit(solution)/shard_map/gather_e/ppermute | solution.py:27
  169.8 0.0 collective-permute-done.9.refs_2_
  169.8 0.1 collective-permute-start.10
  170.0 1.5 collective-permute-start.12
  171.4 0.0 collective-permute-done.13.refs_6_
  171.4 1.8 %collective-permute-start.14 = (bf16[32,8,256]{2,1,0:T(8,128)(2,1)S(1)}, bf16[32,8,256]{2,1,0:T(8,128)(2,1)S(1)}, u32[]{:S(2)}, u32[]{:S(2)}) collective-permute-start(bf16[32,8,256]{2,1,0:T(8,128)(2,1)S(1)} %collective-permute-done.13.refs_6_), channel_id=1, source_target_pairs={{0,1},{1,0},{2,3},{3,2},{4,5},{5,4},{6,7},{7,6},{8,9},{9,8},{10,11... | collective-permute-start | bytes 393224 | tf_op jit(solution)/shard_map/gather_e/ppermute | solution.py:27
  173.2 0.9 fusion.1.cols_ref
  174.1 0.0 collective-permute-done.8.refs_1_
  174.1 0.0 collective-permute-done.12.refs_5_
  174.2 0.1 collective-permute-done.14.refs_7_
  174.2 2.9 %final.1 = bf16[2,512,512]{2,1,0:T(8,128)(2,1)} custom-call(s32[2]{0:T(128)S(1)} %pad_add_fusion.me, bf16[2,512,512]{2,1,0:T(8,128)(2,1)S(1)} %fusion.rows_ref, bf16[2,512,512]{2,1,0:T(8,128)(2,1)S(1)} %fusion.1.cols_ref, bf16[32,8,256]{2,1,0:T(8,128)(2,1)S(1)} %all-to-all-done.3.refs_0_, bf16[32,8,256]{2,1,0:T(8,128)(2,1)S(1)} %collective-permute-done.8.refs_1_, ...), custom_call_target="tpu_custom_call" | custom-call | tf_op jit(solution)/shard_map/final/final/pallas_call | solution.py:163
  (11 shorter events, 0.0 us)
Async XLA Ops:
  0.0 165.2 %copy-start = (bf16[2,512,512]{2,1,0:T(8,128)(2,1)S(1)}, bf16[2,512,512]{2,1,0:T(8,128)(2,1)}, u32[]{:S(2)}) copy-start(bf16[2,512,512]{2,1,0:T(8,128)(2,1)} %param.9) | copy-start | bytes 3145732
  3.2 10.4 %copy-start.2 = (bf16[1,32,64,512]{3,2,1,0:T(8,128)(2,1)S(1)}, bf16[1,32,64,512]{3,2,1,0:T(8,128)(2,1)}, u32[]{:S(2)}) copy-start(bf16[1,32,64,512]{3,2,1,0:T(8,128)(2,1)} %param.5) | copy-start | bytes 6291460
  3.2 58.6 %all-to-all-start.1 = ((bf16[16,256,256]{2,1,0:T(8,128)(2,1)}), bf16[16,256,256]{2,1,0:T(8,128)(2,1)}, u32[]{:S(2)}, u32[]{:S(2)}) async-start(bf16[16,256,256]{2,1,0:T(8,128)(2,1)} %bitcast.45), calls=%async_computation.1 | async-start | bytes 4194304 | tf_op jit(solution)/shard_map/child_rows/all_to_all | solution.py:191
  13.6 13.5 %copy-start.3 = (s32[1,5,2]{1,2,0:T(2,128)S(1)}, s32[1,5,2]{1,2,0:T(2,128)}, u32[]{:S(2)}) copy-start(s32[1,5,2]{1,2,0:T(2,128)} %param.7) | copy-start | bytes 124
  13.6 33.8 %copy-start.1 = (s32[1,5]{1,0:T(1,128)S(1)}, s32[1,5]{1,0:T(1,128)}, u32[]{:S(2)}) copy-start(s32[1,5]{1,0:T(1,128)} %param.8) | copy-start | bytes 64
  14.7 6.0 %collective-permute-start = (bf16[4,64,512]{2,1,0:T(8,128)(2,1)S(1)}, bf16[4,64,512]{2,1,0:T(8,128)(2,1)S(1)}, u32[]{:S(2)}, u32[]{:S(2)}) collective-permute-start(bf16[4,64,512]{2,1,0:T(8,128)(2,1)S(1)} %get-tuple-element.11), channel_id=1, source_target_pairs={{0,1},{1,0},{2,3},{3,2},{4,5},{5,4},{6,7},{7,6},{8,9},{9,8},{10,11... | collective-permute-start | bytes 786440 | tf_op jit(solution)/shard_map/child_first_leg/ppermute | solution.py:27
  15.6 8.0 %collective-permute-start.1 = (bf16[4,64,512]{2,1,0:T(8,128)(2,1)S(1)}, bf16[4,64,512]{2,1,0:T(8,128)(2,1)S(1)}, u32[]{:S(2)}, u32[]{:S(2)}) collective-permute-start(bf16[4,64,512]{2,1,0:T(8,128)(2,1)S(1)} %get-tuple-element.10), channel_id=1, source_target_pairs={{0,2},{1,3},{2,0},{3,1},{4,6},{5,7},{6,4},{7,5},{8,10},{9,11},{10,... | collective-permute-start | bytes 786440 | tf_op jit(solution)/shard_map/child_first_leg/ppermute | solution.py:27
  16.8 13.2 %collective-permute-start.2 = (bf16[4,64,512]{2,1,0:T(8,128)(2,1)}, bf16[4,64,512]{2,1,0:T(8,128)(2,1)S(1)}, u32[]{:S(2)}, u32[]{:S(2)}) collective-permute-start(bf16[4,64,512]{2,1,0:T(8,128)(2,1)} %get-tuple-element.9), channel_id=1, source_target_pairs={{0,3},{1,2},{2,1},{3,0},{4,7},{5,6},{6,5},{7,4},{8,11},{9,10},{10,... | collective-permute-start | bytes 786440 | tf_op jit(solution)/shard_map/child_first_leg/ppermute | solution.py:27
  17.3 19.9 %collective-permute-start.3 = (bf16[4,64,512]{2,1,0:T(8,128)(2,1)}, bf16[4,64,512]{2,1,0:T(8,128)(2,1)S(1)}, u32[]{:S(2)}, u32[]{:S(2)}) collective-permute-start(bf16[4,64,512]{2,1,0:T(8,128)(2,1)} %get-tuple-element.8), channel_id=1, source_target_pairs={{0,4},{1,5},{2,6},{3,7},{4,0},{5,1},{6,2},{7,3},{8,12},{9,13},{10,... | collective-permute-start | bytes 786440 | tf_op jit(solution)/shard_map/child_first_leg/ppermute | solution.py:27
  20.0 22.8 %collective-permute-start.4 = (bf16[4,64,512]{2,1,0:T(8,128)(2,1)}, bf16[4,64,512]{2,1,0:T(8,128)(2,1)S(1)}, u32[]{:S(2)}, u32[]{:S(2)}) collective-permute-start(bf16[4,64,512]{2,1,0:T(8,128)(2,1)} %get-tuple-element.7), channel_id=1, source_target_pairs={{0,5},{1,4},{2,7},{3,6},{4,1},{5,0},{6,3},{7,2},{8,13},{9,12},{10,... | collective-permute-start | bytes 786440 | tf_op jit(solution)/shard_map/child_first_leg/ppermute | solution.py:27
  20.6 22.2 %collective-permute-start.5 = (bf16[4,64,512]{2,1,0:T(8,128)(2,1)}, bf16[4,64,512]{2,1,0:T(8,128)(2,1)S(1)}, u32[]{:S(2)}, u32[]{:S(2)}) collective-permute-start(bf16[4,64,512]{2,1,0:T(8,128)(2,1)} %get-tuple-element.6), channel_id=1, source_target_pairs={{0,6},{1,7},{2,4},{3,5},{4,2},{5,3},{6,0},{7,1},{8,14},{9,15},{10,... | collective-permute-start | bytes 786440 | tf_op jit(solution)/shard_map/child_first_leg/ppermute | solution.py:27
  23.7 23.7 %collective-permute-start.6 = (bf16[4,64,512]{2,1,0:T(8,128)(2,1)}, bf16[4,64,512]{2,1,0:T(8,128)(2,1)S(1)}, u32[]{:S(2)}, u32[]{:S(2)}) collective-permute-start(bf16[4,64,512]{2,1,0:T(8,128)(2,1)} %get-tuple-element.5), channel_id=1, source_target_pairs={{0,7},{1,6},{2,5},{3,4},{4,3},{5,2},{6,1},{7,0},{8,15},{9,14},{10,... | collective-permute-start | bytes 786440 | tf_op jit(solution)/shard_map/child_first_leg/ppermute | solution.py:27
  61.8 61.8 %all-to-all-start = ((bf16[128,32,256]{2,1,0:T(8,128)(2,1)}), bf16[128,32,256]{2,1,0:T(8,128)(2,1)S(1)}, u32[]{:S(2)}, u32[]{:S(2)}) async-start(bf16[128,32,256]{2,1,0:T(8,128)(2,1)} %bitcast.46), calls=%async_computation | async-start | bytes 4194304 | tf_op jit(solution)/shard_map/summed_rows/all_to_all | solution.py:204
  78.2 45.5 %collective-permute-start.7 = (bf16[8,512,256]{2,1,0:T(8,128)(2,1)}, bf16[8,512,256]{2,1,0:T(8,128)(2,1)}, u32[]{:S(2)}, u32[]{:S(2)}) collective-permute-start(bf16[8,512,256]{2,1,0:T(8,128)(2,1)} %turn.1.own_ref), channel_id=1, source_target_pairs={{0,1},{1,0},{2,3},{3,2},{4,5},{5,4},{6,7},{7,6},{8,9},{9,8},{10,11... | collective-permute-start | bytes 6291464 | tf_op jit(solution)/shard_map/turn/ppermute | solution.py:27
  144.8 16.5 %all-to-all-start.3 = ((bf16[32,8,256]{2,1,0:T(8,128)(2,1)}), bf16[32,8,256]{2,1,0:T(8,128)(2,1)S(1)}, u32[]{:S(2)}, u32[]{:S(2)}) async-start(bf16[32,8,256]{2,1,0:T(8,128)(2,1)} %broadcast_in_dim.4), calls=%async_computation.3 | async-start | bytes 262144 | tf_op jit(solution)/shard_map/gather_row/all_to_all | solution.py:216
  161.4 8.5 %collective-permute-start.9 = (bf16[32,8,256]{2,1,0:T(8,128)(2,1)S(1)}, bf16[32,8,256]{2,1,0:T(8,128)(2,1)S(1)}, u32[]{:S(2)}, u32[]{:S(2)}) collective-permute-start(bf16[32,8,256]{2,1,0:T(8,128)(2,1)S(1)} %all-to-all-done.3.refs_0_), channel_id=1, source_target_pairs={{0,2},{2,0},{4,6},{6,4},{1,3},{3,1},{5,7},{7,5},{8,10},{10,8},{12,... | collective-permute-start | bytes 393224 | tf_op jit(solution)/shard_map/gather_x/ppermute | solution.py:27
  161.7 8.2 %collective-permute-start.11 = (bf16[32,8,256]{2,1,0:T(8,128)(2,1)S(1)}, bf16[32,8,256]{2,1,0:T(8,128)(2,1)S(1)}, u32[]{:S(2)}, u32[]{:S(2)}) collective-permute-start(bf16[32,8,256]{2,1,0:T(8,128)(2,1)S(1)} %all-to-all-done.3.refs_0_), channel_id=1, source_target_pairs={{0,4},{2,6},{4,0},{6,2},{1,5},{3,7},{5,1},{7,3},{8,12},{10,14},{12... | collective-permute-start | bytes 393224 | tf_op jit(solution)/shard_map/gather_x/ppermute | solution.py:27
  163.0 8.4 %collective-permute-start.13 = (bf16[32,8,256]{2,1,0:T(8,128)(2,1)S(1)}, bf16[32,8,256]{2,1,0:T(8,128)(2,1)S(1)}, u32[]{:S(2)}, u32[]{:S(2)}) collective-permute-start(bf16[32,8,256]{2,1,0:T(8,128)(2,1)S(1)} %all-to-all-done.3.refs_0_), channel_id=1, source_target_pairs={{0,6},{2,4},{4,2},{6,0},{1,7},{3,5},{5,3},{7,1},{8,14},{10,12},{12... | collective-permute-start | bytes 393224 | tf_op jit(solution)/shard_map/gather_x/ppermute | solution.py:27
  166.0 8.1 %collective-permute-start.8 = (bf16[32,8,256]{2,1,0:T(8,128)(2,1)S(1)}, bf16[32,8,256]{2,1,0:T(8,128)(2,1)S(1)}, u32[]{:S(2)}, u32[]{:S(2)}) collective-permute-start(bf16[32,8,256]{2,1,0:T(8,128)(2,1)S(1)} %all-to-all-done.3.refs_0_), channel_id=1, source_target_pairs={{0,1},{1,0},{2,3},{3,2},{4,5},{5,4},{6,7},{7,6},{8,9},{9,8},{10,11... | collective-permute-start | bytes 393224 | tf_op jit(solution)/shard_map/gather_e/ppermute | solution.py:27
  169.8 4.3 %collective-permute-start.10 = (bf16[32,8,256]{2,1,0:T(8,128)(2,1)S(1)}, bf16[32,8,256]{2,1,0:T(8,128)(2,1)S(1)}, u32[]{:S(2)}, u32[]{:S(2)}) collective-permute-start(bf16[32,8,256]{2,1,0:T(8,128)(2,1)S(1)} %collective-permute-done.9.refs_2_), channel_id=1, source_target_pairs={{0,1},{1,0},{2,3},{3,2},{4,5},{5,4},{6,7},{7,6},{8,9},{9,8},{10,11... | collective-permute-start | bytes 393224 | tf_op jit(solution)/shard_map/gather_e/ppermute | solution.py:27
  170.0 4.2 %collective-permute-start.12 = (bf16[32,8,256]{2,1,0:T(8,128)(2,1)S(1)}, bf16[32,8,256]{2,1,0:T(8,128)(2,1)S(1)}, u32[]{:S(2)}, u32[]{:S(2)}) collective-permute-start(bf16[32,8,256]{2,1,0:T(8,128)(2,1)S(1)} %collective-permute-done.11.refs_4_), channel_id=1, source_target_pairs={{0,1},{1,0},{2,3},{3,2},{4,5},{5,4},{6,7},{7,6},{8,9},{9,8},{10,11... | collective-permute-start | bytes 393224 | tf_op jit(solution)/shard_map/gather_e/ppermute | solution.py:27
  171.4 2.8 %collective-permute-start.14 = (bf16[32,8,256]{2,1,0:T(8,128)(2,1)S(1)}, bf16[32,8,256]{2,1,0:T(8,128)(2,1)S(1)}, u32[]{:S(2)}, u32[]{:S(2)}) collective-permute-start(bf16[32,8,256]{2,1,0:T(8,128)(2,1)S(1)} %collective-permute-done.13.refs_6_), channel_id=1, source_target_pairs={{0,1},{1,0},{2,3},{3,2},{4,5},{5,4},{6,7},{7,6},{8,9},{9,8},{10,11... | collective-permute-start | bytes 393224 | tf_op jit(solution)/shard_map/gather_e/ppermute | solution.py:27
where the time goes:
time: 178 us; the launch traced here: 177 us
  waiting for transfers between devices  76.2 us (43%)
  starting transfers between devices  51.2 us (29%)
  Pallas kernels  25.8 us (14%)
  blocking collectives  16.8 us (9%)
  local copies, waits for them, and re-layouts  5.18 us (3%)
    all_to_all x1, waiting for transfers between devices, on_device(): lax.all_to_all(summed.reshape(128, 32, 256), ROW_COL, 0, 0, tiled=True)  44.6 us
    ppermute x15, starting transfers between devices, swap(): return lax.ppermute(value, axes, [(i, i ^ offset) for i in range(peers)])  23.8 us
    ppermute x15, waiting for transfers between devices, swap(): return lax.ppermute(value, axes, [(i, i ^ offset) for i in range(peers)])  20.7 us
    all_to_all x1, blocking collectives, on_device(): lax.all_to_all(part.reshape(64, 8, 256), ('z', 'y', 'x'), 0, 0, tiled=True)  16.8 us
    pallas_call x1, Pallas kernels, apply_terms(): pl.pallas_call(terms_kernel, out_shape=jax.ShapeDtypeStruct((NZ, NY, NX,...  13.4 us
    all_to_all x1, starting transfers between devices, on_device(): lax.all_to_all(summed.reshape(128, 32, 256), ROW_COL, 0, 0, tiled=True)  10.5 us
    all_to_all x1, starting transfers between devices, on_device(): child_all = lax.all_to_all(cut, ROW, 0, 0, tiled=True)  10.3 us
    all_to_all x1, waiting for transfers between devices, on_device(): env = lax.all_to_all(env, ('half',) + ROW, 0, 0, tiled=True)  9.79 us
  transfers between devices with their start and end apart: 18, of which 9 were waited for; matrix products, arithmetic and copies ran while one was open for 2% of the time, Pallas kernels for 11%

commit v1 on v0

--- a/solution.py
+++ b/solution.py
@@ -27,16 +27,15 @@
     return lax.ppermute(value, axes, [(i, i ^ offset) for i in range(peers)])
 
 
-def terms_kernel(me, site, leg, table, *refs):
-    blocks, (out_ref, whole, inner, acc) = refs[: NX * NE], refs[NX * NE :]
-    col = me[1] * NE + me[0]
-    rows = whole.shape[0]
-    for k, ref in enumerate(blocks):
-        for a in range(rows):
-            whole[a, col ^ k] = ref[a]
+def turn_z(value, offset):
+    return lax.ppermute(value, ("z",), [(i, (i + offset) % NZ) for i in range(NZ)]) if offset else value
+
+
+def terms_kernel(site, leg, table, x_ref, out_ref, inner, acc):
+    rows = x_ref.shape[1]
 
     def x_of(a):
-        return whole[a].reshape(512, 512)
+        return x_ref[:, a].reshape(512, 512)
 
     for term in range(leg.shape[0]):
         code = leg[term]
@@ -74,38 +73,39 @@
                     out_ref[:, y, x, a // 2, a % 2, e] = block.astype(BF).reshape(NZ, 8, 256)
 
 
-def apply_terms(me, site, leg, table, arrived):
+def apply_terms(site, leg, table, arrived):
     return pl.pallas_call(
         terms_kernel,
         out_shape=jax.ShapeDtypeStruct((NZ, NY, NX, NE, 2, NE, 8, 256), BF),
-        in_specs=[SMEM] * 3 + [VMEM] * (1 + NX * NE),
-        out_specs=VMEM,
-        scratch_shapes=[
-            pltpu.VMEM((4, NX * NE, 64, 512), BF),
-            pltpu.VMEM((4, 512, 512), BF),
-            pltpu.VMEM((4, 512, 512), F32),
-        ],
-        compiler_params=LIMIT,
+        in_specs=[SMEM, SMEM, VMEM, VMEM],
+        out_specs=VMEM,
+        scratch_shapes=[pltpu.VMEM((4, 512, 512), BF), pltpu.VMEM((4, 512, 512), F32)],
+        compiler_params=LIMIT,
+        cost_estimate=pl.CostEstimate(flops=8 * 5 * 2 * 512**3, transcendentals=0, bytes_accessed=8 << 20),
         name="terms",
-    )(me, site, leg, table, *arrived)
-
-
-def turn_kernel(in_ref, out_ref):
-    out_ref[...] = jnp.swapaxes(in_ref[...], 0, 1)
-
-
-def turned(value):
-    rows, depth, lanes = value.shape
-    step = 64
+    )(site, leg, table, arrived)
+
+
+SHIFTS = (4, 3, 5, 2, 6, 1, 7, 0)
+
+
+def turn_kernel(me, *refs):
+    blocks, out_ref = refs[:-1], refs[-1]
+    z, y = me[2], me[3]
+    for i, ref in enumerate(blocks):
+        source = lax.rem(z + NZ - SHIFTS[i % NZ], NZ) * NY + (y ^ (i // NZ))
+        out_ref[:, pl.ds(pl.multiple_of(source * 32, 32), 32), :] = jnp.swapaxes(ref[...], 0, 1)
+
+
+def turned(me, blocks):
     return pl.pallas_call(
         turn_kernel,
-        out_shape=jax.ShapeDtypeStruct((depth, rows, lanes), BF),
-        grid=(rows // step,),
-        in_specs=[pl.BlockSpec((step, depth, lanes), lambda i: (i, 0, 0))],
-        out_specs=pl.BlockSpec((depth, step, lanes), lambda i: (0, i, 0)),
+        out_shape=jax.ShapeDtypeStruct((8, 512, 256), BF),
+        in_specs=[SMEM] + [VMEM] * len(blocks),
+        out_specs=VMEM,
         compiler_params=LIMIT,
         name="turn",
-    )(value)
+    )(me, *blocks)
 
 
 def gram_kernel(me, s_ref, own_ref, other_ref, out_ref, acc):
@@ -183,27 +183,33 @@
 
 
 def on_device(children, operators, term_site, term_leg, parent):
-    me = jnp.stack([lax.axis_index(a) for a in ("e", "x")]).astype(jnp.int32)
+    me = jnp.stack([lax.axis_index(a) for a in ("e", "x", "z", "y")]).astype(jnp.int32)
     child = children[0]
+    with jax.named_scope("child_first_leg"):
+        whole = lax.all_to_all(child.reshape(NX * NE, 4 * 64, 512), COL, 0, 0, tiled=True)
     with jax.named_scope("child_rows"):
-        cut = child.reshape(32, NZ, 8, NY, 256).transpose(1, 3, 0, 2, 4)
-        cut = cut.reshape(NZ * NY, 32 * 8, 256)
-        child_all = lax.all_to_all(cut, ROW, 0, 0, tiled=True)
-    with jax.named_scope("child_first_leg"):
-        col = lax.axis_index(COL)
-        blocks = child.reshape(NX * NE, 4, 64, 512)
-        arrived = []
-        for k in range(NX * NE):
-            block = lax.dynamic_index_in_dim(blocks, col ^ k, 0, keepdims=False)
-            arrived.append(swap(block, COL, k) if k else block)
+        z, y = lax.axis_index("z"), lax.axis_index("y")
+        cut = child.reshape(32, NZ, 8, NY * 256)
+
+        def cut_for(shift, which):
+            start = (0, lax.rem(z + shift, NZ), 0, which * 256)
+            return lax.dynamic_slice(cut, start, (32, 1, 8, 256)).reshape(32, 8, 256)
+
+        near, far = [], []
+        for group in (SHIFTS[:4], SHIFTS[4:]):
+            held = swap(jnp.stack([cut_for(shift, y ^ 1) for shift in group]), ("y",), 1)
+            near += [turn_z(cut_for(shift, y), shift) for shift in group]
+            far += [turn_z(held[i], shift) for i, shift in enumerate(group)]
+        blocks = near + far
     with jax.named_scope("terms"):
         summed = apply_terms(
-            me, term_site[0], term_leg[0], operators[0], arrived
+            term_site[0], term_leg[0], operators[0], whole.reshape(NX * NE, 4, 64, 512)
         )
     with jax.named_scope("summed_rows"):
+        summed, blocks = lax.optimization_barrier((summed, blocks))
         summed = lax.all_to_all(summed.reshape(128, 32, 256), ROW_COL, 0, 0, tiled=True)
     with jax.named_scope("turn"):
-        own = turned(child_all.reshape(512, 8, 256))
+        own = turned(me, blocks)
         other = swap(own, ("e",), 1)
         by_rows, by_cols = reordered(parent)
     with jax.named_scope("gram"):

time: 178 us -> 188 us (1.056)
  waiting for transfers between devices: 76.2 us -> 52.3 us
  starting transfers between devices: 51.2 us -> 74.2 us
  local copies, waits for them, and re-layouts: 5.18 us -> 19.8 us
  Pallas kernels: 25.8 us -> 21.8 us
    ppermute x0 -> x14, starting transfers between devices: none -> 32.3 us  [turn_z(): lax.ppermute(value, ('z',), [(i, (i + offset) % NZ) for i in range(NZ)])]
    unnamed x8 -> x64, local copies, waits for them, and re-layouts: 0.02 us -> 16.4 us
    ppermute x15 -> x10, waiting for transfers between devices: 20.7 us -> 6.41 us  [swap(): return lax.ppermute(value, axes, [(i, i ^ offset) for i in range(peers)])]
    all_to_all x1, waiting for transfers between devices: 44.6 us -> 32.1 us  [on_device(): lax.all_to_all(summed.reshape(128, 32, 256), ROW_COL, 0, 0, tiled=True)]
    ppermute x15 -> x10, starting transfers between devices: 23.8 us -> 13.5 us  [swap(): return lax.ppermute(value, axes, [(i, i ^ offset) for i in range(peers)])]
    ppermute x0 -> x14, waiting for transfers between devices: none -> 4 us  [turn_z(): lax.ppermute(value, ('z',), [(i, (i + offset) % NZ) for i in range(NZ)])]
    pallas_call x1, Pallas kernels: 5.83 us -> 2.4 us  [turned(): pl.pallas_call(turn_kernel, out_shape=jax.ShapeDtypeStruct((8, 512, 256),...]
    transpose x1 -> x0, local copies, waits for them, and re-layouts: 3.19 us -> none  [on_device(): cut = child.reshape(32, NZ, 8, NY, 256).transpose(1, 3, 0, 2, 4)]
  transfers between devices with their start and end apart: 18 -> 27, of which waited for: 9 -> 9; matrix products, arithmetic and copies ran while one was open for 2% -> 3% of each run, Pallas kernels for 11% -> 8%
where the time goes in v1:
time: 188 us
  starting transfers between devices  74.2 us (39%)
  waiting for transfers between devices  52.3 us (28%)
  Pallas kernels  21.8 us (12%)
  local copies, waits for them, and re-layouts  19.8 us (11%)
  blocking collectives  16.8 us (9%)
    ppermute x14, starting transfers between devices, turn_z(): lax.ppermute(value, ('z',), [(i, (i + offset) % NZ) for i in range(NZ)])  32.3 us
    all_to_all x1, waiting for transfers between devices, on_device(): lax.all_to_all(summed.reshape(128, 32, 256), ROW_COL, 0, 0, tiled=True)  32.1 us
    all_to_all x1, blocking collectives, on_device(): lax.all_to_all(part.reshape(64, 8, 256), ('z', 'y', 'x'), 0, 0, tiled=True)  16.8 us
    unnamed x64, local copies, waits for them, and re-layouts  16.4 us
    ppermute x10, starting transfers between devices, swap(): return lax.ppermute(value, axes, [(i, i ^ offset) for i in range(peers)])  13.5 us
    all_to_all x1, starting transfers between devices, on_device(): lax.all_to_all(summed.reshape(128, 32, 256), ROW_COL, 0, 0, tiled=True)  13.2 us
    pallas_call x1, Pallas kernels, apply_terms(): pl.pallas_call(terms_kernel, out_shape=jax.ShapeDtypeStruct((NZ, NY, NX,...  12.8 us
    all_to_all x1, waiting for transfers between devices, on_device(): env = lax.all_to_all(env, ('half',) + ROW, 0, 0, tiled=True)  9.79 us
  transfers between devices with their start and end apart: 27, of which 9 were waited for; matrix products, arithmetic and copies ran while one was open for 3% of the time, Pallas kernels for 8%

profile of v1, /device:TPU:1, one launch (start us, length us, event | category | flops | bytes accessed | tf_op | source)
XLA Modules:
  0.0 187.8 jit_solution(9395332138658360361)
XLA Ops:
  0.0 7.7 %all-to-all-start = ((bf16[8,256,512]{2,1,0:T(8,128)(2,1)}), bf16[8,256,512]{2,1,0:T(8,128)(2,1)}, u32[]{:S(2)}, u32[]{:S(2)}) async-start(bf16[8,256,512]{2,1,0:T(8,128)(2,1)} %bitcast.107), calls=%async_computation | async-start | bytes 4194304 | tf_op jit(solution)/shard_map/child_first_leg/all_to_all | solution.py:189
  7.8 1.1 dynamic-slice_bitcast_fusion.3
  9.8 1.5 collective-permute-start.7
  11.3 5.2 %collective-permute-start = (bf16[32,8,256]{2,1,0:T(8,128)(2,1)}, bf16[32,8,256]{2,1,0:T(8,128)(2,1)S(1)}, u32[]{:S(2)}, u32[]{:S(2)}) collective-permute-start(bf16[32,8,256]{2,1,0:T(8,128)(2,1)} %get-tuple-element.53), channel_id=1, source_target_pairs={{0,64},{16,80},{32,96},{48,112},{64,0},{80,16},{96,32},{112,48},{1... | collective-permute-start | bytes 393224 | tf_op jit(solution)/shard_map/child_rows/ppermute | solution.py:31
  16.6 1.6 collective-permute-start.1
  18.2 2.8 %collective-permute-start.2 = (bf16[32,8,256]{2,1,0:T(8,128)(2,1)}, bf16[32,8,256]{2,1,0:T(8,128)(2,1)S(1)}, u32[]{:S(2)}, u32[]{:S(2)}) collective-permute-start(bf16[32,8,256]{2,1,0:T(8,128)(2,1)} %get-tuple-element.51), channel_id=1, source_target_pairs={{0,80},{16,96},{32,112},{48,0},{64,16},{80,32},{96,48},{112,64},{1... | collective-permute-start | bytes 393224 | tf_op jit(solution)/shard_map/child_rows/ppermute | solution.py:31
  21.1 2.2 %collective-permute-done.12 = bf16[4,32,8,256]{3,2,1,0:T(8,128)(2,1)S(1)} collective-permute-done((bf16[4,32,8,256]{3,2,1,0:T(8,128)(2,1)}, bf16[4,32,8,256]{3,2,1,0:T(8,128)(2,1)S(1)}, u32[]{:S(2)}, u32[]{:S(2)}) %collective-permute-start.12) | collective-permute-done | bytes 524320 | tf_op jit(solution)/shard_map/child_rows/ppermute | solution.py:27
  23.3 1.4 collective-permute-start.3
  25.4 3.0 %collective-permute-start.4 = (bf16[32,8,256]{2,1,0:T(8,128)(2,1)}, bf16[32,8,256]{2,1,0:T(8,128)(2,1)S(1)}, u32[]{:S(2)}, u32[]{:S(2)}) collective-permute-start(bf16[32,8,256]{2,1,0:T(8,128)(2,1)} %get-tuple-element.49), channel_id=1, source_target_pairs={{0,96},{16,112},{32,0},{48,16},{64,32},{80,48},{96,64},{112,80},{1... | collective-permute-start | bytes 393224 | tf_op jit(solution)/shard_map/child_rows/ppermute | solution.py:31
  28.4 2.2 %collective-permute-done.1.refs_1_ = bf16[32,8,256]{2,1,0:T(8,128)(2,1)S(1)} collective-permute-done((bf16[32,8,256]{2,1,0:T(8,128)(2,1)}, bf16[32,8,256]{2,1,0:T(8,128)(2,1)S(1)}, u32[]{:S(2)}, u32[]{:S(2)}) %collective-permute-start.1) | collective-permute-done | bytes 131104 | tf_op jit(solution)/shard_map/child_rows/ppermute | solution.py:31
  30.7 1.4 collective-permute-start.5
  32.1 1.3 collective-permute-start.6
  33.3 1.0 collective-permute-done.3.refs_3_
  34.3 2.1 %collective-permute-start.13 = (bf16[32,8,256]{2,1,0:T(8,128)(2,1)S(1)}, bf16[32,8,256]{2,1,0:T(8,128)(2,1)S(1)}, u32[]{:S(2)}, u32[]{:S(2)}) collective-permute-start(bf16[32,8,256]{2,1,0:T(8,128)(2,1)S(1)} %get-tuple-element.58), channel_id=1, source_target_pairs={{0,96},{16,112},{32,0},{48,16},{64,32},{80,48},{96,64},{112,80},{1... | collective-permute-start | bytes 393224 | tf_op jit(solution)/shard_map/child_rows/ppermute | solution.py:31
  36.4 2.2 %collective-permute-start.14 = (bf16[32,8,256]{2,1,0:T(8,128)(2,1)S(1)}, bf16[32,8,256]{2,1,0:T(8,128)(2,1)S(1)}, u32[]{:S(2)}, u32[]{:S(2)}) collective-permute-start(bf16[32,8,256]{2,1,0:T(8,128)(2,1)S(1)} %get-tuple-element.57), channel_id=1, source_target_pairs={{0,16},{16,32},{32,48},{48,64},{64,80},{80,96},{96,112},{112,0},{1... | collective-permute-start | bytes 393224 | tf_op jit(solution)/shard_map/child_rows/ppermute | solution.py:31
  39.3 2.6 %collective-permute-start.15 = (bf16[32,8,256]{2,1,0:T(8,128)(2,1)}, bf16[32,8,256]{2,1,0:T(8,128)(2,1)S(1)}, u32[]{:S(2)}, u32[]{:S(2)}) collective-permute-start(bf16[32,8,256]{2,1,0:T(8,128)(2,1)} %get-tuple-element.56), channel_id=1, source_target_pairs={{0,112},{16,0},{32,16},{48,32},{64,48},{80,64},{96,80},{112,96},{1... | collective-permute-start | bytes 393224 | tf_op jit(solution)/shard_map/child_rows/ppermute | solution.py:31
  41.9 2.5 %collective-permute-start.10 = (bf16[32,8,256]{2,1,0:T(8,128)(2,1)}, bf16[32,8,256]{2,1,0:T(8,128)(2,1)S(1)}, u32[]{:S(2)}, u32[]{:S(2)}) collective-permute-start(bf16[32,8,256]{2,1,0:T(8,128)(2,1)} %get-tuple-element.60), channel_id=1, source_target_pairs={{0,80},{16,96},{32,112},{48,0},{64,16},{80,32},{96,48},{112,64},{1... | collective-permute-start | bytes 393224 | tf_op jit(solution)/shard_map/child_rows/ppermute | solution.py:31
  44.4 1.0 collective-permute-start.11
  45.4 2.3 %collective-permute-start.8 = (bf16[32,8,256]{2,1,0:T(8,128)(2,1)S(1)}, bf16[32,8,256]{2,1,0:T(8,128)(2,1)S(1)}, u32[]{:S(2)}, u32[]{:S(2)}) collective-permute-start(bf16[32,8,256]{2,1,0:T(8,128)(2,1)S(1)} %get-tuple-element.62), channel_id=1, source_target_pairs={{0,64},{16,80},{32,96},{48,112},{64,0},{80,16},{96,32},{112,48},{1... | collective-permute-start | bytes 393224 | tf_op jit(solution)/shard_map/child_rows/ppermute | solution.py:31
  47.8 2.9 %collective-permute-start.9 = (bf16[32,8,256]{2,1,0:T(8,128)(2,1)S(1)}, bf16[32,8,256]{2,1,0:T(8,128)(2,1)S(1)}, u32[]{:S(2)}, u32[]{:S(2)}) collective-permute-start(bf16[32,8,256]{2,1,0:T(8,128)(2,1)S(1)} %get-tuple-element.61), channel_id=1, source_target_pairs={{0,48},{16,64},{32,80},{48,96},{64,112},{80,0},{96,16},{112,32},{1... | collective-permute-start | bytes 393224 | tf_op jit(solution)/shard_map/child_rows/ppermute | solution.py:31
  50.6 12.8 %terms.1 = bf16[8,2,4,2,2,2,8,256]{7,6,5,4,3,2,1,0:T(8,128)(2,1)S(1)} custom-call(s32[5,2]{1,0:T(8,128)S(1)} %copy.25.site, s32[5]{0:T(128)S(1)} %bitcast.106, bf16[2,4,512,512]{3,2,1,0:T(8,128)(2,1)} %bitcast.110, bf16[8,4,64,512]{3,2,1,0:T(8,128)(2,1)} %bitcast.11.x_ref), custom_call_target="tpu_custom_call" | custom-call | flops 10737418240 | bytes 8388608 | tf_op jit(solution)/shard_map/terms/terms/pallas_call | solution.py:77
  63.6 1.3 copy-done.1
  69.0 13.2 %all-to-all-start.1 = ((bf16[128,32,256]{2,1,0:T(8,128)(2,1)}), bf16[128,32,256]{2,1,0:T(8,128)(2,1)S(1)}, u32[]{:S(2)}, u32[]{:S(2)}) async-start(bf16[128,32,256]{2,1,0:T(8,128)(2,1)} %bitcast.104), calls=%async_computation.1 | async-start | bytes 4194304 | tf_op jit(solution)/shard_map/summed_rows/all_to_all | solution.py:210
  82.2 0.9 copy-done.3
  83.1 0.9 copy-done.5
  84.0 0.9 copy-done.7
  84.9 0.9 copy-done.9
  85.8 0.9 copy-done.11
  86.7 0.9 copy-done.13
  87.7 0.9 copy-done.15
  88.6 0.9 copy-done.17
  89.5 0.9 copy-done.19
  90.4 0.9 copy-done.21
  91.3 0.9 copy-done.23
  93.1 0.9 copy-done.27
  94.0 2.4 %turn.1.own_ref = bf16[8,512,256]{2,1,0:T(8,128)(2,1)} custom-call(s32[4]{0:T(128)S(1)} %pad_add_fusion.me, bf16[32,8,256]{2,1,0:T(8,128)(2,1)S(1)} %collective-permute-done.refs_0_, bf16[32,8,256]{2,1,0:T(8,128)(2,1)S(1)} %copy-done.3, bf16[32,8,256]{2,1,0:T(8,128)(2,1)S(1)} %copy-done.5, bf16[32,8,256]{2,1,0:T(8,128)(2,1)S(1)} %copy-done.7, ...), custom_call_target="tpu_custom_call" | custom-call | tf_op jit(solution)/shard_map/turn/turn/pallas_call | solution.py:101
  97.3 4.1 %collective-permute-done.16.other_ref = bf16[8,512,256]{2,1,0:T(8,128)(2,1)} collective-permute-done((bf16[8,512,256]{2,1,0:T(8,128)(2,1)}, bf16[8,512,256]{2,1,0:T(8,128)(2,1)}, u32[]{:S(2)}, u32[]{:S(2)}) %collective-permute-start.16) | collective-permute-done | bytes 2097184 | tf_op jit(solution)/shard_map/turn/ppermute | solution.py:27
  101.4 32.1 %all-to-all-done.1 = bf16[128,32,256]{2,1,0:T(8,128)(2,1)S(1)} async-done(((bf16[128,32,256]{2,1,0:T(8,128)(2,1)}), bf16[128,32,256]{2,1,0:T(8,128)(2,1)S(1)}, u32[]{:S(2)}, u32[]{:S(2)}) %all-to-all-start.1) | async-done | bytes 2097184 | tf_op jit(solution)/shard_map/summed_rows/all_to_all | solution.py:210
  133.5 3.6 %gram.1 = bf16[8,2,4,8,256]{4,3,2,1,0:T(8,128)(2,1)S(1)} custom-call(s32[4]{0:T(128)S(1)} %pad_add_fusion.me, bf16[128,2,2,8,256]{4,3,2,1,0:T(8,128)(2,1)S(1)} %bitcast.103, bf16[8,512,256]{2,1,0:T(8,128)(2,1)} %turn.1.own_ref, bf16[8,512,256]{2,1,0:T(8,128)(2,1)} %collective-permute-done.16.other_ref), custom_call_target="tpu_custom_call" | custom-call | tf_op jit(solution)/shard_map/gram/gram/pallas_call | solution.py:129
  137.1 16.8 %all_to_all.20 = bf16[64,8,256]{2,1,0:T(8,128)(2,1)S(1)} all-to-all(bf16[64,8,256]{2,1,0:T(8,128)(2,1)S(1)} %bitcast.105), channel_id=1, replica_groups=mesh['half'=2,'z'=8,'y'=2,'x'=4,'e'=2] {'z','y','x'}, dimensions={0} | all-to-all | bytes 524288 | tf_op jit(solution)/shard_map/sum/all_to_all | solution.py:218
  154.6 7.4 %all-to-all-start.3 = ((bf16[32,8,256]{2,1,0:T(8,128)(2,1)}), bf16[32,8,256]{2,1,0:T(8,128)(2,1)S(1)}, u32[]{:S(2)}, u32[]{:S(2)}) async-start(bf16[32,8,256]{2,1,0:T(8,128)(2,1)} %broadcast_in_dim.4), calls=%async_computation.3 | async-start | bytes 262144 | tf_op jit(solution)/shard_map/gather_row/all_to_all | solution.py:222
  162.2 9.8 %all-to-all-done.3.refs_0_ = bf16[32,8,256]{2,1,0:T(8,128)(2,1)S(1)} async-done(((bf16[32,8,256]{2,1,0:T(8,128)(2,1)}), bf16[32,8,256]{2,1,0:T(8,128)(2,1)S(1)}, u32[]{:S(2)}, u32[]{:S(2)}) %all-to-all-start.3) | async-done | bytes 131104 | tf_op jit(solution)/shard_map/gather_row/all_to_all | solution.py:222
  172.4 1.3 collective-permute-start.20
  173.7 2.2 %collective-permute-start.22 = (bf16[32,8,256]{2,1,0:T(8,128)(2,1)S(1)}, bf16[32,8,256]{2,1,0:T(8,128)(2,1)S(1)}, u32[]{:S(2)}, u32[]{:S(2)}) collective-permute-start(bf16[32,8,256]{2,1,0:T(8,128)(2,1)S(1)} %all-to-all-done.3.refs_0_), channel_id=1, source_target_pairs={{0,6},{2,4},{4,2},{6,0},{1,7},{3,5},{5,3},{7,1},{8,14},{10,12},{12... | collective-permute-start | bytes 393224 | tf_op jit(solution)/shard_map/gather_x/ppermute | solution.py:27
  176.6 3.8 %collective-permute-start.17 = (bf16[32,8,256]{2,1,0:T(8,128)(2,1)S(1)}, bf16[32,8,256]{2,1,0:T(8,128)(2,1)S(1)}, u32[]{:S(2)}, u32[]{:S(2)}) collective-permute-start(bf16[32,8,256]{2,1,0:T(8,128)(2,1)S(1)} %all-to-all-done.3.refs_0_), channel_id=1, source_target_pairs={{0,1},{1,0},{2,3},{3,2},{4,5},{5,4},{6,7},{7,6},{8,9},{9,8},{10,11... | collective-permute-start | bytes 393224 | tf_op jit(solution)/shard_map/gather_e/ppermute | solution.py:27
  180.6 1.5 collective-permute-start.21
  182.0 1.8 collective-permute-start.23
  184.9 2.9 %final.1 = bf16[2,512,512]{2,1,0:T(8,128)(2,1)} custom-call(s32[4]{0:T(128)S(1)} %pad_add_fusion.me, bf16[2,512,512]{2,1,0:T(8,128)(2,1)S(1)} %fusion.rows_ref, bf16[2,512,512]{2,1,0:T(8,128)(2,1)S(1)} %fusion.1.cols_ref, bf16[32,8,256]{2,1,0:T(8,128)(2,1)S(1)} %all-to-all-done.3.refs_0_, bf16[32,8,256]{2,1,0:T(8,128)(2,1)S(1)} %collective-permute-done.17.refs_1_, ...), custom_call_target="tpu_custom_call" | custom-call | tf_op jit(solution)/shard_map/final/final/pallas_call | solution.py:163
  (88 shorter events, 11.5 us)
Async XLA Ops:
  0.0 175.9 %copy-start = (bf16[2,512,512]{2,1,0:T(8,128)(2,1)S(1)}, bf16[2,512,512]{2,1,0:T(8,128)(2,1)}, u32[]{:S(2)}) copy-start(bf16[2,512,512]{2,1,0:T(8,128)(2,1)} %param.9) | copy-start | bytes 3145732
  0.0 7.7 %copy-start.29 = (bf16[1,32,64,512]{3,2,1,0:T(8,128)(2,1)S(1)}, bf16[1,32,64,512]{3,2,1,0:T(8,128)(2,1)}, u32[]{:S(2)}) copy-start(bf16[1,32,64,512]{3,2,1,0:T(8,128)(2,1)} %param.5) | copy-start | bytes 6291460
  0.0 50.6 %all-to-all-start = ((bf16[8,256,512]{2,1,0:T(8,128)(2,1)}), bf16[8,256,512]{2,1,0:T(8,128)(2,1)}, u32[]{:S(2)}, u32[]{:S(2)}) async-start(bf16[8,256,512]{2,1,0:T(8,128)(2,1)} %bitcast.107), calls=%async_computation | async-start | bytes 4194304 | tf_op jit(solution)/shard_map/child_first_leg/all_to_all | solution.py:189
  8.8 12.2 %copy-start.31 = (s32[1,5,2]{1,2,0:T(2,128)S(1)}, s32[1,5,2]{1,2,0:T(2,128)}, u32[]{:S(2)}) copy-start(s32[1,5,2]{1,2,0:T(2,128)} %param.7) | copy-start | bytes 124
  8.8 14.5 %copy-start.30 = (bf16[32,8,256]{2,1,0:T(8,128)(2,1)S(1)}, bf16[32,8,256]{2,1,0:T(8,128)(2,1)}, u32[]{:S(2)}) copy-start(bf16[32,8,256]{2,1,0:T(8,128)(2,1)} %get-tuple-element.50) | copy-start | bytes 393220
  8.8 41.8 %copy-start.28 = (s32[1,5]{1,0:T(1,128)S(1)}, s32[1,5]{1,0:T(1,128)}, u32[]{:S(2)}) copy-start(s32[1,5]{1,0:T(1,128)} %param.8) | copy-start | bytes 64
  9.7 13.6 %collective-permute-start.12 = (bf16[4,32,8,256]{3,2,1,0:T(8,128)(2,1)}, bf16[4,32,8,256]{3,2,1,0:T(8,128)(2,1)S(1)}, u32[]{:S(2)}, u32[]{:S(2)}) collective-permute-start(bf16[4,32,8,256]{3,2,1,0:T(8,128)(2,1)} %pad_maximum_fusion.1), channel_id=1, source_target_pairs={{0,8},{8,0},{1,9},{9,1},{2,10},{10,2},{3,11},{11,3},{4,12},{12,4},... | collective-permute-start | bytes 1572872 | tf_op jit(solution)/shard_map/child_rows/ppermute | solution.py:27
  9.8 26.6 %collective-permute-start.7 = (bf16[4,32,8,256]{3,2,1,0:T(8,128)(2,1)S(1)}, bf16[4,32,8,256]{3,2,1,0:T(8,128)(2,1)S(1)}, u32[]{:S(2)}, u32[]{:S(2)}) collective-permute-start(bf16[4,32,8,256]{3,2,1,0:T(8,128)(2,1)S(1)} %pad_maximum_fusion), channel_id=1, source_target_pairs={{0,8},{8,0},{1,9},{9,1},{2,10},{10,2},{3,11},{11,3},{4,12},{12,4},... | collective-permute-start | bytes 1572872 | tf_op jit(solution)/shard_map/child_rows/ppermute | solution.py:27
  11.3 14.1 %collective-permute-start = (bf16[32,8,256]{2,1,0:T(8,128)(2,1)}, bf16[32,8,256]{2,1,0:T(8,128)(2,1)S(1)}, u32[]{:S(2)}, u32[]{:S(2)}) collective-permute-start(bf16[32,8,256]{2,1,0:T(8,128)(2,1)} %get-tuple-element.53), channel_id=1, source_target_pairs={{0,64},{16,80},{32,96},{48,112},{64,0},{80,16},{96,32},{112,48},{1... | collective-permute-start | bytes 393224 | tf_op jit(solution)/shard_map/child_rows/ppermute | solution.py:31
  16.6 14.1 %collective-permute-start.1 = (bf16[32,8,256]{2,1,0:T(8,128)(2,1)}, bf16[32,8,256]{2,1,0:T(8,128)(2,1)S(1)}, u32[]{:S(2)}, u32[]{:S(2)}) collective-permute-start(bf16[32,8,256]{2,1,0:T(8,128)(2,1)} %get-tuple-element.52), channel_id=1, source_target_pairs={{0,48},{16,64},{32,80},{48,96},{64,112},{80,0},{96,16},{112,32},{1... | collective-permute-start | bytes 393224 | tf_op jit(solution)/shard_map/child_rows/ppermute | solution.py:31
  18.2 13.9 %collective-permute-start.2 = (bf16[32,8,256]{2,1,0:T(8,128)(2,1)}, bf16[32,8,256]{2,1,0:T(8,128)(2,1)S(1)}, u32[]{:S(2)}, u32[]{:S(2)}) collective-permute-start(bf16[32,8,256]{2,1,0:T(8,128)(2,1)} %get-tuple-element.51), channel_id=1, source_target_pairs={{0,80},{16,96},{32,112},{48,0},{64,16},{80,32},{96,48},{112,64},{1... | collective-permute-start | bytes 393224 | tf_op jit(solution)/shard_map/child_rows/ppermute | solution.py:31
  23.3 11.0 %collective-permute-start.3 = (bf16[32,8,256]{2,1,0:T(8,128)(2,1)S(1)}, bf16[32,8,256]{2,1,0:T(8,128)(2,1)S(1)}, u32[]{:S(2)}, u32[]{:S(2)}) collective-permute-start(bf16[32,8,256]{2,1,0:T(8,128)(2,1)S(1)} %copy-done.30), channel_id=1, source_target_pairs={{0,32},{16,48},{32,64},{48,80},{64,96},{80,112},{96,0},{112,16},{1... | collective-permute-start | bytes 393224 | tf_op jit(solution)/shard_map/child_rows/ppermute | solution.py:31
  25.4 13.9 %collective-permute-start.4 = (bf16[32,8,256]{2,1,0:T(8,128)(2,1)}, bf16[32,8,256]{2,1,0:T(8,128)(2,1)S(1)}, u32[]{:S(2)}, u32[]{:S(2)}) collective-permute-start(bf16[32,8,256]{2,1,0:T(8,128)(2,1)} %get-tuple-element.49), channel_id=1, source_target_pairs={{0,96},{16,112},{32,0},{48,16},{64,32},{80,48},{96,64},{112,80},{1... | collective-permute-start | bytes 393224 | tf_op jit(solution)/shard_map/child_rows/ppermute | solution.py:31
  30.6 32.8 %copy-start.2 = (bf16[32,8,256]{2,1,0:T(8,128)(2,1)}, bf16[32,8,256]{2,1,0:T(8,128)(2,1)S(1)}, u32[]{:S(2)}) copy-start(bf16[32,8,256]{2,1,0:T(8,128)(2,1)S(1)} %collective-permute-done.1.refs_1_) | copy-start | bytes 393220
  30.7 11.2 %collective-permute-start.5 = (bf16[32,8,256]{2,1,0:T(8,128)(2,1)}, bf16[32,8,256]{2,1,0:T(8,128)(2,1)S(1)}, u32[]{:S(2)}, u32[]{:S(2)}) collective-permute-start(bf16[32,8,256]{2,1,0:T(8,128)(2,1)} %get-tuple-element.48), channel_id=1, source_target_pairs={{0,16},{16,32},{32,48},{48,64},{64,80},{80,96},{96,112},{112,0},{1... | collective-permute-start | bytes 393224 | tf_op jit(solution)/shard_map/child_rows/ppermute | solution.py:31
  32.1 31.4 %copy-start.4 = (bf16[32,8,256]{2,1,0:T(8,128)(2,1)}, bf16[32,8,256]{2,1,0:T(8,128)(2,1)S(1)}, u32[]{:S(2)}) copy-start(bf16[32,8,256]{2,1,0:T(8,128)(2,1)S(1)} %collective-permute-done.2.refs_2_) | copy-start | bytes 393220
  32.1 12.3 %collective-permute-start.6 = (bf16[32,8,256]{2,1,0:T(8,128)(2,1)}, bf16[32,8,256]{2,1,0:T(8,128)(2,1)S(1)}, u32[]{:S(2)}, u32[]{:S(2)}) collective-permute-start(bf16[32,8,256]{2,1,0:T(8,128)(2,1)} %get-tuple-element.47), channel_id=1, source_target_pairs={{0,112},{16,0},{32,16},{48,32},{64,48},{80,64},{96,80},{112,96},{1... | collective-permute-start | bytes 393224 | tf_op jit(solution)/shard_map/child_rows/ppermute | solution.py:31
  34.3 29.2 %copy-start.6 = (bf16[32,8,256]{2,1,0:T(8,128)(2,1)}, bf16[32,8,256]{2,1,0:T(8,128)(2,1)S(1)}, u32[]{:S(2)}) copy-start(bf16[32,8,256]{2,1,0:T(8,128)(2,1)S(1)} %collective-permute-done.3.refs_3_) | copy-start | bytes 393220
  34.3 11.1 %collective-permute-start.13 = (bf16[32,8,256]{2,1,0:T(8,128)(2,1)S(1)}, bf16[32,8,256]{2,1,0:T(8,128)(2,1)S(1)}, u32[]{:S(2)}, u32[]{:S(2)}) collective-permute-start(bf16[32,8,256]{2,1,0:T(8,128)(2,1)S(1)} %get-tuple-element.58), channel_id=1, source_target_pairs={{0,96},{16,112},{32,0},{48,16},{64,32},{80,48},{96,64},{112,80},{1... | collective-permute-start | bytes 393224 | tf_op jit(solution)/shard_map/child_rows/ppermute | solution.py:31
  36.4 11.3 %collective-permute-start.14 = (bf16[32,8,256]{2,1,0:T(8,128)(2,1)S(1)}, bf16[32,8,256]{2,1,0:T(8,128)(2,1)S(1)}, u32[]{:S(2)}, u32[]{:S(2)}) collective-permute-start(bf16[32,8,256]{2,1,0:T(8,128)(2,1)S(1)} %get-tuple-element.57), channel_id=1, source_target_pairs={{0,16},{16,32},{32,48},{48,64},{64,80},{80,96},{96,112},{112,0},{1... | collective-permute-start | bytes 393224 | tf_op jit(solution)/shard_map/child_rows/ppermute | solution.py:31
  39.3 24.2 %copy-start.8 = (bf16[32,8,256]{2,1,0:T(8,128)(2,1)}, bf16[32,8,256]{2,1,0:T(8,128)(2,1)S(1)}, u32[]{:S(2)}) copy-start(bf16[32,8,256]{2,1,0:T(8,128)(2,1)S(1)} %collective-permute-done.4.refs_4_) | copy-start | bytes 393220
  39.3 25.6 %collective-permute-start.15 = (bf16[32,8,256]{2,1,0:T(8,128)(2,1)}, bf16[32,8,256]{2,1,0:T(8,128)(2,1)S(1)}, u32[]{:S(2)}, u32[]{:S(2)}) collective-permute-start(bf16[32,8,256]{2,1,0:T(8,128)(2,1)} %get-tuple-element.56), channel_id=1, source_target_pairs={{0,112},{16,0},{32,16},{48,32},{64,48},{80,64},{96,80},{112,96},{1... | collective-permute-start | bytes 393224 | tf_op jit(solution)/shard_map/child_rows/ppermute | solution.py:31
  41.9 21.6 %copy-start.10 = (bf16[32,8,256]{2,1,0:T(8,128)(2,1)}, bf16[32,8,256]{2,1,0:T(8,128)(2,1)S(1)}, u32[]{:S(2)}) copy-start(bf16[32,8,256]{2,1,0:T(8,128)(2,1)S(1)} %collective-permute-done.5.refs_5_) | copy-start | bytes 393220
  41.9 23.7 %collective-permute-start.10 = (bf16[32,8,256]{2,1,0:T(8,128)(2,1)}, bf16[32,8,256]{2,1,0:T(8,128)(2,1)S(1)}, u32[]{:S(2)}, u32[]{:S(2)}) collective-permute-start(bf16[32,8,256]{2,1,0:T(8,128)(2,1)} %get-tuple-element.60), channel_id=1, source_target_pairs={{0,80},{16,96},{32,112},{48,0},{64,16},{80,32},{96,48},{112,64},{1... | collective-permute-start | bytes 393224 | tf_op jit(solution)/shard_map/child_rows/ppermute | solution.py:31
  44.4 19.1 %copy-start.12 = (bf16[32,8,256]{2,1,0:T(8,128)(2,1)}, bf16[32,8,256]{2,1,0:T(8,128)(2,1)S(1)}, u32[]{:S(2)}) copy-start(bf16[32,8,256]{2,1,0:T(8,128)(2,1)S(1)} %collective-permute-done.6.refs_6_) | copy-start | bytes 393220
  44.4 21.9 %collective-permute-start.11 = (bf16[32,8,256]{2,1,0:T(8,128)(2,1)S(1)}, bf16[32,8,256]{2,1,0:T(8,128)(2,1)S(1)}, u32[]{:S(2)}, u32[]{:S(2)}) collective-permute-start(bf16[32,8,256]{2,1,0:T(8,128)(2,1)S(1)} %get-tuple-element.59), channel_id=1, source_target_pairs={{0,32},{16,48},{32,64},{48,80},{64,96},{80,112},{96,0},{112,16},{1... | collective-permute-start | bytes 393224 | tf_op jit(solution)/shard_map/child_rows/ppermute | solution.py:31
  45.4 18.1 %copy-start.14 = (bf16[32,8,256]{2,1,0:T(8,128)(2,1)}, bf16[32,8,256]{2,1,0:T(8,128)(2,1)S(1)}, u32[]{:S(2)}) copy-start(bf16[32,8,256]{2,1,0:T(8,128)(2,1)S(1)} %collective-permute-done.13.refs_12_) | copy-start | bytes 393220
  45.4 21.5 %collective-permute-start.8 = (bf16[32,8,256]{2,1,0:T(8,128)(2,1)S(1)}, bf16[32,8,256]{2,1,0:T(8,128)(2,1)S(1)}, u32[]{:S(2)}, u32[]{:S(2)}) collective-permute-start(bf16[32,8,256]{2,1,0:T(8,128)(2,1)S(1)} %get-tuple-element.62), channel_id=1, source_target_pairs={{0,64},{16,80},{32,96},{48,112},{64,0},{80,16},{96,32},{112,48},{1... | collective-permute-start | bytes 393224 | tf_op jit(solution)/shard_map/child_rows/ppermute | solution.py:31
  47.8 15.8 %copy-start.16 = (bf16[32,8,256]{2,1,0:T(8,128)(2,1)}, bf16[32,8,256]{2,1,0:T(8,128)(2,1)S(1)}, u32[]{:S(2)}) copy-start(bf16[32,8,256]{2,1,0:T(8,128)(2,1)S(1)} %collective-permute-done.14.refs_13_) | copy-start | bytes 393220
  47.8 20.6 %collective-permute-start.9 = (bf16[32,8,256]{2,1,0:T(8,128)(2,1)S(1)}, bf16[32,8,256]{2,1,0:T(8,128)(2,1)S(1)}, u32[]{:S(2)}, u32[]{:S(2)}) collective-permute-start(bf16[32,8,256]{2,1,0:T(8,128)(2,1)S(1)} %get-tuple-element.61), channel_id=1, source_target_pairs={{0,48},{16,64},{32,80},{48,96},{64,112},{80,0},{96,16},{112,32},{1... | collective-permute-start | bytes 393224 | tf_op jit(solution)/shard_map/child_rows/ppermute | solution.py:31
  63.5 1.4 copy-start.1
  69.0 64.5 %all-to-all-start.1 = ((bf16[128,32,256]{2,1,0:T(8,128)(2,1)}), bf16[128,32,256]{2,1,0:T(8,128)(2,1)S(1)}, u32[]{:S(2)}, u32[]{:S(2)}) async-start(bf16[128,32,256]{2,1,0:T(8,128)(2,1)} %bitcast.104), calls=%async_computation.1 | async-start | bytes 4194304 | tf_op jit(solution)/shard_map/summed_rows/all_to_all | solution.py:210
  82.2 0.9 copy-start.3
  85.8 0.9 copy-start.11
  86.7 0.9 copy-start.13
  87.6 0.9 copy-start.15
  88.6 0.9 copy-start.17
  92.2 0.9 copy-start.25
  93.1 0.9 copy-start.27
  96.4 5.0 %collective-permute-start.16 = (bf16[8,512,256]{2,1,0:T(8,128)(2,1)}, bf16[8,512,256]{2,1,0:T(8,128)(2,1)}, u32[]{:S(2)}, u32[]{:S(2)}) collective-permute-start(bf16[8,512,256]{2,1,0:T(8,128)(2,1)} %turn.1.own_ref), channel_id=1, source_target_pairs={{0,1},{1,0},{2,3},{3,2},{4,5},{5,4},{6,7},{7,6},{8,9},{9,8},{10,11... | collective-permute-start | bytes 6291464 | tf_op jit(solution)/shard_map/turn/ppermute | solution.py:27
  154.6 17.4 %all-to-all-start.3 = ((bf16[32,8,256]{2,1,0:T(8,128)(2,1)}), bf16[32,8,256]{2,1,0:T(8,128)(2,1)S(1)}, u32[]{:S(2)}, u32[]{:S(2)}) async-start(bf16[32,8,256]{2,1,0:T(8,128)(2,1)} %broadcast_in_dim.4), calls=%async_computation.3 | async-start | bytes 262144 | tf_op jit(solution)/shard_map/gather_row/all_to_all | solution.py:222
  172.0 8.5 %collective-permute-start.18 = (bf16[32,8,256]{2,1,0:T(8,128)(2,1)S(1)}, bf16[32,8,256]{2,1,0:T(8,128)(2,1)S(1)}, u32[]{:S(2)}, u32[]{:S(2)}) collective-permute-start(bf16[32,8,256]{2,1,0:T(8,128)(2,1)S(1)} %all-to-all-done.3.refs_0_), channel_id=1, source_target_pairs={{0,2},{2,0},{4,6},{6,4},{1,3},{3,1},{5,7},{7,5},{8,10},{10,8},{12,... | collective-permute-start | bytes 393224 | tf_op jit(solution)/shard_map/gather_x/ppermute | solution.py:27
  172.4 8.2 %collective-permute-start.20 = (bf16[32,8,256]{2,1,0:T(8,128)(2,1)S(1)}, bf16[32,8,256]{2,1,0:T(8,128)(2,1)S(1)}, u32[]{:S(2)}, u32[]{:S(2)}) collective-permute-start(bf16[32,8,256]{2,1,0:T(8,128)(2,1)S(1)} %all-to-all-done.3.refs_0_), channel_id=1, source_target_pairs={{0,4},{2,6},{4,0},{6,2},{1,5},{3,7},{5,1},{7,3},{8,12},{10,14},{12... | collective-permute-start | bytes 393224 | tf_op jit(solution)/shard_map/gather_x/ppermute | solution.py:27
  173.7 8.4 %collective-permute-start.22 = (bf16[32,8,256]{2,1,0:T(8,128)(2,1)S(1)}, bf16[32,8,256]{2,1,0:T(8,128)(2,1)S(1)}, u32[]{:S(2)}, u32[]{:S(2)}) collective-permute-start(bf16[32,8,256]{2,1,0:T(8,128)(2,1)S(1)} %all-to-all-done.3.refs_0_), channel_id=1, source_target_pairs={{0,6},{2,4},{4,2},{6,0},{1,7},{3,5},{5,3},{7,1},{8,14},{10,12},{12... | collective-permute-start | bytes 393224 | tf_op jit(solution)/shard_map/gather_x/ppermute | solution.py:27
  176.6 8.1 %collective-permute-start.17 = (bf16[32,8,256]{2,1,0:T(8,128)(2,1)S(1)}, bf16[32,8,256]{2,1,0:T(8,128)(2,1)S(1)}, u32[]{:S(2)}, u32[]{:S(2)}) collective-permute-start(bf16[32,8,256]{2,1,0:T(8,128)(2,1)S(1)} %all-to-all-done.3.refs_0_), channel_id=1, source_target_pairs={{0,1},{1,0},{2,3},{3,2},{4,5},{5,4},{6,7},{7,6},{8,9},{9,8},{10,11... | collective-permute-start | bytes 393224 | tf_op jit(solution)/shard_map/gather_e/ppermute | solution.py:27
  180.5 4.3 %collective-permute-start.19 = (bf16[32,8,256]{2,1,0:T(8,128)(2,1)S(1)}, bf16[32,8,256]{2,1,0:T(8,128)(2,1)S(1)}, u32[]{:S(2)}, u32[]{:S(2)}) collective-permute-start(bf16[32,8,256]{2,1,0:T(8,128)(2,1)S(1)} %collective-permute-done.18.refs_2_), channel_id=1, source_target_pairs={{0,1},{1,0},{2,3},{3,2},{4,5},{5,4},{6,7},{7,6},{8,9},{9,8},{10,11... | collective-permute-start | bytes 393224 | tf_op jit(solution)/shard_map/gather_e/ppermute | solution.py:27
  180.6 4.2 %collective-permute-start.21 = (bf16[32,8,256]{2,1,0:T(8,128)(2,1)S(1)}, bf16[32,8,256]{2,1,0:T(8,128)(2,1)S(1)}, u32[]{:S(2)}, u32[]{:S(2)}) collective-permute-start(bf16[32,8,256]{2,1,0:T(8,128)(2,1)S(1)} %collective-permute-done.20.refs_4_), channel_id=1, source_target_pairs={{0,1},{1,0},{2,3},{3,2},{4,5},{5,4},{6,7},{7,6},{8,9},{9,8},{10,11... | collective-permute-start | bytes 393224 | tf_op jit(solution)/shard_map/gather_e/ppermute | solution.py:27
  182.0 2.8 %collective-permute-start.23 = (bf16[32,8,256]{2,1,0:T(8,128)(2,1)S(1)}, bf16[32,8,256]{2,1,0:T(8,128)(2,1)S(1)}, u32[]{:S(2)}, u32[]{:S(2)}) collective-permute-start(bf16[32,8,256]{2,1,0:T(8,128)(2,1)S(1)} %collective-permute-done.22.refs_6_), channel_id=1, source_target_pairs={{0,1},{1,0},{2,3},{3,2},{4,5},{5,4},{6,7},{7,6},{8,9},{9,8},{10,11... | collective-permute-start | bytes 393224 | tf_op jit(solution)/shard_map/gather_e/ppermute | solution.py:27
  (11 other events, 8.7 us)

commit v2 on v0

--- a/solution.py
+++ b/solution.py
@@ -15,7 +15,11 @@
 ALL = ("half",) + ROW_COL
 VMEM = pl.BlockSpec(memory_space=pltpu.VMEM)
 SMEM = pl.BlockSpec(memory_space=pltpu.SMEM)
-LIMIT = pltpu.CompilerParams(vmem_limit_bytes=50 << 20)
+HBM = pl.BlockSpec(memory_space=pltpu.HBM)
+
+
+def vmem(mebibytes):
+    return pltpu.CompilerParams(vmem_limit_bytes=mebibytes << 20)
 
 
 def dot(a, b, ca, cb):
@@ -28,41 +32,55 @@
 
 
 def terms_kernel(me, site, leg, table, *refs):
-    blocks, (out_ref, whole, inner, acc) = refs[: NX * NE], refs[NX * NE :]
+    blocks, (out_ref, ops, whole, inner, acc, arrived) = refs[: NX * NE], refs[NX * NE :]
+    sites, terms, rows = ops.shape[1], leg.shape[0], whole.shape[0]
+    fetch = [
+        [pltpu.make_async_copy(table.at[w, s], ops.at[w, s], arrived.at[w, s]) for s in range(sites)]
+        for w in range(2)
+    ]
+    for copy in fetch[1] + fetch[0]:
+        copy.start()
     col = me[1] * NE + me[0]
-    rows = whole.shape[0]
     for k, ref in enumerate(blocks):
         for a in range(rows):
             whole[a, col ^ k] = ref[a]
 
-    def x_of(a):
-        return whole[a].reshape(512, 512)
-
-    for term in range(leg.shape[0]):
-        code = leg[term]
-
-        @pl.when(code != 0)
-        def _():
-            right = table[1, site[term, 1]]
-            for a in range(rows):
-                inner[a] = dot(x_of(a), right, 1, 1).astype(BF)
-
-        @pl.when(code == 0)
+    def any_term(test):
+        found = test(0)
+        for term in range(1, terms):
+            found = found | test(term)
+        return found
+
+    @pl.when(any_term(lambda term: leg[term] == 0))
+    def _():
+        for a in range(rows):
+            inner[sites, a] = whole[a].reshape(512, 512)
+
+    for s in range(sites):
+        fetch[1][s].wait()
+
+        @pl.when(any_term(lambda term: (leg[term] != 0) & (site[term, 1] == s)))
         def _():
             for a in range(rows):
-                inner[a] = x_of(a)
+                inner[s, a] = dot(whole[a].reshape(512, 512), ops[1, s], 1, 1).astype(BF)
+
+    for copy in fetch[0]:
+        copy.wait()
+    for term in range(terms):
+        code = leg[term]
+        held = jnp.where(code == 0, sites, site[term, 1])
 
         @pl.when(code != 1)
         def _():
-            left = table[0, site[term, 0]]
+            left = ops[0, site[term, 0]]
             for a in range(rows):
-                part = dot(left, inner[a], 1, 0)
+                part = dot(left, inner[held, a], 1, 0)
                 acc[a] = part if term == 0 else acc[a] + part
 
         @pl.when(code == 1)
         def _():
             for a in range(rows):
-                part = inner[a].astype(F32)
+                part = inner[held, a].astype(F32)
                 acc[a] = part if term == 0 else acc[a] + part
 
     for a in range(rows):
@@ -75,17 +93,20 @@
 
 
 def apply_terms(me, site, leg, table, arrived):
+    sites = table.shape[1]
     return pl.pallas_call(
         terms_kernel,
         out_shape=jax.ShapeDtypeStruct((NZ, NY, NX, NE, 2, NE, 8, 256), BF),
-        in_specs=[SMEM] * 3 + [VMEM] * (1 + NX * NE),
+        in_specs=[SMEM] * 3 + [HBM] + [VMEM] * (NX * NE),
         out_specs=VMEM,
         scratch_shapes=[
+            pltpu.VMEM((2, sites, 512, 512), BF),
             pltpu.VMEM((4, NX * NE, 64, 512), BF),
-            pltpu.VMEM((4, 512, 512), BF),
+            pltpu.VMEM((sites + 1, 4, 512, 512), BF),
             pltpu.VMEM((4, 512, 512), F32),
+            pltpu.SemaphoreType.DMA((2, sites)),
         ],
-        compiler_params=LIMIT,
+        compiler_params=vmem(50),
         name="terms",
     )(me, site, leg, table, *arrived)
 
@@ -103,7 +124,7 @@
         grid=(rows // step,),
         in_specs=[pl.BlockSpec((step, depth, lanes), lambda i: (i, 0, 0))],
         out_specs=pl.BlockSpec((depth, step, lanes), lambda i: (0, i, 0)),
-        compiler_params=LIMIT,
+        compiler_params=vmem(50),
         name="turn",
     )(value)
 
@@ -132,7 +153,7 @@
         in_specs=[SMEM, VMEM, VMEM, VMEM],
         out_specs=VMEM,
         scratch_shapes=[pltpu.VMEM((256, 512), F32)],
-        compiler_params=LIMIT,
+        compiler_params=vmem(50),
         name="gram",
     )(me, summed, own, other)
 
@@ -169,7 +190,7 @@
             pltpu.VMEM((2, NY, 64, 8, 256), BF),
             pltpu.VMEM((2, 512, 512), F32),
         ],
-        compiler_params=LIMIT,
+        compiler_params=vmem(50),
         name="final",
     )(me, by_rows, by_cols, *pieces)
 

time: 178 us -> 178 us (level)
  no operation moved by 1% of the time
where the time goes in v2:
time: 178 us; the launch traced here: 177 us
  waiting for transfers between devices  76.7 us (43%)
  starting transfers between devices  51.2 us (29%)
  Pallas kernels  25.3 us (14%)
  blocking collectives  16.8 us (9%)
  local copies, waits for them, and re-layouts  5.18 us (3%)
    all_to_all x1, waiting for transfers between devices, on_device(): lax.all_to_all(summed.reshape(128, 32, 256), ROW_COL, 0, 0, tiled=True)  44.6 us
    ppermute x15, starting transfers between devices, swap(): return lax.ppermute(value, axes, [(i, i ^ offset) for i in range(peers)])  23.9 us
    ppermute x15, waiting for transfers between devices, swap(): return lax.ppermute(value, axes, [(i, i ^ offset) for i in range(peers)])  20.7 us
    all_to_all x1, blocking collectives, on_device(): lax.all_to_all(part.reshape(64, 8, 256), ('z', 'y', 'x'), 0, 0, tiled=True)  16.8 us
    pallas_call x1, Pallas kernels, apply_terms(): pl.pallas_call(terms_kernel, out_shape=jax.ShapeDtypeStruct((NZ, NY, NX,...  12.9 us
    all_to_all x1, starting transfers between devices, on_device(): lax.all_to_all(summed.reshape(128, 32, 256), ROW_COL, 0, 0, tiled=True)  10.4 us
    all_to_all x1, starting transfers between devices, on_device(): child_all = lax.all_to_all(cut, ROW, 0, 0, tiled=True)  10.3 us
    all_to_all x1, waiting for transfers between devices, on_device(): env = lax.all_to_all(env, ('half',) + ROW, 0, 0, tiled=True)  9.79 us
  transfers between devices with their start and end apart: 18, of which 9 were waited for; matrix products, arithmetic and copies ran while one was open for 2% of the time, Pallas kernels for 11%

profile of v2, /device:TPU:1, one launch (start us, length us, event | category | flops | bytes accessed | tf_op | source)
XLA Modules:
  0.0 177.2 jit_solution(8846851981696735884)
XLA Ops:
  0.0 3.2 %copy.11 = bf16[8,2,32,8,256]{4,3,2,1,0:T(8,128)(2,1)} copy(bf16[8,2,32,8,256]{4,3,1,0,2:T(8,128)(2,1)} %bitcast.43) | data formatting | bytes 4194304 | tf_op jit(solution)/shard_map/child_rows/transpose | solution.py:210
  3.2 10.3 %all-to-all-start.1 = ((bf16[16,256,256]{2,1,0:T(8,128)(2,1)}), bf16[16,256,256]{2,1,0:T(8,128)(2,1)}, u32[]{:S(2)}, u32[]{:S(2)}) async-start(bf16[16,256,256]{2,1,0:T(8,128)(2,1)} %bitcast.45), calls=%async_computation.1 | async-start | bytes 4194304 | tf_op jit(solution)/shard_map/child_rows/all_to_all | solution.py:212
  13.6 0.0 copy-start.3
  13.6 0.0 copy-start.1
  13.6 1.1 dynamic-slice_bitcast_fusion
  14.7 1.0 collective-permute-start
  15.6 1.2 collective-permute-start.1
  16.8 0.4 collective-permute-start.2
  17.3 2.7 %collective-permute-start.3 = (bf16[4,64,512]{2,1,0:T(8,128)(2,1)}, bf16[4,64,512]{2,1,0:T(8,128)(2,1)S(1)}, u32[]{:S(2)}, u32[]{:S(2)}) collective-permute-start(bf16[4,64,512]{2,1,0:T(8,128)(2,1)} %get-tuple-element.8), channel_id=1, source_target_pairs={{0,4},{1,5},{2,6},{3,7},{4,0},{5,1},{6,2},{7,3},{8,12},{9,13},{10,... | collective-permute-start | bytes 786440 | tf_op jit(solution)/shard_map/child_first_leg/ppermute | solution.py:31
  20.0 0.6 collective-permute-start.4
  20.6 2.5 %collective-permute-start.5 = (bf16[4,64,512]{2,1,0:T(8,128)(2,1)}, bf16[4,64,512]{2,1,0:T(8,128)(2,1)S(1)}, u32[]{:S(2)}, u32[]{:S(2)}) collective-permute-start(bf16[4,64,512]{2,1,0:T(8,128)(2,1)} %get-tuple-element.6), channel_id=1, source_target_pairs={{0,6},{1,7},{2,4},{3,5},{4,2},{5,3},{6,0},{7,1},{8,14},{9,15},{10,... | collective-permute-start | bytes 786440 | tf_op jit(solution)/shard_map/child_first_leg/ppermute | solution.py:31
  23.1 0.6 collective-permute-done.1.refs_2_
  23.7 3.4 %collective-permute-start.6 = (bf16[4,64,512]{2,1,0:T(8,128)(2,1)}, bf16[4,64,512]{2,1,0:T(8,128)(2,1)S(1)}, u32[]{:S(2)}, u32[]{:S(2)}) collective-permute-start(bf16[4,64,512]{2,1,0:T(8,128)(2,1)} %get-tuple-element.5), channel_id=1, source_target_pairs={{0,7},{1,6},{2,5},{3,4},{4,3},{5,2},{6,1},{7,0},{8,15},{9,14},{10,... | collective-permute-start | bytes 786440 | tf_op jit(solution)/shard_map/child_first_leg/ppermute | solution.py:31
  27.1 0.1 copy.10.site
  27.2 0.1 pad_add_fusion.me
  27.3 2.8 %collective-permute-done.2.refs_3_ = bf16[4,64,512]{2,1,0:T(8,128)(2,1)S(1)} collective-permute-done((bf16[4,64,512]{2,1,0:T(8,128)(2,1)}, bf16[4,64,512]{2,1,0:T(8,128)(2,1)S(1)}, u32[]{:S(2)}, u32[]{:S(2)}) %collective-permute-start.2) | collective-permute-done | bytes 262176 | tf_op jit(solution)/shard_map/child_first_leg/ppermute | solution.py:31
  30.1 7.1 %collective-permute-done.3.refs_4_ = bf16[4,64,512]{2,1,0:T(8,128)(2,1)S(1)} collective-permute-done((bf16[4,64,512]{2,1,0:T(8,128)(2,1)}, bf16[4,64,512]{2,1,0:T(8,128)(2,1)S(1)}, u32[]{:S(2)}, u32[]{:S(2)}) %collective-permute-start.3) | collective-permute-done | bytes 262176 | tf_op jit(solution)/shard_map/child_first_leg/ppermute | solution.py:31
  37.1 5.7 %collective-permute-done.4.refs_5_ = bf16[4,64,512]{2,1,0:T(8,128)(2,1)S(1)} collective-permute-done((bf16[4,64,512]{2,1,0:T(8,128)(2,1)}, bf16[4,64,512]{2,1,0:T(8,128)(2,1)S(1)}, u32[]{:S(2)}, u32[]{:S(2)}) %collective-permute-start.4) | collective-permute-done | bytes 262176 | tf_op jit(solution)/shard_map/child_first_leg/ppermute | solution.py:31
  42.8 4.5 %collective-permute-done.6.refs_7_ = bf16[4,64,512]{2,1,0:T(8,128)(2,1)S(1)} collective-permute-done((bf16[4,64,512]{2,1,0:T(8,128)(2,1)}, bf16[4,64,512]{2,1,0:T(8,128)(2,1)S(1)}, u32[]{:S(2)}, u32[]{:S(2)}) %collective-permute-start.6) | collective-permute-done | bytes 262176 | tf_op jit(solution)/shard_map/child_first_leg/ppermute | solution.py:31
  47.3 12.9 %terms.1 = bf16[8,2,4,2,2,2,8,256]{7,6,5,4,3,2,1,0:T(8,128)(2,1)} custom-call(s32[2]{0:T(128)S(1)} %pad_add_fusion.me, s32[5,2]{1,0:T(8,128)S(1)} %copy.10.site, s32[5]{0:T(128)S(1)} %bitcast.42, bf16[2,4,512,512]{3,2,1,0:T(8,128)(2,1)} %bitcast.47, bf16[4,64,512]{2,1,0:T(8,128)(2,1)S(1)} %get-tuple-element.12.refs_0_, ...), custom_call_target="tpu_custom_call" | custom-call | tf_op jit(solution)/shard_map/terms/terms/pallas_call | solution.py:97
  60.3 1.6 all-to-all-done.1
  61.8 10.4 %all-to-all-start = ((bf16[128,32,256]{2,1,0:T(8,128)(2,1)}), bf16[128,32,256]{2,1,0:T(8,128)(2,1)S(1)}, u32[]{:S(2)}, u32[]{:S(2)}) async-start(bf16[128,32,256]{2,1,0:T(8,128)(2,1)} %bitcast.46), calls=%async_computation | async-start | bytes 4194304 | tf_op jit(solution)/shard_map/summed_rows/all_to_all | solution.py:225
  72.2 5.8 %turn.1.own_ref = bf16[8,512,256]{2,1,0:T(8,128)(2,1)} custom-call(bf16[512,8,256]{2,1,0:T(8,128)(2,1)} %bitcast.22.in_ref), custom_call_target="tpu_custom_call" | custom-call | tf_op jit(solution)/shard_map/turn/turn/pallas_call | solution.py:121
  78.1 0.9 collective-permute-start.7
  78.9 44.6 %all-to-all-done = bf16[128,32,256]{2,1,0:T(8,128)(2,1)S(1)} async-done(((bf16[128,32,256]{2,1,0:T(8,128)(2,1)}), bf16[128,32,256]{2,1,0:T(8,128)(2,1)S(1)}, u32[]{:S(2)}, u32[]{:S(2)}) %all-to-all-start) | async-done | bytes 2097184 | tf_op jit(solution)/shard_map/summed_rows/all_to_all | solution.py:225
  123.6 0.0 collective-permute-done.7.other_ref
  123.6 3.6 %gram.1 = bf16[8,2,4,8,256]{4,3,2,1,0:T(8,128)(2,1)S(1)} custom-call(s32[2]{0:T(128)S(1)} %pad_add_fusion.me, bf16[128,2,2,8,256]{4,3,2,1,0:T(8,128)(2,1)S(1)} %bitcast.40, bf16[8,512,256]{2,1,0:T(8,128)(2,1)} %turn.1.own_ref, bf16[8,512,256]{2,1,0:T(8,128)(2,1)} %collective-permute-done.7.other_ref), custom_call_target="tpu_custom_call" | custom-call | tf_op jit(solution)/shard_map/gram/gram/pallas_call | solution.py:150
  127.2 16.8 %all_to_all.20 = bf16[64,8,256]{2,1,0:T(8,128)(2,1)S(1)} all-to-all(bf16[64,8,256]{2,1,0:T(8,128)(2,1)S(1)} %bitcast.41), channel_id=1, replica_groups=mesh['half'=2,'z'=8,'y'=2,'x'=4,'e'=2] {'z','y','x'}, dimensions={0} | all-to-all | bytes 524288 | tf_op jit(solution)/shard_map/sum/all_to_all | solution.py:233
  144.0 0.1 reduce_sum.12
  144.0 0.7 broadcast_in_dim.4
  144.7 6.7 %all-to-all-start.3 = ((bf16[32,8,256]{2,1,0:T(8,128)(2,1)}), bf16[32,8,256]{2,1,0:T(8,128)(2,1)S(1)}, u32[]{:S(2)}, u32[]{:S(2)}) async-start(bf16[32,8,256]{2,1,0:T(8,128)(2,1)} %broadcast_in_dim.4), calls=%async_computation.3 | async-start | bytes 262144 | tf_op jit(solution)/shard_map/gather_row/all_to_all | solution.py:237
  151.4 0.1 reshape.75
  151.6 9.8 %all-to-all-done.3.refs_0_ = bf16[32,8,256]{2,1,0:T(8,128)(2,1)S(1)} async-done(((bf16[32,8,256]{2,1,0:T(8,128)(2,1)}), bf16[32,8,256]{2,1,0:T(8,128)(2,1)S(1)}, u32[]{:S(2)}, u32[]{:S(2)}) %all-to-all-start.3) | async-done | bytes 131104 | tf_op jit(solution)/shard_map/gather_row/all_to_all | solution.py:237
  161.4 0.4 collective-permute-start.9
  161.7 1.3 collective-permute-start.11
  163.0 2.2 %collective-permute-start.13 = (bf16[32,8,256]{2,1,0:T(8,128)(2,1)S(1)}, bf16[32,8,256]{2,1,0:T(8,128)(2,1)S(1)}, u32[]{:S(2)}, u32[]{:S(2)}) collective-permute-start(bf16[32,8,256]{2,1,0:T(8,128)(2,1)S(1)} %all-to-all-done.3.refs_0_), channel_id=1, source_target_pairs={{0,6},{2,4},{4,2},{6,0},{1,7},{3,5},{5,3},{7,1},{8,14},{10,12},{12... | collective-permute-start | bytes 393224 | tf_op jit(solution)/shard_map/gather_x/ppermute | solution.py:31
  165.2 0.7 fusion.rows_ref
  166.0 3.9 %collective-permute-start.8 = (bf16[32,8,256]{2,1,0:T(8,128)(2,1)S(1)}, bf16[32,8,256]{2,1,0:T(8,128)(2,1)S(1)}, u32[]{:S(2)}, u32[]{:S(2)}) collective-permute-start(bf16[32,8,256]{2,1,0:T(8,128)(2,1)S(1)} %all-to-all-done.3.refs_0_), channel_id=1, source_target_pairs={{0,1},{1,0},{2,3},{3,2},{4,5},{5,4},{6,7},{7,6},{8,9},{9,8},{10,11... | collective-permute-start | bytes 393224 | tf_op jit(solution)/shard_map/gather_e/ppermute | solution.py:31
  169.8 0.0 collective-permute-done.9.refs_2_
  169.8 0.1 collective-permute-start.10
  170.0 1.5 collective-permute-start.12
  171.4 0.0 collective-permute-done.13.refs_6_
  171.4 1.8 %collective-permute-start.14 = (bf16[32,8,256]{2,1,0:T(8,128)(2,1)S(1)}, bf16[32,8,256]{2,1,0:T(8,128)(2,1)S(1)}, u32[]{:S(2)}, u32[]{:S(2)}) collective-permute-start(bf16[32,8,256]{2,1,0:T(8,128)(2,1)S(1)} %collective-permute-done.13.refs_6_), channel_id=1, source_target_pairs={{0,1},{1,0},{2,3},{3,2},{4,5},{5,4},{6,7},{7,6},{8,9},{9,8},{10,11... | collective-permute-start | bytes 393224 | tf_op jit(solution)/shard_map/gather_e/ppermute | solution.py:31
  173.2 0.9 fusion.1.cols_ref
  174.1 0.0 collective-permute-done.8.refs_1_
  174.1 0.0 collective-permute-done.10.refs_3_
  174.2 0.1 collective-permute-done.14.refs_7_
  174.2 2.9 %final.1 = bf16[2,512,512]{2,1,0:T(8,128)(2,1)} custom-call(s32[2]{0:T(128)S(1)} %pad_add_fusion.me, bf16[2,512,512]{2,1,0:T(8,128)(2,1)S(1)} %fusion.rows_ref, bf16[2,512,512]{2,1,0:T(8,128)(2,1)S(1)} %fusion.1.cols_ref, bf16[32,8,256]{2,1,0:T(8,128)(2,1)S(1)} %all-to-all-done.3.refs_0_, bf16[32,8,256]{2,1,0:T(8,128)(2,1)S(1)} %collective-permute-done.8.refs_1_, ...), custom_call_target="tpu_custom_call" | custom-call | tf_op jit(solution)/shard_map/final/final/pallas_call | solution.py:184
  (11 shorter events, 0.0 us)
Async XLA Ops:
  0.0 165.2 %copy-start = (bf16[2,512,512]{2,1,0:T(8,128)(2,1)S(1)}, bf16[2,512,512]{2,1,0:T(8,128)(2,1)}, u32[]{:S(2)}) copy-start(bf16[2,512,512]{2,1,0:T(8,128)(2,1)} %param.9) | copy-start | bytes 3145732
  3.2 10.4 %copy-start.2 = (bf16[1,32,64,512]{3,2,1,0:T(8,128)(2,1)S(1)}, bf16[1,32,64,512]{3,2,1,0:T(8,128)(2,1)}, u32[]{:S(2)}) copy-start(bf16[1,32,64,512]{3,2,1,0:T(8,128)(2,1)} %param.5) | copy-start | bytes 6291460
  3.2 58.6 %all-to-all-start.1 = ((bf16[16,256,256]{2,1,0:T(8,128)(2,1)}), bf16[16,256,256]{2,1,0:T(8,128)(2,1)}, u32[]{:S(2)}, u32[]{:S(2)}) async-start(bf16[16,256,256]{2,1,0:T(8,128)(2,1)} %bitcast.45), calls=%async_computation.1 | async-start | bytes 4194304 | tf_op jit(solution)/shard_map/child_rows/all_to_all | solution.py:212
  13.6 13.5 %copy-start.3 = (s32[1,5,2]{1,2,0:T(2,128)S(1)}, s32[1,5,2]{1,2,0:T(2,128)}, u32[]{:S(2)}) copy-start(s32[1,5,2]{1,2,0:T(2,128)} %param.7) | copy-start | bytes 124
  13.6 33.8 %copy-start.1 = (s32[1,5]{1,0:T(1,128)S(1)}, s32[1,5]{1,0:T(1,128)}, u32[]{:S(2)}) copy-start(s32[1,5]{1,0:T(1,128)} %param.8) | copy-start | bytes 64
  14.7 6.0 %collective-permute-start = (bf16[4,64,512]{2,1,0:T(8,128)(2,1)S(1)}, bf16[4,64,512]{2,1,0:T(8,128)(2,1)S(1)}, u32[]{:S(2)}, u32[]{:S(2)}) collective-permute-start(bf16[4,64,512]{2,1,0:T(8,128)(2,1)S(1)} %get-tuple-element.11), channel_id=1, source_target_pairs={{0,1},{1,0},{2,3},{3,2},{4,5},{5,4},{6,7},{7,6},{8,9},{9,8},{10,11... | collective-permute-start | bytes 786440 | tf_op jit(solution)/shard_map/child_first_leg/ppermute | solution.py:31
  15.6 8.0 %collective-permute-start.1 = (bf16[4,64,512]{2,1,0:T(8,128)(2,1)S(1)}, bf16[4,64,512]{2,1,0:T(8,128)(2,1)S(1)}, u32[]{:S(2)}, u32[]{:S(2)}) collective-permute-start(bf16[4,64,512]{2,1,0:T(8,128)(2,1)S(1)} %get-tuple-element.10), channel_id=1, source_target_pairs={{0,2},{1,3},{2,0},{3,1},{4,6},{5,7},{6,4},{7,5},{8,10},{9,11},{10,... | collective-permute-start | bytes 786440 | tf_op jit(solution)/shard_map/child_first_leg/ppermute | solution.py:31
  16.8 13.2 %collective-permute-start.2 = (bf16[4,64,512]{2,1,0:T(8,128)(2,1)}, bf16[4,64,512]{2,1,0:T(8,128)(2,1)S(1)}, u32[]{:S(2)}, u32[]{:S(2)}) collective-permute-start(bf16[4,64,512]{2,1,0:T(8,128)(2,1)} %get-tuple-element.9), channel_id=1, source_target_pairs={{0,3},{1,2},{2,1},{3,0},{4,7},{5,6},{6,5},{7,4},{8,11},{9,10},{10,... | collective-permute-start | bytes 786440 | tf_op jit(solution)/shard_map/child_first_leg/ppermute | solution.py:31
  17.3 19.9 %collective-permute-start.3 = (bf16[4,64,512]{2,1,0:T(8,128)(2,1)}, bf16[4,64,512]{2,1,0:T(8,128)(2,1)S(1)}, u32[]{:S(2)}, u32[]{:S(2)}) collective-permute-start(bf16[4,64,512]{2,1,0:T(8,128)(2,1)} %get-tuple-element.8), channel_id=1, source_target_pairs={{0,4},{1,5},{2,6},{3,7},{4,0},{5,1},{6,2},{7,3},{8,12},{9,13},{10,... | collective-permute-start | bytes 786440 | tf_op jit(solution)/shard_map/child_first_leg/ppermute | solution.py:31
  20.0 22.8 %collective-permute-start.4 = (bf16[4,64,512]{2,1,0:T(8,128)(2,1)}, bf16[4,64,512]{2,1,0:T(8,128)(2,1)S(1)}, u32[]{:S(2)}, u32[]{:S(2)}) collective-permute-start(bf16[4,64,512]{2,1,0:T(8,128)(2,1)} %get-tuple-element.7), channel_id=1, source_target_pairs={{0,5},{1,4},{2,7},{3,6},{4,1},{5,0},{6,3},{7,2},{8,13},{9,12},{10,... | collective-permute-start | bytes 786440 | tf_op jit(solution)/shard_map/child_first_leg/ppermute | solution.py:31
  20.6 22.2 %collective-permute-start.5 = (bf16[4,64,512]{2,1,0:T(8,128)(2,1)}, bf16[4,64,512]{2,1,0:T(8,128)(2,1)S(1)}, u32[]{:S(2)}, u32[]{:S(2)}) collective-permute-start(bf16[4,64,512]{2,1,0:T(8,128)(2,1)} %get-tuple-element.6), channel_id=1, source_target_pairs={{0,6},{1,7},{2,4},{3,5},{4,2},{5,3},{6,0},{7,1},{8,14},{9,15},{10,... | collective-permute-start | bytes 786440 | tf_op jit(solution)/shard_map/child_first_leg/ppermute | solution.py:31
  23.7 23.7 %collective-permute-start.6 = (bf16[4,64,512]{2,1,0:T(8,128)(2,1)}, bf16[4,64,512]{2,1,0:T(8,128)(2,1)S(1)}, u32[]{:S(2)}, u32[]{:S(2)}) collective-permute-start(bf16[4,64,512]{2,1,0:T(8,128)(2,1)} %get-tuple-element.5), channel_id=1, source_target_pairs={{0,7},{1,6},{2,5},{3,4},{4,3},{5,2},{6,1},{7,0},{8,15},{9,14},{10,... | collective-permute-start | bytes 786440 | tf_op jit(solution)/shard_map/child_first_leg/ppermute | solution.py:31
  61.8 61.7 %all-to-all-start = ((bf16[128,32,256]{2,1,0:T(8,128)(2,1)}), bf16[128,32,256]{2,1,0:T(8,128)(2,1)S(1)}, u32[]{:S(2)}, u32[]{:S(2)}) async-start(bf16[128,32,256]{2,1,0:T(8,128)(2,1)} %bitcast.46), calls=%async_computation | async-start | bytes 4194304 | tf_op jit(solution)/shard_map/summed_rows/all_to_all | solution.py:225
  78.1 45.5 %collective-permute-start.7 = (bf16[8,512,256]{2,1,0:T(8,128)(2,1)}, bf16[8,512,256]{2,1,0:T(8,128)(2,1)}, u32[]{:S(2)}, u32[]{:S(2)}) collective-permute-start(bf16[8,512,256]{2,1,0:T(8,128)(2,1)} %turn.1.own_ref), channel_id=1, source_target_pairs={{0,1},{1,0},{2,3},{3,2},{4,5},{5,4},{6,7},{7,6},{8,9},{9,8},{10,11... | collective-permute-start | bytes 6291464 | tf_op jit(solution)/shard_map/turn/ppermute | solution.py:31
  144.7 16.7 %all-to-all-start.3 = ((bf16[32,8,256]{2,1,0:T(8,128)(2,1)}), bf16[32,8,256]{2,1,0:T(8,128)(2,1)S(1)}, u32[]{:S(2)}, u32[]{:S(2)}) async-start(bf16[32,8,256]{2,1,0:T(8,128)(2,1)} %broadcast_in_dim.4), calls=%async_computation.3 | async-start | bytes 262144 | tf_op jit(solution)/shard_map/gather_row/all_to_all | solution.py:237
  161.4 8.5 %collective-permute-start.9 = (bf16[32,8,256]{2,1,0:T(8,128)(2,1)S(1)}, bf16[32,8,256]{2,1,0:T(8,128)(2,1)S(1)}, u32[]{:S(2)}, u32[]{:S(2)}) collective-permute-start(bf16[32,8,256]{2,1,0:T(8,128)(2,1)S(1)} %all-to-all-done.3.refs_0_), channel_id=1, source_target_pairs={{0,2},{2,0},{4,6},{6,4},{1,3},{3,1},{5,7},{7,5},{8,10},{10,8},{12,... | collective-permute-start | bytes 393224 | tf_op jit(solution)/shard_map/gather_x/ppermute | solution.py:31
  161.7 8.2 %collective-permute-start.11 = (bf16[32,8,256]{2,1,0:T(8,128)(2,1)S(1)}, bf16[32,8,256]{2,1,0:T(8,128)(2,1)S(1)}, u32[]{:S(2)}, u32[]{:S(2)}) collective-permute-start(bf16[32,8,256]{2,1,0:T(8,128)(2,1)S(1)} %all-to-all-done.3.refs_0_), channel_id=1, source_target_pairs={{0,4},{2,6},{4,0},{6,2},{1,5},{3,7},{5,1},{7,3},{8,12},{10,14},{12... | collective-permute-start | bytes 393224 | tf_op jit(solution)/shard_map/gather_x/ppermute | solution.py:31
  163.0 8.4 %collective-permute-start.13 = (bf16[32,8,256]{2,1,0:T(8,128)(2,1)S(1)}, bf16[32,8,256]{2,1,0:T(8,128)(2,1)S(1)}, u32[]{:S(2)}, u32[]{:S(2)}) collective-permute-start(bf16[32,8,256]{2,1,0:T(8,128)(2,1)S(1)} %all-to-all-done.3.refs_0_), channel_id=1, source_target_pairs={{0,6},{2,4},{4,2},{6,0},{1,7},{3,5},{5,3},{7,1},{8,14},{10,12},{12... | collective-permute-start | bytes 393224 | tf_op jit(solution)/shard_map/gather_x/ppermute | solution.py:31
  166.0 8.1 %collective-permute-start.8 = (bf16[32,8,256]{2,1,0:T(8,128)(2,1)S(1)}, bf16[32,8,256]{2,1,0:T(8,128)(2,1)S(1)}, u32[]{:S(2)}, u32[]{:S(2)}) collective-permute-start(bf16[32,8,256]{2,1,0:T(8,128)(2,1)S(1)} %all-to-all-done.3.refs_0_), channel_id=1, source_target_pairs={{0,1},{1,0},{2,3},{3,2},{4,5},{5,4},{6,7},{7,6},{8,9},{9,8},{10,11... | collective-permute-start | bytes 393224 | tf_op jit(solution)/shard_map/gather_e/ppermute | solution.py:31
  169.8 4.3 %collective-permute-start.10 = (bf16[32,8,256]{2,1,0:T(8,128)(2,1)S(1)}, bf16[32,8,256]{2,1,0:T(8,128)(2,1)S(1)}, u32[]{:S(2)}, u32[]{:S(2)}) collective-permute-start(bf16[32,8,256]{2,1,0:T(8,128)(2,1)S(1)} %collective-permute-done.9.refs_2_), channel_id=1, source_target_pairs={{0,1},{1,0},{2,3},{3,2},{4,5},{5,4},{6,7},{7,6},{8,9},{9,8},{10,11... | collective-permute-start | bytes 393224 | tf_op jit(solution)/shard_map/gather_e/ppermute | solution.py:31
  170.0 4.2 %collective-permute-start.12 = (bf16[32,8,256]{2,1,0:T(8,128)(2,1)S(1)}, bf16[32,8,256]{2,1,0:T(8,128)(2,1)S(1)}, u32[]{:S(2)}, u32[]{:S(2)}) collective-permute-start(bf16[32,8,256]{2,1,0:T(8,128)(2,1)S(1)} %collective-permute-done.11.refs_4_), channel_id=1, source_target_pairs={{0,1},{1,0},{2,3},{3,2},{4,5},{5,4},{6,7},{7,6},{8,9},{9,8},{10,11... | collective-permute-start | bytes 393224 | tf_op jit(solution)/shard_map/gather_e/ppermute | solution.py:31
  171.4 2.8 %collective-permute-start.14 = (bf16[32,8,256]{2,1,0:T(8,128)(2,1)S(1)}, bf16[32,8,256]{2,1,0:T(8,128)(2,1)S(1)}, u32[]{:S(2)}, u32[]{:S(2)}) collective-permute-start(bf16[32,8,256]{2,1,0:T(8,128)(2,1)S(1)} %collective-permute-done.13.refs_6_), channel_id=1, source_target_pairs={{0,1},{1,0},{2,3},{3,2},{4,5},{5,4},{6,7},{7,6},{8,9},{9,8},{10,11... | collective-permute-start | bytes 393224 | tf_op jit(solution)/shard_map/gather_e/ppermute | solution.py:31

commit v3 on v2

--- a/solution.py
+++ b/solution.py
@@ -9,10 +9,12 @@
 BF = jnp.bfloat16
 F32 = jnp.float32
 NZ, NY, NX, NE = 8, 2, 4, 2
+NF, NL = 2, 4
 COL = ("x", "e")
-ROW = ("z", "y")
-ROW_COL = ROW + COL
-ALL = ("half",) + ROW_COL
+ROW = ("far", "near", "y")
+ALL = ("half",) + ROW + COL
+MIXED_ROW = ("near", "far", "y")
+MIXED_ALL = COL + ("y", "near", "far")
 VMEM = pl.BlockSpec(memory_space=pltpu.VMEM)
 SMEM = pl.BlockSpec(memory_space=pltpu.SMEM)
 HBM = pl.BlockSpec(memory_space=pltpu.HBM)
@@ -88,15 +90,16 @@
             for e in range(NE):
                 at = x * 128 + e * 64
                 for y in range(NY):
-                    block = acc[a, at : at + 64, y * 256 : (y + 1) * 256]
-                    out_ref[:, y, x, a // 2, a % 2, e] = block.astype(BF).reshape(NZ, 8, 256)
+                    block = acc[a, at : at + 64, y * 256 : (y + 1) * 256].astype(BF).reshape(NF, NL, 8, 256)
+                    for far in range(NF):
+                        out_ref[x, a // 2, y, :, far, a % 2, e] = block[far]
 
 
 def apply_terms(me, site, leg, table, arrived):
     sites = table.shape[1]
     return pl.pallas_call(
         terms_kernel,
-        out_shape=jax.ShapeDtypeStruct((NZ, NY, NX, NE, 2, NE, 8, 256), BF),
+        out_shape=jax.ShapeDtypeStruct((NX, NE, NY, NL, NF, 2, NE, 8, 256), BF),
         in_specs=[SMEM] * 3 + [HBM] + [VMEM] * (NX * NE),
         out_specs=VMEM,
         scratch_shapes=[
@@ -116,14 +119,18 @@
 
 
 def turned(value):
-    rows, depth, lanes = value.shape
-    step = 64
+    peers, rows, depth, lanes = value.shape
+
+    def place(i):
+        near, far, y = i // (NF * NY), i // NY % NF, i % NY
+        return 0, (far * NL + near) * NY + y, 0
+
     return pl.pallas_call(
         turn_kernel,
-        out_shape=jax.ShapeDtypeStruct((depth, rows, lanes), BF),
-        grid=(rows // step,),
-        in_specs=[pl.BlockSpec((step, depth, lanes), lambda i: (i, 0, 0))],
-        out_specs=pl.BlockSpec((depth, step, lanes), lambda i: (0, i, 0)),
+        out_shape=jax.ShapeDtypeStruct((depth, peers * rows, lanes), BF),
+        grid=(peers,),
+        in_specs=[pl.BlockSpec((None, rows, depth, lanes), lambda i: (i, 0, 0, 0))],
+        out_specs=pl.BlockSpec((depth, rows, lanes), place),
         compiler_params=vmem(50),
         name="turn",
     )(value)
@@ -196,7 +203,8 @@
 
 
 def reordered(parent):
-    wanted = jnp.arange(512).reshape(128, NE, 2).swapaxes(0, 1).reshape(512)
+    wanted = jnp.arange(512).reshape(NF, NL, NY, NX, NE, NE, 2)
+    wanted = wanted.transpose(5, 3, 4, 2, 1, 0, 6).reshape(512)
     pick = (jnp.arange(512)[:, None] == wanted[None, :]).astype(BF)
     by_rows = jnp.einsum("aq,cab->cqb", pick, parent, preferred_element_type=F32)
     by_cols = jnp.einsum("cab,bq->caq", parent, pick, preferred_element_type=F32)
@@ -207,9 +215,9 @@
     me = jnp.stack([lax.axis_index(a) for a in ("e", "x")]).astype(jnp.int32)
     child = children[0]
     with jax.named_scope("child_rows"):
-        cut = child.reshape(32, NZ, 8, NY, 256).transpose(1, 3, 0, 2, 4)
+        cut = child.reshape(32, NF, NL, 8, NY, 256).transpose(2, 1, 4, 0, 3, 5)
         cut = cut.reshape(NZ * NY, 32 * 8, 256)
-        child_all = lax.all_to_all(cut, ROW, 0, 0, tiled=True)
+        child_all = lax.all_to_all(cut, MIXED_ROW, 0, 0, tiled=True)
     with jax.named_scope("child_first_leg"):
         col = lax.axis_index(COL)
         blocks = child.reshape(NX * NE, 4, 64, 512)
@@ -222,15 +230,15 @@
             me, term_site[0], term_leg[0], operators[0], arrived
         )
     with jax.named_scope("summed_rows"):
-        summed = lax.all_to_all(summed.reshape(128, 32, 256), ROW_COL, 0, 0, tiled=True)
+        summed = lax.all_to_all(summed.reshape(128, 32, 256), MIXED_ALL, 0, 0, tiled=True)
     with jax.named_scope("turn"):
-        own = turned(child_all.reshape(512, 8, 256))
+        own = turned(child_all.reshape(NZ * NY, 32, 8, 256))
         other = swap(own, ("e",), 1)
         by_rows, by_cols = reordered(parent)
     with jax.named_scope("gram"):
         part = gram(me, summed.reshape(128, 2, NE, 8, 256), own, other)
     with jax.named_scope("sum"):
-        parts = lax.all_to_all(part.reshape(64, 8, 256), ("z", "y", "x"), 0, 0, tiled=True)
+        parts = lax.all_to_all(part.reshape(64, 8, 256), ROW + ("x",), 0, 0, tiled=True)
         env = jnp.sum(parts.astype(F32), axis=0).astype(BF)
     with jax.named_scope("gather_row"):
         env = jnp.broadcast_to(env, (2 * NZ * NY, 8, 256))
@@ -247,7 +255,7 @@
 
 def solution(mesh):
     torus = Mesh(
-        mesh.devices.reshape(2, NZ, NY, NX, NE), ("half", "z", "y", "x", "e")
+        mesh.devices.reshape(2, NF, NL, NY, NX, NE), ALL
     )
     in_specs = (
         P("half", ROW, COL, None),

time: 178 us -> 181 us (1.017)
  Pallas kernels: 25.3 us -> 28.1 us
  waiting for transfers between devices: 76.7 us -> 74.8 us
    pallas_call x2, Pallas kernels: 18.8 us -> 21.5 us  [the longest x1 11.8 us: apply_terms(): pl.pallas_call(terms_kernel, out_shape=jax.ShapeDtypeStruct((NX, NE, NY,...]
    all_to_all x2, starting transfers between devices: 20.7 us -> 23.2 us  [the longest x1 12.9 us: on_device(): lax.all_to_all(summed.reshape(128, 32, 256), MIXED_ALL, 0, 0, tiled=True)]
  transfers between devices with their start and end apart: 18 -> 18, of which waited for: 9 -> 9; matrix products, arithmetic and copies ran while one was open for 2% -> 2% of each run, Pallas kernels for 11% -> 12%
where the time goes in v3:
time: 181 us
  waiting for transfers between devices  74.8 us (41%)
  starting transfers between devices  53 us (29%)
  Pallas kernels  28.1 us (16%)
  blocking collectives  17.7 us (10%)
  local copies, waits for them, and re-layouts  5.23 us (3%)
    all_to_all x1, waiting for transfers between devices, on_device(): lax.all_to_all(summed.reshape(128, 32, 256), MIXED_ALL, 0, 0, tiled=True)  41 us
    ppermute x15, starting transfers between devices, swap(): return lax.ppermute(value, axes, [(i, i ^ offset) for i in range(peers)])  23.8 us
    ppermute x15, waiting for transfers between devices, swap(): return lax.ppermute(value, axes, [(i, i ^ offset) for i in range(peers)])  20.7 us
    all_to_all x1, blocking collectives, on_device(): lax.all_to_all(part.reshape(64, 8, 256), ROW + ('x',), 0, 0, tiled=True)  17.7 us
    all_to_all x1, starting transfers between devices, on_device(): lax.all_to_all(summed.reshape(128, 32, 256), MIXED_ALL, 0, 0, tiled=True)  12.9 us
    pallas_call x1, Pallas kernels, apply_terms(): pl.pallas_call(terms_kernel, out_shape=jax.ShapeDtypeStruct((NX, NE, NY,...  11.8 us
    all_to_all x1, starting transfers between devices, on_device(): child_all = lax.all_to_all(cut, MIXED_ROW, 0, 0, tiled=True)  10.3 us
    pallas_call x1, Pallas kernels, turned(): pl.pallas_call(turn_kernel, out_shape=jax.ShapeDtypeStruct((depth, peers...  9.74 us
  transfers between devices with their start and end apart: 18, of which 9 were waited for; matrix products, arithmetic and copies ran while one was open for 2% of the time, Pallas kernels for 12%

profile of v3, /device:TPU:1, one launch (start us, length us, event | category | flops | bytes accessed | tf_op | source)
XLA Modules:
  0.0 180.8 jit_solution(14233283667590816779)
XLA Ops:
  0.0 3.2 %copy.11 = bf16[4,2,2,32,8,256]{5,4,3,2,1,0:T(8,128)(2,1)} copy(bf16[4,2,2,32,8,256]{5,4,2,0,1,3:T(8,128)(2,1)} %bitcast.43) | data formatting | bytes 4194304 | tf_op jit(solution)/shard_map/child_rows/transpose | solution.py:218
  3.2 10.3 %all-to-all-start.1 = ((bf16[16,256,256]{2,1,0:T(8,128)(2,1)}), bf16[16,256,256]{2,1,0:T(8,128)(2,1)}, u32[]{:S(2)}, u32[]{:S(2)}) async-start(bf16[16,256,256]{2,1,0:T(8,128)(2,1)} %bitcast.45), calls=%async_computation.1 | async-start | bytes 4194304 | tf_op jit(solution)/shard_map/child_rows/all_to_all | solution.py:220
  13.6 0.0 copy-start.3
  13.6 0.0 copy-start.1
  13.6 1.1 dynamic-slice_bitcast_fusion
  14.7 1.0 collective-permute-start
  15.6 1.2 collective-permute-start.1
  16.8 0.4 collective-permute-start.2
  17.3 2.7 %collective-permute-start.3 = (bf16[4,64,512]{2,1,0:T(8,128)(2,1)}, bf16[4,64,512]{2,1,0:T(8,128)(2,1)S(1)}, u32[]{:S(2)}, u32[]{:S(2)}) collective-permute-start(bf16[4,64,512]{2,1,0:T(8,128)(2,1)} %get-tuple-element.8), channel_id=1, source_target_pairs={{0,4},{1,5},{2,6},{3,7},{4,0},{5,1},{6,2},{7,3},{8,12},{9,13},{10,... | collective-permute-start | bytes 786440 | tf_op jit(solution)/shard_map/child_first_leg/ppermute | solution.py:33
  20.0 0.6 collective-permute-start.4
  20.6 0.0 collective-permute-done.refs_1_
  20.6 2.5 %collective-permute-start.5 = (bf16[4,64,512]{2,1,0:T(8,128)(2,1)}, bf16[4,64,512]{2,1,0:T(8,128)(2,1)S(1)}, u32[]{:S(2)}, u32[]{:S(2)}) collective-permute-start(bf16[4,64,512]{2,1,0:T(8,128)(2,1)} %get-tuple-element.6), channel_id=1, source_target_pairs={{0,6},{1,7},{2,4},{3,5},{4,2},{5,3},{6,0},{7,1},{8,14},{9,15},{10,... | collective-permute-start | bytes 786440 | tf_op jit(solution)/shard_map/child_first_leg/ppermute | solution.py:33
  23.1 0.6 collective-permute-done.1.refs_2_
  23.7 3.4 %collective-permute-start.6 = (bf16[4,64,512]{2,1,0:T(8,128)(2,1)}, bf16[4,64,512]{2,1,0:T(8,128)(2,1)S(1)}, u32[]{:S(2)}, u32[]{:S(2)}) collective-permute-start(bf16[4,64,512]{2,1,0:T(8,128)(2,1)} %get-tuple-element.5), channel_id=1, source_target_pairs={{0,7},{1,6},{2,5},{3,4},{4,3},{5,2},{6,1},{7,0},{8,15},{9,14},{10,... | collective-permute-start | bytes 786440 | tf_op jit(solution)/shard_map/child_first_leg/ppermute | solution.py:33
  27.1 0.1 copy.10.site
  27.2 0.1 pad_add_fusion.me
  27.3 2.8 %collective-permute-done.2.refs_3_ = bf16[4,64,512]{2,1,0:T(8,128)(2,1)S(1)} collective-permute-done((bf16[4,64,512]{2,1,0:T(8,128)(2,1)}, bf16[4,64,512]{2,1,0:T(8,128)(2,1)S(1)}, u32[]{:S(2)}, u32[]{:S(2)}) %collective-permute-start.2) | collective-permute-done | bytes 262176 | tf_op jit(solution)/shard_map/child_first_leg/ppermute | solution.py:33
  30.1 7.1 %collective-permute-done.3.refs_4_ = bf16[4,64,512]{2,1,0:T(8,128)(2,1)S(1)} collective-permute-done((bf16[4,64,512]{2,1,0:T(8,128)(2,1)}, bf16[4,64,512]{2,1,0:T(8,128)(2,1)S(1)}, u32[]{:S(2)}, u32[]{:S(2)}) %collective-permute-start.3) | collective-permute-done | bytes 262176 | tf_op jit(solution)/shard_map/child_first_leg/ppermute | solution.py:33
  37.1 6.0 %collective-permute-done.4.refs_5_ = bf16[4,64,512]{2,1,0:T(8,128)(2,1)S(1)} collective-permute-done((bf16[4,64,512]{2,1,0:T(8,128)(2,1)}, bf16[4,64,512]{2,1,0:T(8,128)(2,1)S(1)}, u32[]{:S(2)}, u32[]{:S(2)}) %collective-permute-start.4) | collective-permute-done | bytes 262176 | tf_op jit(solution)/shard_map/child_first_leg/ppermute | solution.py:33
  43.2 0.0 collective-permute-done.5.refs_6_
  43.2 4.2 %collective-permute-done.6.refs_7_ = bf16[4,64,512]{2,1,0:T(8,128)(2,1)S(1)} collective-permute-done((bf16[4,64,512]{2,1,0:T(8,128)(2,1)}, bf16[4,64,512]{2,1,0:T(8,128)(2,1)S(1)}, u32[]{:S(2)}, u32[]{:S(2)}) %collective-permute-start.6) | collective-permute-done | bytes 262176 | tf_op jit(solution)/shard_map/child_first_leg/ppermute | solution.py:33
  47.3 11.8 %terms.1 = bf16[4,2,2,4,2,2,2,8,256]{8,7,6,5,4,3,2,1,0:T(8,128)(2,1)} custom-call(s32[2]{0:T(128)S(1)} %pad_add_fusion.me, s32[5,2]{1,0:T(8,128)S(1)} %copy.10.site, s32[5]{0:T(128)S(1)} %bitcast.42, bf16[2,4,512,512]{3,2,1,0:T(8,128)(2,1)} %bitcast.47, bf16[4,64,512]{2,1,0:T(8,128)(2,1)S(1)} %get-tuple-element.12.refs_0_, ...), custom_call_target="tpu_custom_call" | custom-call | tf_op jit(solution)/shard_map/terms/terms/pallas_call | solution.py:100
  59.2 3.4 %all-to-all-done.1 = bf16[16,256,256]{2,1,0:T(8,128)(2,1)} async-done(((bf16[16,256,256]{2,1,0:T(8,128)(2,1)}), bf16[16,256,256]{2,1,0:T(8,128)(2,1)}, u32[]{:S(2)}, u32[]{:S(2)}) %all-to-all-start.1) | async-done | bytes 2097184 | tf_op jit(solution)/shard_map/child_rows/all_to_all | solution.py:220
  62.5 12.9 %all-to-all-start = ((bf16[128,32,256]{2,1,0:T(8,128)(2,1)}), bf16[128,32,256]{2,1,0:T(8,128)(2,1)S(1)}, u32[]{:S(2)}, u32[]{:S(2)}) async-start(bf16[128,32,256]{2,1,0:T(8,128)(2,1)} %bitcast.46), calls=%async_computation | async-start | bytes 4194304 | tf_op jit(solution)/shard_map/summed_rows/all_to_all | solution.py:233
  75.4 9.7 %turn.1.own_ref = bf16[8,512,256]{2,1,0:T(8,128)(2,1)} custom-call(bf16[16,32,8,256]{3,2,1,0:T(8,128)(2,1)} %bitcast.22.in_ref), custom_call_target="tpu_custom_call" | custom-call | tf_op jit(solution)/shard_map/turn/turn/pallas_call | solution.py:128
  85.1 0.9 collective-permute-start.7
  86.0 41.0 %all-to-all-done = bf16[128,32,256]{2,1,0:T(8,128)(2,1)S(1)} async-done(((bf16[128,32,256]{2,1,0:T(8,128)(2,1)}), bf16[128,32,256]{2,1,0:T(8,128)(2,1)S(1)}, u32[]{:S(2)}, u32[]{:S(2)}) %all-to-all-start) | async-done | bytes 2097184 | tf_op jit(solution)/shard_map/summed_rows/all_to_all | solution.py:233
  127.0 0.0 collective-permute-done.7.other_ref
  127.0 3.6 %gram.1 = bf16[8,2,4,8,256]{4,3,2,1,0:T(8,128)(2,1)S(1)} custom-call(s32[2]{0:T(128)S(1)} %pad_add_fusion.me, bf16[128,2,2,8,256]{4,3,2,1,0:T(8,128)(2,1)S(1)} %bitcast.40, bf16[8,512,256]{2,1,0:T(8,128)(2,1)} %turn.1.own_ref, bf16[8,512,256]{2,1,0:T(8,128)(2,1)} %collective-permute-done.7.other_ref), custom_call_target="tpu_custom_call" | custom-call | tf_op jit(solution)/shard_map/gram/gram/pallas_call | solution.py:157
  130.6 17.7 %all_to_all.20 = bf16[64,8,256]{2,1,0:T(8,128)(2,1)S(1)} all-to-all(bf16[64,8,256]{2,1,0:T(8,128)(2,1)S(1)} %bitcast.41), channel_id=1, replica_groups=mesh['half'=2,'far'=2,'near'=4,'y'=2,'x'=4,'e'=2] {'far','near','y','x'}, dimensions={0} | all-to-all | bytes 524288 | tf_op jit(solution)/shard_map/sum/all_to_all | solution.py:241
  148.3 0.1 reduce_sum.12
  148.4 0.7 broadcast_in_dim.4
  149.0 6.1 %all-to-all-start.3 = ((bf16[32,8,256]{2,1,0:T(8,128)(2,1)}), bf16[32,8,256]{2,1,0:T(8,128)(2,1)S(1)}, u32[]{:S(2)}, u32[]{:S(2)}) async-start(bf16[32,8,256]{2,1,0:T(8,128)(2,1)} %broadcast_in_dim.4), calls=%async_computation.3 | async-start | bytes 262144 | tf_op jit(solution)/shard_map/gather_row/all_to_all | solution.py:245
  155.2 0.2 reshape.194
  155.4 9.7 %all-to-all-done.3.refs_0_ = bf16[32,8,256]{2,1,0:T(8,128)(2,1)S(1)} async-done(((bf16[32,8,256]{2,1,0:T(8,128)(2,1)}), bf16[32,8,256]{2,1,0:T(8,128)(2,1)S(1)}, u32[]{:S(2)}, u32[]{:S(2)}) %all-to-all-start.3) | async-done | bytes 131104 | tf_op jit(solution)/shard_map/gather_row/all_to_all | solution.py:245
  165.1 0.3 collective-permute-start.9
  165.4 1.6 collective-permute-start.11
  167.0 2.0 %collective-permute-start.13 = (bf16[32,8,256]{2,1,0:T(8,128)(2,1)S(1)}, bf16[32,8,256]{2,1,0:T(8,128)(2,1)S(1)}, u32[]{:S(2)}, u32[]{:S(2)}) collective-permute-start(bf16[32,8,256]{2,1,0:T(8,128)(2,1)S(1)} %all-to-all-done.3.refs_0_), channel_id=1, source_target_pairs={{0,6},{2,4},{4,2},{6,0},{1,7},{3,5},{5,3},{7,1},{8,14},{10,12},{12... | collective-permute-start | bytes 393224 | tf_op jit(solution)/shard_map/gather_x/ppermute | solution.py:33
  168.9 0.7 fusion.rows_ref
  169.7 3.8 %collective-permute-start.8 = (bf16[32,8,256]{2,1,0:T(8,128)(2,1)S(1)}, bf16[32,8,256]{2,1,0:T(8,128)(2,1)S(1)}, u32[]{:S(2)}, u32[]{:S(2)}) collective-permute-start(bf16[32,8,256]{2,1,0:T(8,128)(2,1)S(1)} %all-to-all-done.3.refs_0_), channel_id=1, source_target_pairs={{0,1},{1,0},{2,3},{3,2},{4,5},{5,4},{6,7},{7,6},{8,9},{9,8},{10,11... | collective-permute-start | bytes 393224 | tf_op jit(solution)/shard_map/gather_e/ppermute | solution.py:33
  173.5 0.1 collective-permute-start.10
  173.6 1.5 collective-permute-start.12
  175.0 1.8 %collective-permute-start.14 = (bf16[32,8,256]{2,1,0:T(8,128)(2,1)S(1)}, bf16[32,8,256]{2,1,0:T(8,128)(2,1)S(1)}, u32[]{:S(2)}, u32[]{:S(2)}) collective-permute-start(bf16[32,8,256]{2,1,0:T(8,128)(2,1)S(1)} %collective-permute-done.13.refs_6_), channel_id=1, source_target_pairs={{0,1},{1,0},{2,3},{3,2},{4,5},{5,4},{6,7},{7,6},{8,9},{9,8},{10,11... | collective-permute-start | bytes 393224 | tf_op jit(solution)/shard_map/gather_e/ppermute | solution.py:33
  176.9 0.9 fusion.1.cols_ref
  177.8 0.0 collective-permute-done.8.refs_1_
  177.8 0.0 collective-permute-done.12.refs_5_
  177.8 0.1 collective-permute-done.14.refs_7_
  177.9 2.9 %final.1 = bf16[2,512,512]{2,1,0:T(8,128)(2,1)} custom-call(s32[2]{0:T(128)S(1)} %pad_add_fusion.me, bf16[2,512,512]{2,1,0:T(8,128)(2,1)S(1)} %fusion.rows_ref, bf16[2,512,512]{2,1,0:T(8,128)(2,1)S(1)} %fusion.1.cols_ref, bf16[32,8,256]{2,1,0:T(8,128)(2,1)S(1)} %all-to-all-done.3.refs_0_, bf16[32,8,256]{2,1,0:T(8,128)(2,1)S(1)} %collective-permute-done.8.refs_1_, ...), custom_call_target="tpu_custom_call" | custom-call | tf_op jit(solution)/shard_map/final/final/pallas_call | solution.py:191
  (11 shorter events, 0.1 us)
Async XLA Ops:
  0.0 168.9 %copy-start = (bf16[2,512,512]{2,1,0:T(8,128)(2,1)S(1)}, bf16[2,512,512]{2,1,0:T(8,128)(2,1)}, u32[]{:S(2)}) copy-start(bf16[2,512,512]{2,1,0:T(8,128)(2,1)} %param.9) | copy-start | bytes 3145732
  3.2 10.4 %copy-start.2 = (bf16[1,32,64,512]{3,2,1,0:T(8,128)(2,1)S(1)}, bf16[1,32,64,512]{3,2,1,0:T(8,128)(2,1)}, u32[]{:S(2)}) copy-start(bf16[1,32,64,512]{3,2,1,0:T(8,128)(2,1)} %param.5) | copy-start | bytes 6291460
  3.2 59.3 %all-to-all-start.1 = ((bf16[16,256,256]{2,1,0:T(8,128)(2,1)}), bf16[16,256,256]{2,1,0:T(8,128)(2,1)}, u32[]{:S(2)}, u32[]{:S(2)}) async-start(bf16[16,256,256]{2,1,0:T(8,128)(2,1)} %bitcast.45), calls=%async_computation.1 | async-start | bytes 4194304 | tf_op jit(solution)/shard_map/child_rows/all_to_all | solution.py:220
  13.6 13.5 %copy-start.3 = (s32[1,5,2]{1,2,0:T(2,128)S(1)}, s32[1,5,2]{1,2,0:T(2,128)}, u32[]{:S(2)}) copy-start(s32[1,5,2]{1,2,0:T(2,128)} %param.7) | copy-start | bytes 124
  13.6 33.8 %copy-start.1 = (s32[1,5]{1,0:T(1,128)S(1)}, s32[1,5]{1,0:T(1,128)}, u32[]{:S(2)}) copy-start(s32[1,5]{1,0:T(1,128)} %param.8) | copy-start | bytes 64
  14.7 6.0 %collective-permute-start = (bf16[4,64,512]{2,1,0:T(8,128)(2,1)S(1)}, bf16[4,64,512]{2,1,0:T(8,128)(2,1)S(1)}, u32[]{:S(2)}, u32[]{:S(2)}) collective-permute-start(bf16[4,64,512]{2,1,0:T(8,128)(2,1)S(1)} %get-tuple-element.11), channel_id=1, source_target_pairs={{0,1},{1,0},{2,3},{3,2},{4,5},{5,4},{6,7},{7,6},{8,9},{9,8},{10,11... | collective-permute-start | bytes 786440 | tf_op jit(solution)/shard_map/child_first_leg/ppermute | solution.py:33
  15.6 8.0 %collective-permute-start.1 = (bf16[4,64,512]{2,1,0:T(8,128)(2,1)S(1)}, bf16[4,64,512]{2,1,0:T(8,128)(2,1)S(1)}, u32[]{:S(2)}, u32[]{:S(2)}) collective-permute-start(bf16[4,64,512]{2,1,0:T(8,128)(2,1)S(1)} %get-tuple-element.10), channel_id=1, source_target_pairs={{0,2},{1,3},{2,0},{3,1},{4,6},{5,7},{6,4},{7,5},{8,10},{9,11},{10,... | collective-permute-start | bytes 786440 | tf_op jit(solution)/shard_map/child_first_leg/ppermute | solution.py:33
  16.8 13.2 %collective-permute-start.2 = (bf16[4,64,512]{2,1,0:T(8,128)(2,1)}, bf16[4,64,512]{2,1,0:T(8,128)(2,1)S(1)}, u32[]{:S(2)}, u32[]{:S(2)}) collective-permute-start(bf16[4,64,512]{2,1,0:T(8,128)(2,1)} %get-tuple-element.9), channel_id=1, source_target_pairs={{0,3},{1,2},{2,1},{3,0},{4,7},{5,6},{6,5},{7,4},{8,11},{9,10},{10,... | collective-permute-start | bytes 786440 | tf_op jit(solution)/shard_map/child_first_leg/ppermute | solution.py:33
  17.3 19.9 %collective-permute-start.3 = (bf16[4,64,512]{2,1,0:T(8,128)(2,1)}, bf16[4,64,512]{2,1,0:T(8,128)(2,1)S(1)}, u32[]{:S(2)}, u32[]{:S(2)}) collective-permute-start(bf16[4,64,512]{2,1,0:T(8,128)(2,1)} %get-tuple-element.8), channel_id=1, source_target_pairs={{0,4},{1,5},{2,6},{3,7},{4,0},{5,1},{6,2},{7,3},{8,12},{9,13},{10,... | collective-permute-start | bytes 786440 | tf_op jit(solution)/shard_map/child_first_leg/ppermute | solution.py:33
  20.0 23.1 %collective-permute-start.4 = (bf16[4,64,512]{2,1,0:T(8,128)(2,1)}, bf16[4,64,512]{2,1,0:T(8,128)(2,1)S(1)}, u32[]{:S(2)}, u32[]{:S(2)}) collective-permute-start(bf16[4,64,512]{2,1,0:T(8,128)(2,1)} %get-tuple-element.7), channel_id=1, source_target_pairs={{0,5},{1,4},{2,7},{3,6},{4,1},{5,0},{6,3},{7,2},{8,13},{9,12},{10,... | collective-permute-start | bytes 786440 | tf_op jit(solution)/shard_map/child_first_leg/ppermute | solution.py:33
  20.6 22.5 %collective-permute-start.5 = (bf16[4,64,512]{2,1,0:T(8,128)(2,1)}, bf16[4,64,512]{2,1,0:T(8,128)(2,1)S(1)}, u32[]{:S(2)}, u32[]{:S(2)}) collective-permute-start(bf16[4,64,512]{2,1,0:T(8,128)(2,1)} %get-tuple-element.6), channel_id=1, source_target_pairs={{0,6},{1,7},{2,4},{3,5},{4,2},{5,3},{6,0},{7,1},{8,14},{9,15},{10,... | collective-permute-start | bytes 786440 | tf_op jit(solution)/shard_map/child_first_leg/ppermute | solution.py:33
  23.7 23.7 %collective-permute-start.6 = (bf16[4,64,512]{2,1,0:T(8,128)(2,1)}, bf16[4,64,512]{2,1,0:T(8,128)(2,1)S(1)}, u32[]{:S(2)}, u32[]{:S(2)}) collective-permute-start(bf16[4,64,512]{2,1,0:T(8,128)(2,1)} %get-tuple-element.5), channel_id=1, source_target_pairs={{0,7},{1,6},{2,5},{3,4},{4,3},{5,2},{6,1},{7,0},{8,15},{9,14},{10,... | collective-permute-start | bytes 786440 | tf_op jit(solution)/shard_map/child_first_leg/ppermute | solution.py:33
  62.5 64.5 %all-to-all-start = ((bf16[128,32,256]{2,1,0:T(8,128)(2,1)}), bf16[128,32,256]{2,1,0:T(8,128)(2,1)S(1)}, u32[]{:S(2)}, u32[]{:S(2)}) async-start(bf16[128,32,256]{2,1,0:T(8,128)(2,1)} %bitcast.46), calls=%async_computation | async-start | bytes 4194304 | tf_op jit(solution)/shard_map/summed_rows/all_to_all | solution.py:233
  85.1 41.9 %collective-permute-start.7 = (bf16[8,512,256]{2,1,0:T(8,128)(2,1)}, bf16[8,512,256]{2,1,0:T(8,128)(2,1)}, u32[]{:S(2)}, u32[]{:S(2)}) collective-permute-start(bf16[8,512,256]{2,1,0:T(8,128)(2,1)} %turn.1.own_ref), channel_id=1, source_target_pairs={{0,1},{1,0},{2,3},{3,2},{4,5},{5,4},{6,7},{7,6},{8,9},{9,8},{10,11... | collective-permute-start | bytes 6291464 | tf_op jit(solution)/shard_map/turn/ppermute | solution.py:33
  149.0 16.0 %all-to-all-start.3 = ((bf16[32,8,256]{2,1,0:T(8,128)(2,1)}), bf16[32,8,256]{2,1,0:T(8,128)(2,1)S(1)}, u32[]{:S(2)}, u32[]{:S(2)}) async-start(bf16[32,8,256]{2,1,0:T(8,128)(2,1)} %broadcast_in_dim.4), calls=%async_computation.3 | async-start | bytes 262144 | tf_op jit(solution)/shard_map/gather_row/all_to_all | solution.py:245
  165.1 8.4 %collective-permute-start.9 = (bf16[32,8,256]{2,1,0:T(8,128)(2,1)S(1)}, bf16[32,8,256]{2,1,0:T(8,128)(2,1)S(1)}, u32[]{:S(2)}, u32[]{:S(2)}) collective-permute-start(bf16[32,8,256]{2,1,0:T(8,128)(2,1)S(1)} %all-to-all-done.3.refs_0_), channel_id=1, source_target_pairs={{0,2},{2,0},{4,6},{6,4},{1,3},{3,1},{5,7},{7,5},{8,10},{10,8},{12,... | collective-permute-start | bytes 393224 | tf_op jit(solution)/shard_map/gather_x/ppermute | solution.py:33
  165.4 8.2 %collective-permute-start.11 = (bf16[32,8,256]{2,1,0:T(8,128)(2,1)S(1)}, bf16[32,8,256]{2,1,0:T(8,128)(2,1)S(1)}, u32[]{:S(2)}, u32[]{:S(2)}) collective-permute-start(bf16[32,8,256]{2,1,0:T(8,128)(2,1)S(1)} %all-to-all-done.3.refs_0_), channel_id=1, source_target_pairs={{0,4},{2,6},{4,0},{6,2},{1,5},{3,7},{5,1},{7,3},{8,12},{10,14},{12... | collective-permute-start | bytes 393224 | tf_op jit(solution)/shard_map/gather_x/ppermute | solution.py:33
  167.0 8.1 %collective-permute-start.13 = (bf16[32,8,256]{2,1,0:T(8,128)(2,1)S(1)}, bf16[32,8,256]{2,1,0:T(8,128)(2,1)S(1)}, u32[]{:S(2)}, u32[]{:S(2)}) collective-permute-start(bf16[32,8,256]{2,1,0:T(8,128)(2,1)S(1)} %all-to-all-done.3.refs_0_), channel_id=1, source_target_pairs={{0,6},{2,4},{4,2},{6,0},{1,7},{3,5},{5,3},{7,1},{8,14},{10,12},{12... | collective-permute-start | bytes 393224 | tf_op jit(solution)/shard_map/gather_x/ppermute | solution.py:33
  169.7 8.1 %collective-permute-start.8 = (bf16[32,8,256]{2,1,0:T(8,128)(2,1)S(1)}, bf16[32,8,256]{2,1,0:T(8,128)(2,1)S(1)}, u32[]{:S(2)}, u32[]{:S(2)}) collective-permute-start(bf16[32,8,256]{2,1,0:T(8,128)(2,1)S(1)} %all-to-all-done.3.refs_0_), channel_id=1, source_target_pairs={{0,1},{1,0},{2,3},{3,2},{4,5},{5,4},{6,7},{7,6},{8,9},{9,8},{10,11... | collective-permute-start | bytes 393224 | tf_op jit(solution)/shard_map/gather_e/ppermute | solution.py:33
  173.5 4.3 %collective-permute-start.10 = (bf16[32,8,256]{2,1,0:T(8,128)(2,1)S(1)}, bf16[32,8,256]{2,1,0:T(8,128)(2,1)S(1)}, u32[]{:S(2)}, u32[]{:S(2)}) collective-permute-start(bf16[32,8,256]{2,1,0:T(8,128)(2,1)S(1)} %collective-permute-done.9.refs_2_), channel_id=1, source_target_pairs={{0,1},{1,0},{2,3},{3,2},{4,5},{5,4},{6,7},{7,6},{8,9},{9,8},{10,11... | collective-permute-start | bytes 393224 | tf_op jit(solution)/shard_map/gather_e/ppermute | solution.py:33
  173.6 4.2 %collective-permute-start.12 = (bf16[32,8,256]{2,1,0:T(8,128)(2,1)S(1)}, bf16[32,8,256]{2,1,0:T(8,128)(2,1)S(1)}, u32[]{:S(2)}, u32[]{:S(2)}) collective-permute-start(bf16[32,8,256]{2,1,0:T(8,128)(2,1)S(1)} %collective-permute-done.11.refs_4_), channel_id=1, source_target_pairs={{0,1},{1,0},{2,3},{3,2},{4,5},{5,4},{6,7},{7,6},{8,9},{9,8},{10,11... | collective-permute-start | bytes 393224 | tf_op jit(solution)/shard_map/gather_e/ppermute | solution.py:33
  175.0 2.8 %collective-permute-start.14 = (bf16[32,8,256]{2,1,0:T(8,128)(2,1)S(1)}, bf16[32,8,256]{2,1,0:T(8,128)(2,1)S(1)}, u32[]{:S(2)}, u32[]{:S(2)}) collective-permute-start(bf16[32,8,256]{2,1,0:T(8,128)(2,1)S(1)} %collective-permute-done.13.refs_6_), channel_id=1, source_target_pairs={{0,1},{1,0},{2,3},{3,2},{4,5},{5,4},{6,7},{7,6},{8,9},{9,8},{10,11... | collective-permute-start | bytes 393224 | tf_op jit(solution)/shard_map/gather_e/ppermute | solution.py:33

commit v4 on v2

--- a/solution.py
+++ b/solution.py
@@ -159,15 +159,14 @@
 
 
 def final_kernel(me, rows_ref, cols_ref, *refs):
-    pieces, (out_ref, env, acc) = refs[: NX * NE], refs[-3:]
-    e, x = me[0], me[1]
+    pieces, (out_ref, env, acc) = refs[:NE], refs[-3:]
+    e = me[0]
     for i, ref in enumerate(pieces):
-        ke, kx = i % NE, i // NE
-        block = (e ^ ke) * 32 + (x ^ kx)
         for half in range(2):
             for z in range(NZ):
                 for y in range(NY):
-                    env[half, y, block + z * NX] = ref[(half * NZ + z) * NY + y]
+                    for x in range(NX):
+                        env[half, y, (e ^ i) * 32 + z * NX + x] = ref[((half * NZ + z) * NY + y) * NX + x]
     for part in range(2):
         at = slice(part * 256, part * 256 + 256)
         one = env[0, part].reshape(512, 256)
@@ -184,7 +183,7 @@
     return pl.pallas_call(
         final_kernel,
         out_shape=jax.ShapeDtypeStruct((2, 512, 512), BF),
-        in_specs=[SMEM] + [VMEM] * (2 + NX * NE),
+        in_specs=[SMEM] + [VMEM] * (2 + NE),
         out_specs=VMEM,
         scratch_shapes=[
             pltpu.VMEM((2, NY, 64, 8, 256), BF),
@@ -232,15 +231,10 @@
     with jax.named_scope("sum"):
         parts = lax.all_to_all(part.reshape(64, 8, 256), ("z", "y", "x"), 0, 0, tiled=True)
         env = jnp.sum(parts.astype(F32), axis=0).astype(BF)
-    with jax.named_scope("gather_row"):
-        env = jnp.broadcast_to(env, (2 * NZ * NY, 8, 256))
-        env = lax.all_to_all(env, ("half",) + ROW, 0, 0, tiled=True)
-    with jax.named_scope("gather_x"):
-        across = [env] + [swap(env, ("x",), k) for k in range(1, NX)]
-    with jax.named_scope("gather_e"):
-        pieces = []
-        for piece in across:
-            pieces += [piece, swap(piece, ("e",), 1)]
+    with jax.named_scope("gather"):
+        env = jnp.broadcast_to(env, (2 * NZ * NY * NX, 8, 256))
+        env = lax.all_to_all(env, ("half",) + ROW + ("x",), 0, 0, tiled=True)
+        pieces = [env, swap(env, ("e",), 1)]
     with jax.named_scope("final"):
         return final(me, by_rows, by_cols, pieces)
 

time: 178 us -> 181 us (1.017)
  waiting for transfers between devices: 76.7 us -> 83.7 us
  starting transfers between devices: 51.2 us -> 46.7 us
    all_to_all x1, waiting for transfers between devices: 9.79 us -> 17.8 us  [on_device(): env = lax.all_to_all(env, ('half',) + ROW + ('x',), 0, 0, tiled=True)]
    ppermute x15 -> x9, starting transfers between devices: 23.9 us -> 16.4 us  [swap(): return lax.ppermute(value, axes, [(i, i ^ offset) for i in range(peers)])]
    all_to_all x1, starting transfers between devices: 6.69 us -> 8.97 us  [on_device(): env = lax.all_to_all(env, ('half',) + ROW + ('x',), 0, 0, tiled=True)]
    ppermute x15 -> x9, waiting for transfers between devices: 20.7 us -> 20.6 us  [swap(): return lax.ppermute(value, axes, [(i, i ^ offset) for i in range(peers)])]
  transfers between devices with their start and end apart: 18 -> 12, of which waited for: 9 -> 8; matrix products, arithmetic and copies ran while one was open for 2% -> 2% of each run, Pallas kernels for 11% -> 11%
where the time goes in v4:
time: 181 us
  waiting for transfers between devices  83.7 us (46%)
  starting transfers between devices  46.7 us (26%)
  Pallas kernels  26.1 us (14%)
  blocking collectives  16.8 us (9%)
  local copies, waits for them, and re-layouts  5.38 us (3%)
    all_to_all x1, waiting for transfers between devices, on_device(): lax.all_to_all(summed.reshape(128, 32, 256), ROW_COL, 0, 0, tiled=True)  44.6 us
    ppermute x9, waiting for transfers between devices, swap(): return lax.ppermute(value, axes, [(i, i ^ offset) for i in range(peers)])  20.6 us
    all_to_all x1, waiting for transfers between devices, on_device(): env = lax.all_to_all(env, ('half',) + ROW + ('x',), 0, 0, tiled=True)  17.8 us
    all_to_all x1, blocking collectives, on_device(): lax.all_to_all(part.reshape(64, 8, 256), ('z', 'y', 'x'), 0, 0, tiled=True)  16.8 us
    ppermute x9, starting transfers between devices, swap(): return lax.ppermute(value, axes, [(i, i ^ offset) for i in range(peers)])  16.4 us
    pallas_call x1, Pallas kernels, apply_terms(): pl.pallas_call(terms_kernel, out_shape=jax.ShapeDtypeStruct((NZ, NY, NX,...  13.8 us
    all_to_all x1, starting transfers between devices, on_device(): lax.all_to_all(summed.reshape(128, 32, 256), ROW_COL, 0, 0, tiled=True)  11 us
    all_to_all x1, starting transfers between devices, on_device(): child_all = lax.all_to_all(cut, ROW, 0, 0, tiled=True)  10.3 us
  transfers between devices with their start and end apart: 12, of which 8 were waited for; matrix products, arithmetic and copies ran while one was open for 2% of the time, Pallas kernels for 11%

profile of v4, /device:TPU:1, one launch (start us, length us, event | category | flops | bytes accessed | tf_op | source)
XLA Modules:
  0.0 180.6 jit_solution(11528972482401892144)
XLA Ops:
  0.0 0.0 copy-start
  0.0 3.2 %copy.11 = bf16[8,2,32,8,256]{4,3,2,1,0:T(8,128)(2,1)} copy(bf16[8,2,32,8,256]{4,3,1,0,2:T(8,128)(2,1)} %bitcast.43) | data formatting | bytes 4194304 | tf_op jit(solution)/shard_map/child_rows/transpose | solution.py:209
  3.2 0.0 copy-start.2
  3.2 10.3 %all-to-all-start.1 = ((bf16[16,256,256]{2,1,0:T(8,128)(2,1)}), bf16[16,256,256]{2,1,0:T(8,128)(2,1)}, u32[]{:S(2)}, u32[]{:S(2)}) async-start(bf16[16,256,256]{2,1,0:T(8,128)(2,1)} %bitcast.45), calls=%async_computation.1 | async-start | bytes 4194304 | tf_op jit(solution)/shard_map/child_rows/all_to_all | solution.py:211
  13.6 0.0 copy-done.2
  13.6 0.0 copy-start.3
  13.6 0.0 copy-start.1
  13.6 1.1 dynamic-slice_bitcast_fusion
  14.7 1.0 collective-permute-start
  15.7 1.2 collective-permute-start.1
  16.9 0.4 collective-permute-start.2
  17.3 2.7 %collective-permute-start.3 = (bf16[4,64,512]{2,1,0:T(8,128)(2,1)}, bf16[4,64,512]{2,1,0:T(8,128)(2,1)S(1)}, u32[]{:S(2)}, u32[]{:S(2)}) collective-permute-start(bf16[4,64,512]{2,1,0:T(8,128)(2,1)} %get-tuple-element.8), channel_id=1, source_target_pairs={{0,4},{1,5},{2,6},{3,7},{4,0},{5,1},{6,2},{7,3},{8,12},{9,13},{10,... | collective-permute-start | bytes 786440 | tf_op jit(solution)/shard_map/child_first_leg/ppermute | solution.py:31
  20.0 0.6 collective-permute-start.4
  20.7 0.0 collective-permute-done.refs_1_
  20.7 2.5 %collective-permute-start.5 = (bf16[4,64,512]{2,1,0:T(8,128)(2,1)}, bf16[4,64,512]{2,1,0:T(8,128)(2,1)S(1)}, u32[]{:S(2)}, u32[]{:S(2)}) collective-permute-start(bf16[4,64,512]{2,1,0:T(8,128)(2,1)} %get-tuple-element.6), channel_id=1, source_target_pairs={{0,6},{1,7},{2,4},{3,5},{4,2},{5,3},{6,0},{7,1},{8,14},{9,15},{10,... | collective-permute-start | bytes 786440 | tf_op jit(solution)/shard_map/child_first_leg/ppermute | solution.py:31
  23.1 0.6 collective-permute-done.1.refs_2_
  23.7 3.4 %collective-permute-start.6 = (bf16[4,64,512]{2,1,0:T(8,128)(2,1)}, bf16[4,64,512]{2,1,0:T(8,128)(2,1)S(1)}, u32[]{:S(2)}, u32[]{:S(2)}) collective-permute-start(bf16[4,64,512]{2,1,0:T(8,128)(2,1)} %get-tuple-element.5), channel_id=1, source_target_pairs={{0,7},{1,6},{2,5},{3,4},{4,3},{5,2},{6,1},{7,0},{8,15},{9,14},{10,... | collective-permute-start | bytes 786440 | tf_op jit(solution)/shard_map/child_first_leg/ppermute | solution.py:31
  27.1 0.0 copy-done.3
  27.1 0.1 copy.10.site
  27.2 0.1 pad_add_fusion.me
  27.3 2.8 %collective-permute-done.2.refs_3_ = bf16[4,64,512]{2,1,0:T(8,128)(2,1)S(1)} collective-permute-done((bf16[4,64,512]{2,1,0:T(8,128)(2,1)}, bf16[4,64,512]{2,1,0:T(8,128)(2,1)S(1)}, u32[]{:S(2)}, u32[]{:S(2)}) %collective-permute-start.2) | collective-permute-done | bytes 262176 | tf_op jit(solution)/shard_map/child_first_leg/ppermute | solution.py:31
  30.1 7.1 %collective-permute-done.3.refs_4_ = bf16[4,64,512]{2,1,0:T(8,128)(2,1)S(1)} collective-permute-done((bf16[4,64,512]{2,1,0:T(8,128)(2,1)}, bf16[4,64,512]{2,1,0:T(8,128)(2,1)S(1)}, u32[]{:S(2)}, u32[]{:S(2)}) %collective-permute-start.3) | collective-permute-done | bytes 262176 | tf_op jit(solution)/shard_map/child_first_leg/ppermute | solution.py:31
  37.2 5.7 %collective-permute-done.4.refs_5_ = bf16[4,64,512]{2,1,0:T(8,128)(2,1)S(1)} collective-permute-done((bf16[4,64,512]{2,1,0:T(8,128)(2,1)}, bf16[4,64,512]{2,1,0:T(8,128)(2,1)S(1)}, u32[]{:S(2)}, u32[]{:S(2)}) %collective-permute-start.4) | collective-permute-done | bytes 262176 | tf_op jit(solution)/shard_map/child_first_leg/ppermute | solution.py:31
  42.9 0.0 collective-permute-done.5.refs_6_
  42.9 4.5 %collective-permute-done.6.refs_7_ = bf16[4,64,512]{2,1,0:T(8,128)(2,1)S(1)} collective-permute-done((bf16[4,64,512]{2,1,0:T(8,128)(2,1)}, bf16[4,64,512]{2,1,0:T(8,128)(2,1)S(1)}, u32[]{:S(2)}, u32[]{:S(2)}) %collective-permute-start.6) | collective-permute-done | bytes 262176 | tf_op jit(solution)/shard_map/child_first_leg/ppermute | solution.py:31
  47.4 0.0 copy-done.1
  47.4 13.8 %terms.1 = bf16[8,2,4,2,2,2,8,256]{7,6,5,4,3,2,1,0:T(8,128)(2,1)} custom-call(s32[2]{0:T(128)S(1)} %pad_add_fusion.me, s32[5,2]{1,0:T(8,128)S(1)} %copy.10.site, s32[5]{0:T(128)S(1)} %bitcast.42, bf16[2,4,512,512]{3,2,1,0:T(8,128)(2,1)} %bitcast.47, bf16[4,64,512]{2,1,0:T(8,128)(2,1)S(1)} %get-tuple-element.12.refs_0_, ...), custom_call_target="tpu_custom_call" | custom-call | tf_op jit(solution)/shard_map/terms/terms/pallas_call | solution.py:97
  61.2 0.6 all-to-all-done.1
  61.9 11.0 %all-to-all-start = ((bf16[128,32,256]{2,1,0:T(8,128)(2,1)}), bf16[128,32,256]{2,1,0:T(8,128)(2,1)S(1)}, u32[]{:S(2)}, u32[]{:S(2)}) async-start(bf16[128,32,256]{2,1,0:T(8,128)(2,1)} %bitcast.46), calls=%async_computation | async-start | bytes 4194304 | tf_op jit(solution)/shard_map/summed_rows/all_to_all | solution.py:224
  72.8 5.8 %turn.1.own_ref = bf16[8,512,256]{2,1,0:T(8,128)(2,1)} custom-call(bf16[512,8,256]{2,1,0:T(8,128)(2,1)} %bitcast.22.in_ref), custom_call_target="tpu_custom_call" | custom-call | tf_op jit(solution)/shard_map/turn/turn/pallas_call | solution.py:121
  78.7 0.9 collective-permute-start.7
  79.5 44.6 %all-to-all-done = bf16[128,32,256]{2,1,0:T(8,128)(2,1)S(1)} async-done(((bf16[128,32,256]{2,1,0:T(8,128)(2,1)}), bf16[128,32,256]{2,1,0:T(8,128)(2,1)S(1)}, u32[]{:S(2)}, u32[]{:S(2)}) %all-to-all-start) | async-done | bytes 2097184 | tf_op jit(solution)/shard_map/summed_rows/all_to_all | solution.py:224
  124.2 0.0 collective-permute-done.7.other_ref
  124.2 3.6 %gram.1 = bf16[8,2,4,8,256]{4,3,2,1,0:T(8,128)(2,1)S(1)} custom-call(s32[2]{0:T(128)S(1)} %pad_add_fusion.me, bf16[128,2,2,8,256]{4,3,2,1,0:T(8,128)(2,1)S(1)} %bitcast.40, bf16[8,512,256]{2,1,0:T(8,128)(2,1)} %turn.1.own_ref, bf16[8,512,256]{2,1,0:T(8,128)(2,1)} %collective-permute-done.7.other_ref), custom_call_target="tpu_custom_call" | custom-call | tf_op jit(solution)/shard_map/gram/gram/pallas_call | solution.py:150
  127.8 16.8 %all_to_all.20 = bf16[64,8,256]{2,1,0:T(8,128)(2,1)S(1)} all-to-all(bf16[64,8,256]{2,1,0:T(8,128)(2,1)S(1)} %bitcast.41), channel_id=1, replica_groups=mesh['half'=2,'z'=8,'y'=2,'x'=4,'e'=2] {'z','y','x'}, dimensions={0} | all-to-all | bytes 524288 | tf_op jit(solution)/shard_map/sum/all_to_all | solution.py:232
  144.6 0.1 reduce_sum.12
  144.6 0.8 broadcast_in_dim.4
  145.5 9.0 %all-to-all-start.3 = ((bf16[128,8,256]{2,1,0:T(8,128)(2,1)}), bf16[128,8,256]{2,1,0:T(8,128)(2,1)S(1)}, u32[]{:S(2)}, u32[]{:S(2)}) async-start(bf16[128,8,256]{2,1,0:T(8,128)(2,1)} %broadcast_in_dim.4), calls=%async_computation.3 | async-start | bytes 1048576 | tf_op jit(solution)/shard_map/gather/all_to_all | solution.py:236
  154.5 0.1 reshape.75
  154.6 17.8 %all-to-all-done.3.refs_0_ = bf16[128,8,256]{2,1,0:T(8,128)(2,1)S(1)} async-done(((bf16[128,8,256]{2,1,0:T(8,128)(2,1)}), bf16[128,8,256]{2,1,0:T(8,128)(2,1)S(1)}, u32[]{:S(2)}, u32[]{:S(2)}) %all-to-all-start.3) | async-done | bytes 524320 | tf_op jit(solution)/shard_map/gather/all_to_all | solution.py:236
  172.4 3.7 %collective-permute-start.8 = (bf16[128,8,256]{2,1,0:T(8,128)(2,1)S(1)}, bf16[128,8,256]{2,1,0:T(8,128)(2,1)S(1)}, u32[]{:S(2)}, u32[]{:S(2)}) collective-permute-start(bf16[128,8,256]{2,1,0:T(8,128)(2,1)S(1)} %all-to-all-done.3.refs_0_), channel_id=1, source_target_pairs={{0,1},{1,0},{2,3},{3,2},{4,5},{5,4},{6,7},{7,6},{8,9},{9,8},{10,11... | collective-permute-start | bytes 1572872 | tf_op jit(solution)/shard_map/gather/ppermute | solution.py:31
  176.1 0.0 copy-done
  176.1 0.7 fusion.rows_ref
  176.9 0.9 fusion.1.cols_ref
  177.7 0.0 collective-permute-done.8.refs_1_
  177.7 2.9 %final.1 = bf16[2,512,512]{2,1,0:T(8,128)(2,1)} custom-call(s32[2]{0:T(128)S(1)} %pad_add_fusion.me, bf16[2,512,512]{2,1,0:T(8,128)(2,1)S(1)} %fusion.rows_ref, bf16[2,512,512]{2,1,0:T(8,128)(2,1)S(1)} %fusion.1.cols_ref, bf16[128,8,256]{2,1,0:T(8,128)(2,1)S(1)} %all-to-all-done.3.refs_0_, bf16[128,8,256]{2,1,0:T(8,128)(2,1)S(1)} %collective-permute-done.8.refs_1_), custom_call_target="tpu_custom_call" | custom-call | tf_op jit(solution)/shard_map/final/final/pallas_call | solution.py:183
  (1 shorter events, 0.0 us)
Async XLA Ops:
  0.0 176.1 %copy-start = (bf16[2,512,512]{2,1,0:T(8,128)(2,1)S(1)}, bf16[2,512,512]{2,1,0:T(8,128)(2,1)}, u32[]{:S(2)}) copy-start(bf16[2,512,512]{2,1,0:T(8,128)(2,1)} %param.9) | copy-start | bytes 3145732
  3.2 10.4 %copy-start.2 = (bf16[1,32,64,512]{3,2,1,0:T(8,128)(2,1)S(1)}, bf16[1,32,64,512]{3,2,1,0:T(8,128)(2,1)}, u32[]{:S(2)}) copy-start(bf16[1,32,64,512]{3,2,1,0:T(8,128)(2,1)} %param.5) | copy-start | bytes 6291460
  3.2 58.6 %all-to-all-start.1 = ((bf16[16,256,256]{2,1,0:T(8,128)(2,1)}), bf16[16,256,256]{2,1,0:T(8,128)(2,1)}, u32[]{:S(2)}, u32[]{:S(2)}) async-start(bf16[16,256,256]{2,1,0:T(8,128)(2,1)} %bitcast.45), calls=%async_computation.1 | async-start | bytes 4194304 | tf_op jit(solution)/shard_map/child_rows/all_to_all | solution.py:211
  13.6 13.5 %copy-start.3 = (s32[1,5,2]{1,2,0:T(2,128)S(1)}, s32[1,5,2]{1,2,0:T(2,128)}, u32[]{:S(2)}) copy-start(s32[1,5,2]{1,2,0:T(2,128)} %param.7) | copy-start | bytes 124
  13.6 33.8 %copy-start.1 = (s32[1,5]{1,0:T(1,128)S(1)}, s32[1,5]{1,0:T(1,128)}, u32[]{:S(2)}) copy-start(s32[1,5]{1,0:T(1,128)} %param.8) | copy-start | bytes 64
  14.7 6.0 %collective-permute-start = (bf16[4,64,512]{2,1,0:T(8,128)(2,1)S(1)}, bf16[4,64,512]{2,1,0:T(8,128)(2,1)S(1)}, u32[]{:S(2)}, u32[]{:S(2)}) collective-permute-start(bf16[4,64,512]{2,1,0:T(8,128)(2,1)S(1)} %get-tuple-element.11), channel_id=1, source_target_pairs={{0,1},{1,0},{2,3},{3,2},{4,5},{5,4},{6,7},{7,6},{8,9},{9,8},{10,11... | collective-permute-start | bytes 786440 | tf_op jit(solution)/shard_map/child_first_leg/ppermute | solution.py:31
  15.7 8.0 %collective-permute-start.1 = (bf16[4,64,512]{2,1,0:T(8,128)(2,1)S(1)}, bf16[4,64,512]{2,1,0:T(8,128)(2,1)S(1)}, u32[]{:S(2)}, u32[]{:S(2)}) collective-permute-start(bf16[4,64,512]{2,1,0:T(8,128)(2,1)S(1)} %get-tuple-element.10), channel_id=1, source_target_pairs={{0,2},{1,3},{2,0},{3,1},{4,6},{5,7},{6,4},{7,5},{8,10},{9,11},{10,... | collective-permute-start | bytes 786440 | tf_op jit(solution)/shard_map/child_first_leg/ppermute | solution.py:31
  16.9 13.2 %collective-permute-start.2 = (bf16[4,64,512]{2,1,0:T(8,128)(2,1)}, bf16[4,64,512]{2,1,0:T(8,128)(2,1)S(1)}, u32[]{:S(2)}, u32[]{:S(2)}) collective-permute-start(bf16[4,64,512]{2,1,0:T(8,128)(2,1)} %get-tuple-element.9), channel_id=1, source_target_pairs={{0,3},{1,2},{2,1},{3,0},{4,7},{5,6},{6,5},{7,4},{8,11},{9,10},{10,... | collective-permute-start | bytes 786440 | tf_op jit(solution)/shard_map/child_first_leg/ppermute | solution.py:31
  17.3 19.9 %collective-permute-start.3 = (bf16[4,64,512]{2,1,0:T(8,128)(2,1)}, bf16[4,64,512]{2,1,0:T(8,128)(2,1)S(1)}, u32[]{:S(2)}, u32[]{:S(2)}) collective-permute-start(bf16[4,64,512]{2,1,0:T(8,128)(2,1)} %get-tuple-element.8), channel_id=1, source_target_pairs={{0,4},{1,5},{2,6},{3,7},{4,0},{5,1},{6,2},{7,3},{8,12},{9,13},{10,... | collective-permute-start | bytes 786440 | tf_op jit(solution)/shard_map/child_first_leg/ppermute | solution.py:31
  20.0 22.8 %collective-permute-start.4 = (bf16[4,64,512]{2,1,0:T(8,128)(2,1)}, bf16[4,64,512]{2,1,0:T(8,128)(2,1)S(1)}, u32[]{:S(2)}, u32[]{:S(2)}) collective-permute-start(bf16[4,64,512]{2,1,0:T(8,128)(2,1)} %get-tuple-element.7), channel_id=1, source_target_pairs={{0,5},{1,4},{2,7},{3,6},{4,1},{5,0},{6,3},{7,2},{8,13},{9,12},{10,... | collective-permute-start | bytes 786440 | tf_op jit(solution)/shard_map/child_first_leg/ppermute | solution.py:31
  20.7 22.2 %collective-permute-start.5 = (bf16[4,64,512]{2,1,0:T(8,128)(2,1)}, bf16[4,64,512]{2,1,0:T(8,128)(2,1)S(1)}, u32[]{:S(2)}, u32[]{:S(2)}) collective-permute-start(bf16[4,64,512]{2,1,0:T(8,128)(2,1)} %get-tuple-element.6), channel_id=1, source_target_pairs={{0,6},{1,7},{2,4},{3,5},{4,2},{5,3},{6,0},{7,1},{8,14},{9,15},{10,... | collective-permute-start | bytes 786440 | tf_op jit(solution)/shard_map/child_first_leg/ppermute | solution.py:31
  23.7 23.7 %collective-permute-start.6 = (bf16[4,64,512]{2,1,0:T(8,128)(2,1)}, bf16[4,64,512]{2,1,0:T(8,128)(2,1)S(1)}, u32[]{:S(2)}, u32[]{:S(2)}) collective-permute-start(bf16[4,64,512]{2,1,0:T(8,128)(2,1)} %get-tuple-element.5), channel_id=1, source_target_pairs={{0,7},{1,6},{2,5},{3,4},{4,3},{5,2},{6,1},{7,0},{8,15},{9,14},{10,... | collective-permute-start | bytes 786440 | tf_op jit(solution)/shard_map/child_first_leg/ppermute | solution.py:31
  61.9 62.3 %all-to-all-start = ((bf16[128,32,256]{2,1,0:T(8,128)(2,1)}), bf16[128,32,256]{2,1,0:T(8,128)(2,1)S(1)}, u32[]{:S(2)}, u32[]{:S(2)}) async-start(bf16[128,32,256]{2,1,0:T(8,128)(2,1)} %bitcast.46), calls=%async_computation | async-start | bytes 4194304 | tf_op jit(solution)/shard_map/summed_rows/all_to_all | solution.py:224
  78.7 45.5 %collective-permute-start.7 = (bf16[8,512,256]{2,1,0:T(8,128)(2,1)}, bf16[8,512,256]{2,1,0:T(8,128)(2,1)}, u32[]{:S(2)}, u32[]{:S(2)}) collective-permute-start(bf16[8,512,256]{2,1,0:T(8,128)(2,1)} %turn.1.own_ref), channel_id=1, source_target_pairs={{0,1},{1,0},{2,3},{3,2},{4,5},{5,4},{6,7},{7,6},{8,9},{9,8},{10,11... | collective-permute-start | bytes 6291464 | tf_op jit(solution)/shard_map/turn/ppermute | solution.py:31
  145.5 26.9 %all-to-all-start.3 = ((bf16[128,8,256]{2,1,0:T(8,128)(2,1)}), bf16[128,8,256]{2,1,0:T(8,128)(2,1)S(1)}, u32[]{:S(2)}, u32[]{:S(2)}) async-start(bf16[128,8,256]{2,1,0:T(8,128)(2,1)} %broadcast_in_dim.4), calls=%async_computation.3 | async-start | bytes 1048576 | tf_op jit(solution)/shard_map/gather/all_to_all | solution.py:236
  172.4 5.3 %collective-permute-start.8 = (bf16[128,8,256]{2,1,0:T(8,128)(2,1)S(1)}, bf16[128,8,256]{2,1,0:T(8,128)(2,1)S(1)}, u32[]{:S(2)}, u32[]{:S(2)}) collective-permute-start(bf16[128,8,256]{2,1,0:T(8,128)(2,1)S(1)} %all-to-all-done.3.refs_0_), channel_id=1, source_target_pairs={{0,1},{1,0},{2,3},{3,2},{4,5},{5,4},{6,7},{7,6},{8,9},{9,8},{10,11... | collective-permute-start | bytes 1572872 | tf_op jit(solution)/shard_map/gather/ppermute | solution.py:31

commit v5 on v2

--- a/solution.py
+++ b/solution.py
@@ -29,6 +29,41 @@
 def swap(value, axes, offset):
     peers = lax.axis_size(axes)
     return lax.ppermute(value, axes, [(i, i ^ offset) for i in range(peers)])
+
+
+def cut_kernel(child, out, held, arrived, left):
+    pieces = [(z, y) for z in range(NZ) for y in range(NY)]
+    takes = [
+        pltpu.make_async_copy(
+            child.at[:, z * 8 : z * 8 + 8, y * 256 : y * 256 + 256], held.at[i], arrived.at[i]
+        )
+        for i, (z, y) in enumerate(pieces)
+    ]
+    gives = [pltpu.make_async_copy(held.at[i], out.at[i], left.at[i]) for i in range(len(pieces))]
+    for take in takes:
+        take.start()
+    for take, give in zip(takes, gives):
+        take.wait()
+        give.start()
+    for give in gives:
+        give.wait()
+
+
+def cut_for_row(child):
+    peers = NZ * NY
+    return pl.pallas_call(
+        cut_kernel,
+        out_shape=jax.ShapeDtypeStruct((peers, 32, 8, 256), BF),
+        in_specs=[HBM],
+        out_specs=HBM,
+        scratch_shapes=[
+            pltpu.VMEM((peers, 32, 8, 256), BF),
+            pltpu.SemaphoreType.DMA((peers,)),
+            pltpu.SemaphoreType.DMA((peers,)),
+        ],
+        compiler_params=vmem(60),
+        name="cut",
+    )(child)
 
 
 def terms_kernel(me, site, leg, table, *refs):
@@ -207,8 +242,7 @@
     me = jnp.stack([lax.axis_index(a) for a in ("e", "x")]).astype(jnp.int32)
     child = children[0]
     with jax.named_scope("child_rows"):
-        cut = child.reshape(32, NZ, 8, NY, 256).transpose(1, 3, 0, 2, 4)
-        cut = cut.reshape(NZ * NY, 32 * 8, 256)
+        cut = cut_for_row(child).reshape(NZ * NY, 32 * 8, 256)
         child_all = lax.all_to_all(cut, ROW, 0, 0, tiled=True)
     with jax.named_scope("child_first_leg"):
         col = lax.axis_index(COL)
@@ -236,7 +270,8 @@
         env = jnp.broadcast_to(env, (2 * NZ * NY, 8, 256))
         env = lax.all_to_all(env, ("half",) + ROW, 0, 0, tiled=True)
     with jax.named_scope("gather_x"):
-        across = [env] + [swap(env, ("x",), k) for k in range(1, NX)]
+        far = swap(env, ("x",), 2)
+        across = [env, swap(env, ("x",), 1), far, swap(env, ("x",), 3)]
     with jax.named_scope("gather_e"):
         pieces = []
         for piece in across:

time: 178 us -> 177 us (level)
  local copies, waits for them, and re-layouts: 5.18 us -> 2 us
  waiting for transfers between devices: 76.7 us -> 79.2 us
    transpose x1 -> x0, local copies, waits for them, and re-layouts: 3.19 us -> none  [on_device(): cut = child.reshape(32, NZ, 8, NY, 256).transpose(1, 3, 0, 2, 4)]
    pallas_call x0 -> x1, Pallas kernels: none -> 2.68 us  [cut_for_row(): pl.pallas_call(cut_kernel, out_shape=jax.ShapeDtypeStruct((peers, 32, 8,...]
    all_to_all x1, waiting for transfers between devices: 1.56 us -> 4.04 us  [on_device(): child_all = lax.all_to_all(cut, ROW, 0, 0, tiled=True)]
    pallas_call x1, Pallas kernels: 12.9 us -> 10.4 us  [apply_terms(): pl.pallas_call(terms_kernel, out_shape=jax.ShapeDtypeStruct((NZ, NY, NX,...]
  transfers between devices with their start and end apart: 18 -> 18, of which waited for: 9 -> 9; matrix products, arithmetic and copies ran while one was open for 2% -> 2% of each run, Pallas kernels for 11% -> 9%
where the time goes in v5:
time: 177 us
  waiting for transfers between devices  79.2 us (45%)
  starting transfers between devices  51.3 us (29%)
  Pallas kernels  25.5 us (14%)
  blocking collectives  16.8 us (9%)
  local copies, waits for them, and re-layouts  2 us (1%)
    all_to_all x1, waiting for transfers between devices, on_device(): lax.all_to_all(summed.reshape(128, 32, 256), ROW_COL, 0, 0, tiled=True)  44.6 us
    ppermute x15, starting transfers between devices, swap(): return lax.ppermute(value, axes, [(i, i ^ offset) for i in range(peers)])  23.8 us
    ppermute x15, waiting for transfers between devices, swap(): return lax.ppermute(value, axes, [(i, i ^ offset) for i in range(peers)])  20.7 us
    all_to_all x1, blocking collectives, on_device(): lax.all_to_all(part.reshape(64, 8, 256), ('z', 'y', 'x'), 0, 0, tiled=True)  16.8 us
    pallas_call x1, Pallas kernels, apply_terms(): pl.pallas_call(terms_kernel, out_shape=jax.ShapeDtypeStruct((NZ, NY, NX,...  10.4 us
    all_to_all x1, starting transfers between devices, on_device(): lax.all_to_all(summed.reshape(128, 32, 256), ROW_COL, 0, 0, tiled=True)  10.4 us
    all_to_all x1, starting transfers between devices, on_device(): child_all = lax.all_to_all(cut, ROW, 0, 0, tiled=True)  10.3 us
    all_to_all x1, waiting for transfers between devices, on_device(): env = lax.all_to_all(env, ('half',) + ROW, 0, 0, tiled=True)  9.79 us
  transfers between devices with their start and end apart: 18, of which 9 were waited for; matrix products, arithmetic and copies ran while one was open for 2% of the time, Pallas kernels for 9%

profile of v5, /device:TPU:1, one launch (start us, length us, event | category | flops | bytes accessed | tf_op | source)
XLA Modules:
  0.0 176.7 jit_solution(2363576039454407021)
XLA Ops:
  0.0 2.7 %cut.1 = bf16[16,32,8,256]{3,2,1,0:T(8,128)(2,1)} custom-call(bf16[32,64,512]{2,1,0:T(8,128)(2,1)} %bitcast.41), custom_call_target="tpu_custom_call" | custom-call | tf_op jit(solution)/shard_map/child_rows/cut/pallas_call | solution.py:54
  2.7 0.0 copy-start.2
  2.7 10.3 %all-to-all-start.1 = ((bf16[16,256,256]{2,1,0:T(8,128)(2,1)}), bf16[16,256,256]{2,1,0:T(8,128)(2,1)}, u32[]{:S(2)}, u32[]{:S(2)}) async-start(bf16[16,256,256]{2,1,0:T(8,128)(2,1)} %bitcast.43), calls=%async_computation.1 | async-start | bytes 4194304 | tf_op jit(solution)/shard_map/child_rows/all_to_all | solution.py:246
  13.1 0.0 copy-start.3
  13.1 0.0 copy-start.1
  13.1 1.1 dynamic-slice_bitcast_fusion
  14.2 1.0 collective-permute-start
  15.2 1.2 collective-permute-start.1
  16.4 0.4 collective-permute-start.2
  16.8 2.7 %collective-permute-start.3 = (bf16[4,64,512]{2,1,0:T(8,128)(2,1)}, bf16[4,64,512]{2,1,0:T(8,128)(2,1)S(1)}, u32[]{:S(2)}, u32[]{:S(2)}) collective-permute-start(bf16[4,64,512]{2,1,0:T(8,128)(2,1)} %get-tuple-element.8), channel_id=1, source_target_pairs={{0,4},{1,5},{2,6},{3,7},{4,0},{5,1},{6,2},{7,3},{8,12},{9,13},{10,... | collective-permute-start | bytes 786440 | tf_op jit(solution)/shard_map/child_first_leg/ppermute | solution.py:31
  19.5 0.6 collective-permute-start.4
  20.2 2.5 %collective-permute-start.5 = (bf16[4,64,512]{2,1,0:T(8,128)(2,1)}, bf16[4,64,512]{2,1,0:T(8,128)(2,1)S(1)}, u32[]{:S(2)}, u32[]{:S(2)}) collective-permute-start(bf16[4,64,512]{2,1,0:T(8,128)(2,1)} %get-tuple-element.6), channel_id=1, source_target_pairs={{0,6},{1,7},{2,4},{3,5},{4,2},{5,3},{6,0},{7,1},{8,14},{9,15},{10,... | collective-permute-start | bytes 786440 | tf_op jit(solution)/shard_map/child_first_leg/ppermute | solution.py:31
  22.6 0.6 collective-permute-done.1.refs_2_
  23.2 3.4 %collective-permute-start.6 = (bf16[4,64,512]{2,1,0:T(8,128)(2,1)}, bf16[4,64,512]{2,1,0:T(8,128)(2,1)S(1)}, u32[]{:S(2)}, u32[]{:S(2)}) collective-permute-start(bf16[4,64,512]{2,1,0:T(8,128)(2,1)} %get-tuple-element.5), channel_id=1, source_target_pairs={{0,7},{1,6},{2,5},{3,4},{4,3},{5,2},{6,1},{7,0},{8,15},{9,14},{10,... | collective-permute-start | bytes 786440 | tf_op jit(solution)/shard_map/child_first_leg/ppermute | solution.py:31
  26.6 0.1 copy.9.site
  26.7 0.1 pad_add_fusion.me
  26.8 2.8 %collective-permute-done.2.refs_3_ = bf16[4,64,512]{2,1,0:T(8,128)(2,1)S(1)} collective-permute-done((bf16[4,64,512]{2,1,0:T(8,128)(2,1)}, bf16[4,64,512]{2,1,0:T(8,128)(2,1)S(1)}, u32[]{:S(2)}, u32[]{:S(2)}) %collective-permute-start.2) | collective-permute-done | bytes 262176 | tf_op jit(solution)/shard_map/child_first_leg/ppermute | solution.py:31
  29.6 7.1 %collective-permute-done.3.refs_4_ = bf16[4,64,512]{2,1,0:T(8,128)(2,1)S(1)} collective-permute-done((bf16[4,64,512]{2,1,0:T(8,128)(2,1)}, bf16[4,64,512]{2,1,0:T(8,128)(2,1)S(1)}, u32[]{:S(2)}, u32[]{:S(2)}) %collective-permute-start.3) | collective-permute-done | bytes 262176 | tf_op jit(solution)/shard_map/child_first_leg/ppermute | solution.py:31
  36.7 5.7 %collective-permute-done.4.refs_5_ = bf16[4,64,512]{2,1,0:T(8,128)(2,1)S(1)} collective-permute-done((bf16[4,64,512]{2,1,0:T(8,128)(2,1)}, bf16[4,64,512]{2,1,0:T(8,128)(2,1)S(1)}, u32[]{:S(2)}, u32[]{:S(2)}) %collective-permute-start.4) | collective-permute-done | bytes 262176 | tf_op jit(solution)/shard_map/child_first_leg/ppermute | solution.py:31
  42.3 4.5 %collective-permute-done.6.refs_7_ = bf16[4,64,512]{2,1,0:T(8,128)(2,1)S(1)} collective-permute-done((bf16[4,64,512]{2,1,0:T(8,128)(2,1)}, bf16[4,64,512]{2,1,0:T(8,128)(2,1)S(1)}, u32[]{:S(2)}, u32[]{:S(2)}) %collective-permute-start.6) | collective-permute-done | bytes 262176 | tf_op jit(solution)/shard_map/child_first_leg/ppermute | solution.py:31
  46.9 10.4 %terms.1 = bf16[8,2,4,2,2,2,8,256]{7,6,5,4,3,2,1,0:T(8,128)(2,1)} custom-call(s32[2]{0:T(128)S(1)} %pad_add_fusion.me, s32[5,2]{1,0:T(8,128)S(1)} %copy.9.site, s32[5]{0:T(128)S(1)} %bitcast.40, bf16[2,4,512,512]{3,2,1,0:T(8,128)(2,1)} %bitcast.45, bf16[4,64,512]{2,1,0:T(8,128)(2,1)S(1)} %get-tuple-element.12.refs_0_, ...), custom_call_target="tpu_custom_call" | custom-call | tf_op jit(solution)/shard_map/terms/terms/pallas_call | solution.py:132
  57.3 4.0 %all-to-all-done.1 = bf16[16,256,256]{2,1,0:T(8,128)(2,1)} async-done(((bf16[16,256,256]{2,1,0:T(8,128)(2,1)}), bf16[16,256,256]{2,1,0:T(8,128)(2,1)}, u32[]{:S(2)}, u32[]{:S(2)}) %all-to-all-start.1) | async-done | bytes 2097184 | tf_op jit(solution)/shard_map/child_rows/all_to_all | solution.py:246
  61.4 10.4 %all-to-all-start = ((bf16[128,32,256]{2,1,0:T(8,128)(2,1)}), bf16[128,32,256]{2,1,0:T(8,128)(2,1)S(1)}, u32[]{:S(2)}, u32[]{:S(2)}) async-start(bf16[128,32,256]{2,1,0:T(8,128)(2,1)} %bitcast.44), calls=%async_computation | async-start | bytes 4194304 | tf_op jit(solution)/shard_map/summed_rows/all_to_all | solution.py:259
  71.7 5.8 %turn.1.own_ref = bf16[8,512,256]{2,1,0:T(8,128)(2,1)} custom-call(bf16[512,8,256]{2,1,0:T(8,128)(2,1)} %bitcast.21.in_ref), custom_call_target="tpu_custom_call" | custom-call | tf_op jit(solution)/shard_map/turn/turn/pallas_call | solution.py:156
  77.6 0.9 collective-permute-start.7
  78.5 44.6 %all-to-all-done = bf16[128,32,256]{2,1,0:T(8,128)(2,1)S(1)} async-done(((bf16[128,32,256]{2,1,0:T(8,128)(2,1)}), bf16[128,32,256]{2,1,0:T(8,128)(2,1)S(1)}, u32[]{:S(2)}, u32[]{:S(2)}) %all-to-all-start) | async-done | bytes 2097184 | tf_op jit(solution)/shard_map/summed_rows/all_to_all | solution.py:259
  123.1 0.0 collective-permute-done.7.other_ref
  123.1 3.6 %gram.1 = bf16[8,2,4,8,256]{4,3,2,1,0:T(8,128)(2,1)S(1)} custom-call(s32[2]{0:T(128)S(1)} %pad_add_fusion.me, bf16[128,2,2,8,256]{4,3,2,1,0:T(8,128)(2,1)S(1)} %bitcast.38, bf16[8,512,256]{2,1,0:T(8,128)(2,1)} %turn.1.own_ref, bf16[8,512,256]{2,1,0:T(8,128)(2,1)} %collective-permute-done.7.other_ref), custom_call_target="tpu_custom_call" | custom-call | tf_op jit(solution)/shard_map/gram/gram/pallas_call | solution.py:185
  126.7 16.8 %all_to_all.20 = bf16[64,8,256]{2,1,0:T(8,128)(2,1)S(1)} all-to-all(bf16[64,8,256]{2,1,0:T(8,128)(2,1)S(1)} %bitcast.39), channel_id=1, replica_groups=mesh['half'=2,'z'=8,'y'=2,'x'=4,'e'=2] {'z','y','x'}, dimensions={0} | all-to-all | bytes 524288 | tf_op jit(solution)/shard_map/sum/all_to_all | solution.py:267
  143.5 0.1 reduce_sum.12
  143.6 0.7 broadcast_in_dim.4
  144.2 6.7 %all-to-all-start.3 = ((bf16[32,8,256]{2,1,0:T(8,128)(2,1)}), bf16[32,8,256]{2,1,0:T(8,128)(2,1)S(1)}, u32[]{:S(2)}, u32[]{:S(2)}) async-start(bf16[32,8,256]{2,1,0:T(8,128)(2,1)} %broadcast_in_dim.4), calls=%async_computation.3 | async-start | bytes 262144 | tf_op jit(solution)/shard_map/gather_row/all_to_all | solution.py:271
  151.0 0.1 reshape.75
  151.1 9.8 %all-to-all-done.3.refs_0_ = bf16[32,8,256]{2,1,0:T(8,128)(2,1)S(1)} async-done(((bf16[32,8,256]{2,1,0:T(8,128)(2,1)}), bf16[32,8,256]{2,1,0:T(8,128)(2,1)S(1)}, u32[]{:S(2)}, u32[]{:S(2)}) %all-to-all-start.3) | async-done | bytes 131104 | tf_op jit(solution)/shard_map/gather_row/all_to_all | solution.py:271
  160.9 0.4 collective-permute-start.9
  161.2 1.3 collective-permute-start.11
  162.5 2.2 %collective-permute-start.13 = (bf16[32,8,256]{2,1,0:T(8,128)(2,1)S(1)}, bf16[32,8,256]{2,1,0:T(8,128)(2,1)S(1)}, u32[]{:S(2)}, u32[]{:S(2)}) collective-permute-start(bf16[32,8,256]{2,1,0:T(8,128)(2,1)S(1)} %all-to-all-done.3.refs_0_), channel_id=1, source_target_pairs={{0,6},{2,4},{4,2},{6,0},{1,7},{3,5},{5,3},{7,1},{8,14},{10,12},{12... | collective-permute-start | bytes 393224 | tf_op jit(solution)/shard_map/gather_x/ppermute | solution.py:31
  164.8 0.7 fusion.rows_ref
  165.5 3.9 %collective-permute-start.8 = (bf16[32,8,256]{2,1,0:T(8,128)(2,1)S(1)}, bf16[32,8,256]{2,1,0:T(8,128)(2,1)S(1)}, u32[]{:S(2)}, u32[]{:S(2)}) collective-permute-start(bf16[32,8,256]{2,1,0:T(8,128)(2,1)S(1)} %all-to-all-done.3.refs_0_), channel_id=1, source_target_pairs={{0,1},{1,0},{2,3},{3,2},{4,5},{5,4},{6,7},{7,6},{8,9},{9,8},{10,11... | collective-permute-start | bytes 393224 | tf_op jit(solution)/shard_map/gather_e/ppermute | solution.py:31
  169.4 0.0 collective-permute-done.9.refs_2_
  169.4 0.1 collective-permute-start.10
  169.5 1.5 collective-permute-start.12
  170.9 0.0 collective-permute-done.13.refs_6_
  170.9 1.8 %collective-permute-start.14 = (bf16[32,8,256]{2,1,0:T(8,128)(2,1)S(1)}, bf16[32,8,256]{2,1,0:T(8,128)(2,1)S(1)}, u32[]{:S(2)}, u32[]{:S(2)}) collective-permute-start(bf16[32,8,256]{2,1,0:T(8,128)(2,1)S(1)} %collective-permute-done.13.refs_6_), channel_id=1, source_target_pairs={{0,1},{1,0},{2,3},{3,2},{4,5},{5,4},{6,7},{7,6},{8,9},{9,8},{10,11... | collective-permute-start | bytes 393224 | tf_op jit(solution)/shard_map/gather_e/ppermute | solution.py:31
  172.8 0.9 fusion.1.cols_ref
  173.6 0.0 collective-permute-done.8.refs_1_
  173.7 0.1 collective-permute-done.14.refs_7_
  173.7 2.9 %final.1 = bf16[2,512,512]{2,1,0:T(8,128)(2,1)} custom-call(s32[2]{0:T(128)S(1)} %pad_add_fusion.me, bf16[2,512,512]{2,1,0:T(8,128)(2,1)S(1)} %fusion.rows_ref, bf16[2,512,512]{2,1,0:T(8,128)(2,1)S(1)} %fusion.1.cols_ref, bf16[32,8,256]{2,1,0:T(8,128)(2,1)S(1)} %all-to-all-done.3.refs_0_, bf16[32,8,256]{2,1,0:T(8,128)(2,1)S(1)} %collective-permute-done.8.refs_1_, ...), custom_call_target="tpu_custom_call" | custom-call | tf_op jit(solution)/shard_map/final/final/pallas_call | solution.py:219
  (11 shorter events, 0.0 us)
Async XLA Ops:
  0.0 164.8 %copy-start = (bf16[2,512,512]{2,1,0:T(8,128)(2,1)S(1)}, bf16[2,512,512]{2,1,0:T(8,128)(2,1)}, u32[]{:S(2)}) copy-start(bf16[2,512,512]{2,1,0:T(8,128)(2,1)} %param.9) | copy-start | bytes 3145732
  2.7 10.4 %copy-start.2 = (bf16[1,32,64,512]{3,2,1,0:T(8,128)(2,1)S(1)}, bf16[1,32,64,512]{3,2,1,0:T(8,128)(2,1)}, u32[]{:S(2)}) copy-start(bf16[1,32,64,512]{3,2,1,0:T(8,128)(2,1)} %param.5) | copy-start | bytes 6291460
  2.7 58.7 %all-to-all-start.1 = ((bf16[16,256,256]{2,1,0:T(8,128)(2,1)}), bf16[16,256,256]{2,1,0:T(8,128)(2,1)}, u32[]{:S(2)}, u32[]{:S(2)}) async-start(bf16[16,256,256]{2,1,0:T(8,128)(2,1)} %bitcast.43), calls=%async_computation.1 | async-start | bytes 4194304 | tf_op jit(solution)/shard_map/child_rows/all_to_all | solution.py:246
  13.1 13.5 %copy-start.3 = (s32[1,5,2]{1,2,0:T(2,128)S(1)}, s32[1,5,2]{1,2,0:T(2,128)}, u32[]{:S(2)}) copy-start(s32[1,5,2]{1,2,0:T(2,128)} %param.7) | copy-start | bytes 124
  13.1 33.8 %copy-start.1 = (s32[1,5]{1,0:T(1,128)S(1)}, s32[1,5]{1,0:T(1,128)}, u32[]{:S(2)}) copy-start(s32[1,5]{1,0:T(1,128)} %param.8) | copy-start | bytes 64
  14.2 6.0 %collective-permute-start = (bf16[4,64,512]{2,1,0:T(8,128)(2,1)S(1)}, bf16[4,64,512]{2,1,0:T(8,128)(2,1)S(1)}, u32[]{:S(2)}, u32[]{:S(2)}) collective-permute-start(bf16[4,64,512]{2,1,0:T(8,128)(2,1)S(1)} %get-tuple-element.11), channel_id=1, source_target_pairs={{0,1},{1,0},{2,3},{3,2},{4,5},{5,4},{6,7},{7,6},{8,9},{9,8},{10,11... | collective-permute-start | bytes 786440 | tf_op jit(solution)/shard_map/child_first_leg/ppermute | solution.py:31
  15.2 8.0 %collective-permute-start.1 = (bf16[4,64,512]{2,1,0:T(8,128)(2,1)S(1)}, bf16[4,64,512]{2,1,0:T(8,128)(2,1)S(1)}, u32[]{:S(2)}, u32[]{:S(2)}) collective-permute-start(bf16[4,64,512]{2,1,0:T(8,128)(2,1)S(1)} %get-tuple-element.10), channel_id=1, source_target_pairs={{0,2},{1,3},{2,0},{3,1},{4,6},{5,7},{6,4},{7,5},{8,10},{9,11},{10,... | collective-permute-start | bytes 786440 | tf_op jit(solution)/shard_map/child_first_leg/ppermute | solution.py:31
  16.4 13.2 %collective-permute-start.2 = (bf16[4,64,512]{2,1,0:T(8,128)(2,1)}, bf16[4,64,512]{2,1,0:T(8,128)(2,1)S(1)}, u32[]{:S(2)}, u32[]{:S(2)}) collective-permute-start(bf16[4,64,512]{2,1,0:T(8,128)(2,1)} %get-tuple-element.9), channel_id=1, source_target_pairs={{0,3},{1,2},{2,1},{3,0},{4,7},{5,6},{6,5},{7,4},{8,11},{9,10},{10,... | collective-permute-start | bytes 786440 | tf_op jit(solution)/shard_map/child_first_leg/ppermute | solution.py:31
  16.8 19.9 %collective-permute-start.3 = (bf16[4,64,512]{2,1,0:T(8,128)(2,1)}, bf16[4,64,512]{2,1,0:T(8,128)(2,1)S(1)}, u32[]{:S(2)}, u32[]{:S(2)}) collective-permute-start(bf16[4,64,512]{2,1,0:T(8,128)(2,1)} %get-tuple-element.8), channel_id=1, source_target_pairs={{0,4},{1,5},{2,6},{3,7},{4,0},{5,1},{6,2},{7,3},{8,12},{9,13},{10,... | collective-permute-start | bytes 786440 | tf_op jit(solution)/shard_map/child_first_leg/ppermute | solution.py:31
  19.5 22.8 %collective-permute-start.4 = (bf16[4,64,512]{2,1,0:T(8,128)(2,1)}, bf16[4,64,512]{2,1,0:T(8,128)(2,1)S(1)}, u32[]{:S(2)}, u32[]{:S(2)}) collective-permute-start(bf16[4,64,512]{2,1,0:T(8,128)(2,1)} %get-tuple-element.7), channel_id=1, source_target_pairs={{0,5},{1,4},{2,7},{3,6},{4,1},{5,0},{6,3},{7,2},{8,13},{9,12},{10,... | collective-permute-start | bytes 786440 | tf_op jit(solution)/shard_map/child_first_leg/ppermute | solution.py:31
  20.2 22.2 %collective-permute-start.5 = (bf16[4,64,512]{2,1,0:T(8,128)(2,1)}, bf16[4,64,512]{2,1,0:T(8,128)(2,1)S(1)}, u32[]{:S(2)}, u32[]{:S(2)}) collective-permute-start(bf16[4,64,512]{2,1,0:T(8,128)(2,1)} %get-tuple-element.6), channel_id=1, source_target_pairs={{0,6},{1,7},{2,4},{3,5},{4,2},{5,3},{6,0},{7,1},{8,14},{9,15},{10,... | collective-permute-start | bytes 786440 | tf_op jit(solution)/shard_map/child_first_leg/ppermute | solution.py:31
  23.2 23.7 %collective-permute-start.6 = (bf16[4,64,512]{2,1,0:T(8,128)(2,1)}, bf16[4,64,512]{2,1,0:T(8,128)(2,1)S(1)}, u32[]{:S(2)}, u32[]{:S(2)}) collective-permute-start(bf16[4,64,512]{2,1,0:T(8,128)(2,1)} %get-tuple-element.5), channel_id=1, source_target_pairs={{0,7},{1,6},{2,5},{3,4},{4,3},{5,2},{6,1},{7,0},{8,15},{9,14},{10,... | collective-permute-start | bytes 786440 | tf_op jit(solution)/shard_map/child_first_leg/ppermute | solution.py:31
  61.4 61.7 %all-to-all-start = ((bf16[128,32,256]{2,1,0:T(8,128)(2,1)}), bf16[128,32,256]{2,1,0:T(8,128)(2,1)S(1)}, u32[]{:S(2)}, u32[]{:S(2)}) async-start(bf16[128,32,256]{2,1,0:T(8,128)(2,1)} %bitcast.44), calls=%async_computation | async-start | bytes 4194304 | tf_op jit(solution)/shard_map/summed_rows/all_to_all | solution.py:259
  77.6 45.5 %collective-permute-start.7 = (bf16[8,512,256]{2,1,0:T(8,128)(2,1)}, bf16[8,512,256]{2,1,0:T(8,128)(2,1)}, u32[]{:S(2)}, u32[]{:S(2)}) collective-permute-start(bf16[8,512,256]{2,1,0:T(8,128)(2,1)} %turn.1.own_ref), channel_id=1, source_target_pairs={{0,1},{1,0},{2,3},{3,2},{4,5},{5,4},{6,7},{7,6},{8,9},{9,8},{10,11... | collective-permute-start | bytes 6291464 | tf_op jit(solution)/shard_map/turn/ppermute | solution.py:31
  144.2 16.7 %all-to-all-start.3 = ((bf16[32,8,256]{2,1,0:T(8,128)(2,1)}), bf16[32,8,256]{2,1,0:T(8,128)(2,1)S(1)}, u32[]{:S(2)}, u32[]{:S(2)}) async-start(bf16[32,8,256]{2,1,0:T(8,128)(2,1)} %broadcast_in_dim.4), calls=%async_computation.3 | async-start | bytes 262144 | tf_op jit(solution)/shard_map/gather_row/all_to_all | solution.py:271
  160.9 8.5 %collective-permute-start.9 = (bf16[32,8,256]{2,1,0:T(8,128)(2,1)S(1)}, bf16[32,8,256]{2,1,0:T(8,128)(2,1)S(1)}, u32[]{:S(2)}, u32[]{:S(2)}) collective-permute-start(bf16[32,8,256]{2,1,0:T(8,128)(2,1)S(1)} %all-to-all-done.3.refs_0_), channel_id=1, source_target_pairs={{0,2},{2,0},{4,6},{6,4},{1,3},{3,1},{5,7},{7,5},{8,10},{10,8},{12,... | collective-permute-start | bytes 393224 | tf_op jit(solution)/shard_map/gather_x/ppermute | solution.py:31
  161.2 8.2 %collective-permute-start.11 = (bf16[32,8,256]{2,1,0:T(8,128)(2,1)S(1)}, bf16[32,8,256]{2,1,0:T(8,128)(2,1)S(1)}, u32[]{:S(2)}, u32[]{:S(2)}) collective-permute-start(bf16[32,8,256]{2,1,0:T(8,128)(2,1)S(1)} %all-to-all-done.3.refs_0_), channel_id=1, source_target_pairs={{0,4},{2,6},{4,0},{6,2},{1,5},{3,7},{5,1},{7,3},{8,12},{10,14},{12... | collective-permute-start | bytes 393224 | tf_op jit(solution)/shard_map/gather_x/ppermute | solution.py:31
  162.5 8.4 %collective-permute-start.13 = (bf16[32,8,256]{2,1,0:T(8,128)(2,1)S(1)}, bf16[32,8,256]{2,1,0:T(8,128)(2,1)S(1)}, u32[]{:S(2)}, u32[]{:S(2)}) collective-permute-start(bf16[32,8,256]{2,1,0:T(8,128)(2,1)S(1)} %all-to-all-done.3.refs_0_), channel_id=1, source_target_pairs={{0,6},{2,4},{4,2},{6,0},{1,7},{3,5},{5,3},{7,1},{8,14},{10,12},{12... | collective-permute-start | bytes 393224 | tf_op jit(solution)/shard_map/gather_x/ppermute | solution.py:31
  165.5 8.1 %collective-permute-start.8 = (bf16[32,8,256]{2,1,0:T(8,128)(2,1)S(1)}, bf16[32,8,256]{2,1,0:T(8,128)(2,1)S(1)}, u32[]{:S(2)}, u32[]{:S(2)}) collective-permute-start(bf16[32,8,256]{2,1,0:T(8,128)(2,1)S(1)} %all-to-all-done.3.refs_0_), channel_id=1, source_target_pairs={{0,1},{1,0},{2,3},{3,2},{4,5},{5,4},{6,7},{7,6},{8,9},{9,8},{10,11... | collective-permute-start | bytes 393224 | tf_op jit(solution)/shard_map/gather_e/ppermute | solution.py:31
  169.4 4.3 %collective-permute-start.10 = (bf16[32,8,256]{2,1,0:T(8,128)(2,1)S(1)}, bf16[32,8,256]{2,1,0:T(8,128)(2,1)S(1)}, u32[]{:S(2)}, u32[]{:S(2)}) collective-permute-start(bf16[32,8,256]{2,1,0:T(8,128)(2,1)S(1)} %collective-permute-done.9.refs_2_), channel_id=1, source_target_pairs={{0,1},{1,0},{2,3},{3,2},{4,5},{5,4},{6,7},{7,6},{8,9},{9,8},{10,11... | collective-permute-start | bytes 393224 | tf_op jit(solution)/shard_map/gather_e/ppermute | solution.py:31
  169.5 4.2 %collective-permute-start.12 = (bf16[32,8,256]{2,1,0:T(8,128)(2,1)S(1)}, bf16[32,8,256]{2,1,0:T(8,128)(2,1)S(1)}, u32[]{:S(2)}, u32[]{:S(2)}) collective-permute-start(bf16[32,8,256]{2,1,0:T(8,128)(2,1)S(1)} %collective-permute-done.11.refs_4_), channel_id=1, source_target_pairs={{0,1},{1,0},{2,3},{3,2},{4,5},{5,4},{6,7},{7,6},{8,9},{9,8},{10,11... | collective-permute-start | bytes 393224 | tf_op jit(solution)/shard_map/gather_e/ppermute | solution.py:31
  170.9 2.8 %collective-permute-start.14 = (bf16[32,8,256]{2,1,0:T(8,128)(2,1)S(1)}, bf16[32,8,256]{2,1,0:T(8,128)(2,1)S(1)}, u32[]{:S(2)}, u32[]{:S(2)}) collective-permute-start(bf16[32,8,256]{2,1,0:T(8,128)(2,1)S(1)} %collective-permute-done.13.refs_6_), channel_id=1, source_target_pairs={{0,1},{1,0},{2,3},{3,2},{4,5},{5,4},{6,7},{7,6},{8,9},{9,8},{10,11... | collective-permute-start | bytes 393224 | tf_op jit(solution)/shard_map/gather_e/ppermute | solution.py:31

commit v6 on v5

--- a/solution.py
+++ b/solution.py
@@ -202,7 +202,7 @@
         for half in range(2):
             for z in range(NZ):
                 for y in range(NY):
-                    env[half, y, block + z * NX] = ref[(half * NZ + z) * NY + y]
+                    env[half, y, block + z * NX] = ref[(z * 2 + half) * NY + y]
     for part in range(2):
         at = slice(part * 256, part * 256 + 256)
         one = env[0, part].reshape(512, 256)
@@ -268,7 +268,7 @@
         env = jnp.sum(parts.astype(F32), axis=0).astype(BF)
     with jax.named_scope("gather_row"):
         env = jnp.broadcast_to(env, (2 * NZ * NY, 8, 256))
-        env = lax.all_to_all(env, ("half",) + ROW, 0, 0, tiled=True)
+        env = lax.all_to_all(env, ("z", "half", "y"), 0, 0, tiled=True)
     with jax.named_scope("gather_x"):
         far = swap(env, ("x",), 2)
         across = [env, swap(env, ("x",), 1), far, swap(env, ("x",), 3)]

time: 177 us -> 177 us (level)
  transfers between devices with their start and end apart: 18 -> 18, of which waited for: 9 -> 9; matrix products, arithmetic and copies ran while one was open for 2% -> 2% of each run, Pallas kernels for 9% -> 10%
where the time goes in v6:
time: 177 us; the launch traced here: 176 us
  waiting for transfers between devices  77.5 us (44%)
  starting transfers between devices  51.3 us (29%)
  Pallas kernels  26.5 us (15%)
  blocking collectives  16.8 us (9%)
  local copies, waits for them, and re-layouts  2 us (1%)
    all_to_all x1, waiting for transfers between devices, on_device(): lax.all_to_all(summed.reshape(128, 32, 256), ROW_COL, 0, 0, tiled=True)  44.6 us
    ppermute x15, starting transfers between devices, swap(): return lax.ppermute(value, axes, [(i, i ^ offset) for i in range(peers)])  23.9 us
    ppermute x15, waiting for transfers between devices, swap(): return lax.ppermute(value, axes, [(i, i ^ offset) for i in range(peers)])  20.7 us
    all_to_all x1, blocking collectives, on_device(): lax.all_to_all(part.reshape(64, 8, 256), ('z', 'y', 'x'), 0, 0, tiled=True)  16.8 us
    pallas_call x1, Pallas kernels, apply_terms(): pl.pallas_call(terms_kernel, out_shape=jax.ShapeDtypeStruct((NZ, NY, NX,...  11.5 us
    all_to_all x1, starting transfers between devices, on_device(): lax.all_to_all(summed.reshape(128, 32, 256), ROW_COL, 0, 0, tiled=True)  10.4 us
    all_to_all x1, starting transfers between devices, on_device(): child_all = lax.all_to_all(cut, ROW, 0, 0, tiled=True)  10.3 us
    all_to_all x1, waiting for transfers between devices, on_device(): env = lax.all_to_all(env, ('z', 'half', 'y'), 0, 0, tiled=True)  9.19 us
  transfers between devices with their start and end apart: 18, of which 9 were waited for; matrix products, arithmetic and copies ran while one was open for 2% of the time, Pallas kernels for 10%

profile of v6, /device:TPU:1, one launch (start us, length us, event | category | flops | bytes accessed | tf_op | source)
XLA Modules:
  0.0 176.1 jit_solution(6163795658002357521)
XLA Ops:
  0.0 2.7 %cut.1 = bf16[16,32,8,256]{3,2,1,0:T(8,128)(2,1)} custom-call(bf16[32,64,512]{2,1,0:T(8,128)(2,1)} %bitcast.41), custom_call_target="tpu_custom_call" | custom-call | tf_op jit(solution)/shard_map/child_rows/cut/pallas_call | solution.py:54
  2.7 0.0 copy-start.2
  2.7 10.3 %all-to-all-start.1 = ((bf16[16,256,256]{2,1,0:T(8,128)(2,1)}), bf16[16,256,256]{2,1,0:T(8,128)(2,1)}, u32[]{:S(2)}, u32[]{:S(2)}) async-start(bf16[16,256,256]{2,1,0:T(8,128)(2,1)} %bitcast.43), calls=%async_computation.1 | async-start | bytes 4194304 | tf_op jit(solution)/shard_map/child_rows/all_to_all | solution.py:246
  13.1 0.0 copy-start.3
  13.1 0.0 copy-start.1
  13.1 1.1 dynamic-slice_bitcast_fusion
  14.2 1.0 collective-permute-start
  15.2 1.2 collective-permute-start.1
  16.4 0.4 collective-permute-start.2
  16.8 2.7 %collective-permute-start.3 = (bf16[4,64,512]{2,1,0:T(8,128)(2,1)}, bf16[4,64,512]{2,1,0:T(8,128)(2,1)S(1)}, u32[]{:S(2)}, u32[]{:S(2)}) collective-permute-start(bf16[4,64,512]{2,1,0:T(8,128)(2,1)} %get-tuple-element.8), channel_id=1, source_target_pairs={{0,4},{1,5},{2,6},{3,7},{4,0},{5,1},{6,2},{7,3},{8,12},{9,13},{10,... | collective-permute-start | bytes 786440 | tf_op jit(solution)/shard_map/child_first_leg/ppermute | solution.py:31
  19.5 0.6 collective-permute-start.4
  20.1 0.0 collective-permute-done.refs_1_
  20.2 2.5 %collective-permute-start.5 = (bf16[4,64,512]{2,1,0:T(8,128)(2,1)}, bf16[4,64,512]{2,1,0:T(8,128)(2,1)S(1)}, u32[]{:S(2)}, u32[]{:S(2)}) collective-permute-start(bf16[4,64,512]{2,1,0:T(8,128)(2,1)} %get-tuple-element.6), channel_id=1, source_target_pairs={{0,6},{1,7},{2,4},{3,5},{4,2},{5,3},{6,0},{7,1},{8,14},{9,15},{10,... | collective-permute-start | bytes 786440 | tf_op jit(solution)/shard_map/child_first_leg/ppermute | solution.py:31
  22.6 0.6 collective-permute-done.1.refs_2_
  23.2 3.4 %collective-permute-start.6 = (bf16[4,64,512]{2,1,0:T(8,128)(2,1)}, bf16[4,64,512]{2,1,0:T(8,128)(2,1)S(1)}, u32[]{:S(2)}, u32[]{:S(2)}) collective-permute-start(bf16[4,64,512]{2,1,0:T(8,128)(2,1)} %get-tuple-element.5), channel_id=1, source_target_pairs={{0,7},{1,6},{2,5},{3,4},{4,3},{5,2},{6,1},{7,0},{8,15},{9,14},{10,... | collective-permute-start | bytes 786440 | tf_op jit(solution)/shard_map/child_first_leg/ppermute | solution.py:31
  26.6 0.1 copy.9.site
  26.7 0.1 pad_add_fusion.me
  26.8 2.8 %collective-permute-done.2.refs_3_ = bf16[4,64,512]{2,1,0:T(8,128)(2,1)S(1)} collective-permute-done((bf16[4,64,512]{2,1,0:T(8,128)(2,1)}, bf16[4,64,512]{2,1,0:T(8,128)(2,1)S(1)}, u32[]{:S(2)}, u32[]{:S(2)}) %collective-permute-start.2) | collective-permute-done | bytes 262176 | tf_op jit(solution)/shard_map/child_first_leg/ppermute | solution.py:31
  29.6 7.1 %collective-permute-done.3.refs_4_ = bf16[4,64,512]{2,1,0:T(8,128)(2,1)S(1)} collective-permute-done((bf16[4,64,512]{2,1,0:T(8,128)(2,1)}, bf16[4,64,512]{2,1,0:T(8,128)(2,1)S(1)}, u32[]{:S(2)}, u32[]{:S(2)}) %collective-permute-start.3) | collective-permute-done | bytes 262176 | tf_op jit(solution)/shard_map/child_first_leg/ppermute | solution.py:31
  36.7 5.7 %collective-permute-done.4.refs_5_ = bf16[4,64,512]{2,1,0:T(8,128)(2,1)S(1)} collective-permute-done((bf16[4,64,512]{2,1,0:T(8,128)(2,1)}, bf16[4,64,512]{2,1,0:T(8,128)(2,1)S(1)}, u32[]{:S(2)}, u32[]{:S(2)}) %collective-permute-start.4) | collective-permute-done | bytes 262176 | tf_op jit(solution)/shard_map/child_first_leg/ppermute | solution.py:31
  42.3 0.0 collective-permute-done.5.refs_6_
  42.3 4.5 %collective-permute-done.6.refs_7_ = bf16[4,64,512]{2,1,0:T(8,128)(2,1)S(1)} collective-permute-done((bf16[4,64,512]{2,1,0:T(8,128)(2,1)}, bf16[4,64,512]{2,1,0:T(8,128)(2,1)S(1)}, u32[]{:S(2)}, u32[]{:S(2)}) %collective-permute-start.6) | collective-permute-done | bytes 262176 | tf_op jit(solution)/shard_map/child_first_leg/ppermute | solution.py:31
  46.9 11.5 %terms.1 = bf16[8,2,4,2,2,2,8,256]{7,6,5,4,3,2,1,0:T(8,128)(2,1)} custom-call(s32[2]{0:T(128)S(1)} %pad_add_fusion.me, s32[5,2]{1,0:T(8,128)S(1)} %copy.9.site, s32[5]{0:T(128)S(1)} %bitcast.40, bf16[2,4,512,512]{3,2,1,0:T(8,128)(2,1)} %bitcast.45, bf16[4,64,512]{2,1,0:T(8,128)(2,1)S(1)} %get-tuple-element.12.refs_0_, ...), custom_call_target="tpu_custom_call" | custom-call | tf_op jit(solution)/shard_map/terms/terms/pallas_call | solution.py:132
  58.4 3.0 %all-to-all-done.1 = bf16[16,256,256]{2,1,0:T(8,128)(2,1)} async-done(((bf16[16,256,256]{2,1,0:T(8,128)(2,1)}), bf16[16,256,256]{2,1,0:T(8,128)(2,1)}, u32[]{:S(2)}, u32[]{:S(2)}) %all-to-all-start.1) | async-done | bytes 2097184 | tf_op jit(solution)/shard_map/child_rows/all_to_all | solution.py:246
  61.4 10.4 %all-to-all-start = ((bf16[128,32,256]{2,1,0:T(8,128)(2,1)}), bf16[128,32,256]{2,1,0:T(8,128)(2,1)S(1)}, u32[]{:S(2)}, u32[]{:S(2)}) async-start(bf16[128,32,256]{2,1,0:T(8,128)(2,1)} %bitcast.44), calls=%async_computation | async-start | bytes 4194304 | tf_op jit(solution)/shard_map/summed_rows/all_to_all | solution.py:259
  71.7 5.8 %turn.1.own_ref = bf16[8,512,256]{2,1,0:T(8,128)(2,1)} custom-call(bf16[512,8,256]{2,1,0:T(8,128)(2,1)} %bitcast.21.in_ref), custom_call_target="tpu_custom_call" | custom-call | tf_op jit(solution)/shard_map/turn/turn/pallas_call | solution.py:156
  77.6 0.9 collective-permute-start.7
  78.5 44.6 %all-to-all-done = bf16[128,32,256]{2,1,0:T(8,128)(2,1)S(1)} async-done(((bf16[128,32,256]{2,1,0:T(8,128)(2,1)}), bf16[128,32,256]{2,1,0:T(8,128)(2,1)S(1)}, u32[]{:S(2)}, u32[]{:S(2)}) %all-to-all-start) | async-done | bytes 2097184 | tf_op jit(solution)/shard_map/summed_rows/all_to_all | solution.py:259
  123.1 3.6 %gram.1 = bf16[8,2,4,8,256]{4,3,2,1,0:T(8,128)(2,1)S(1)} custom-call(s32[2]{0:T(128)S(1)} %pad_add_fusion.me, bf16[128,2,2,8,256]{4,3,2,1,0:T(8,128)(2,1)S(1)} %bitcast.38, bf16[8,512,256]{2,1,0:T(8,128)(2,1)} %turn.1.own_ref, bf16[8,512,256]{2,1,0:T(8,128)(2,1)} %collective-permute-done.7.other_ref), custom_call_target="tpu_custom_call" | custom-call | tf_op jit(solution)/shard_map/gram/gram/pallas_call | solution.py:185
  126.7 16.8 %all_to_all.20 = bf16[64,8,256]{2,1,0:T(8,128)(2,1)S(1)} all-to-all(bf16[64,8,256]{2,1,0:T(8,128)(2,1)S(1)} %bitcast.39), channel_id=1, replica_groups=mesh['half'=2,'z'=8,'y'=2,'x'=4,'e'=2] {'z','y','x'}, dimensions={0} | all-to-all | bytes 524288 | tf_op jit(solution)/shard_map/sum/all_to_all | solution.py:267
  143.5 0.1 reduce_sum.12
  143.6 0.7 broadcast_in_dim.4
  144.2 6.7 %all-to-all-start.3 = ((bf16[32,8,256]{2,1,0:T(8,128)(2,1)}), bf16[32,8,256]{2,1,0:T(8,128)(2,1)S(1)}, u32[]{:S(2)}, u32[]{:S(2)}) async-start(bf16[32,8,256]{2,1,0:T(8,128)(2,1)} %broadcast_in_dim.4), calls=%async_computation.3 | async-start | bytes 262144 | tf_op jit(solution)/shard_map/gather_row/all_to_all | solution.py:271
  151.0 0.1 reshape.75
  151.1 9.2 %all-to-all-done.3.refs_0_ = bf16[32,8,256]{2,1,0:T(8,128)(2,1)S(1)} async-done(((bf16[32,8,256]{2,1,0:T(8,128)(2,1)}), bf16[32,8,256]{2,1,0:T(8,128)(2,1)S(1)}, u32[]{:S(2)}, u32[]{:S(2)}) %all-to-all-start.3) | async-done | bytes 131104 | tf_op jit(solution)/shard_map/gather_row/all_to_all | solution.py:271
  160.3 0.4 collective-permute-start.9
  160.6 1.3 collective-permute-start.11
  161.9 2.2 %collective-permute-start.13 = (bf16[32,8,256]{2,1,0:T(8,128)(2,1)S(1)}, bf16[32,8,256]{2,1,0:T(8,128)(2,1)S(1)}, u32[]{:S(2)}, u32[]{:S(2)}) collective-permute-start(bf16[32,8,256]{2,1,0:T(8,128)(2,1)S(1)} %all-to-all-done.3.refs_0_), channel_id=1, source_target_pairs={{0,6},{2,4},{4,2},{6,0},{1,7},{3,5},{5,3},{7,1},{8,14},{10,12},{12... | collective-permute-start | bytes 393224 | tf_op jit(solution)/shard_map/gather_x/ppermute | solution.py:31
  164.1 0.7 fusion.rows_ref
  164.9 4.0 %collective-permute-start.8 = (bf16[32,8,256]{2,1,0:T(8,128)(2,1)S(1)}, bf16[32,8,256]{2,1,0:T(8,128)(2,1)S(1)}, u32[]{:S(2)}, u32[]{:S(2)}) collective-permute-start(bf16[32,8,256]{2,1,0:T(8,128)(2,1)S(1)} %all-to-all-done.3.refs_0_), channel_id=1, source_target_pairs={{0,1},{1,0},{2,3},{3,2},{4,5},{5,4},{6,7},{7,6},{8,9},{9,8},{10,11... | collective-permute-start | bytes 393224 | tf_op jit(solution)/shard_map/gather_e/ppermute | solution.py:31
  168.9 0.0 collective-permute-done.9.refs_2_
  168.9 0.1 collective-permute-start.10
  169.0 1.3 collective-permute-start.12
  170.4 1.8 %collective-permute-start.14 = (bf16[32,8,256]{2,1,0:T(8,128)(2,1)S(1)}, bf16[32,8,256]{2,1,0:T(8,128)(2,1)S(1)}, u32[]{:S(2)}, u32[]{:S(2)}) collective-permute-start(bf16[32,8,256]{2,1,0:T(8,128)(2,1)S(1)} %collective-permute-done.13.refs_6_), channel_id=1, source_target_pairs={{0,1},{1,0},{2,3},{3,2},{4,5},{5,4},{6,7},{7,6},{8,9},{9,8},{10,11... | collective-permute-start | bytes 393224 | tf_op jit(solution)/shard_map/gather_e/ppermute | solution.py:31
  172.2 0.9 fusion.1.cols_ref
  173.1 0.0 collective-permute-done.10.refs_3_
  173.1 0.1 collective-permute-done.14.refs_7_
  173.2 2.9 %final.1 = bf16[2,512,512]{2,1,0:T(8,128)(2,1)} custom-call(s32[2]{0:T(128)S(1)} %pad_add_fusion.me, bf16[2,512,512]{2,1,0:T(8,128)(2,1)S(1)} %fusion.rows_ref, bf16[2,512,512]{2,1,0:T(8,128)(2,1)S(1)} %fusion.1.cols_ref, bf16[32,8,256]{2,1,0:T(8,128)(2,1)S(1)} %all-to-all-done.3.refs_0_, bf16[32,8,256]{2,1,0:T(8,128)(2,1)S(1)} %collective-permute-done.8.refs_1_, ...), custom_call_target="tpu_custom_call" | custom-call | tf_op jit(solution)/shard_map/final/final/pallas_call | solution.py:219
  (11 shorter events, 0.0 us)
Async XLA Ops:
  0.0 164.1 %copy-start = (bf16[2,512,512]{2,1,0:T(8,128)(2,1)S(1)}, bf16[2,512,512]{2,1,0:T(8,128)(2,1)}, u32[]{:S(2)}) copy-start(bf16[2,512,512]{2,1,0:T(8,128)(2,1)} %param.9) | copy-start | bytes 3145732
  2.7 10.4 %copy-start.2 = (bf16[1,32,64,512]{3,2,1,0:T(8,128)(2,1)S(1)}, bf16[1,32,64,512]{3,2,1,0:T(8,128)(2,1)}, u32[]{:S(2)}) copy-start(bf16[1,32,64,512]{3,2,1,0:T(8,128)(2,1)} %param.5) | copy-start | bytes 6291460
  2.7 58.7 %all-to-all-start.1 = ((bf16[16,256,256]{2,1,0:T(8,128)(2,1)}), bf16[16,256,256]{2,1,0:T(8,128)(2,1)}, u32[]{:S(2)}, u32[]{:S(2)}) async-start(bf16[16,256,256]{2,1,0:T(8,128)(2,1)} %bitcast.43), calls=%async_computation.1 | async-start | bytes 4194304 | tf_op jit(solution)/shard_map/child_rows/all_to_all | solution.py:246
  13.1 13.5 %copy-start.3 = (s32[1,5,2]{1,2,0:T(2,128)S(1)}, s32[1,5,2]{1,2,0:T(2,128)}, u32[]{:S(2)}) copy-start(s32[1,5,2]{1,2,0:T(2,128)} %param.7) | copy-start | bytes 124
  13.1 33.8 %copy-start.1 = (s32[1,5]{1,0:T(1,128)S(1)}, s32[1,5]{1,0:T(1,128)}, u32[]{:S(2)}) copy-start(s32[1,5]{1,0:T(1,128)} %param.8) | copy-start | bytes 64
  14.2 6.0 %collective-permute-start = (bf16[4,64,512]{2,1,0:T(8,128)(2,1)S(1)}, bf16[4,64,512]{2,1,0:T(8,128)(2,1)S(1)}, u32[]{:S(2)}, u32[]{:S(2)}) collective-permute-start(bf16[4,64,512]{2,1,0:T(8,128)(2,1)S(1)} %get-tuple-element.11), channel_id=1, source_target_pairs={{0,1},{1,0},{2,3},{3,2},{4,5},{5,4},{6,7},{7,6},{8,9},{9,8},{10,11... | collective-permute-start | bytes 786440 | tf_op jit(solution)/shard_map/child_first_leg/ppermute | solution.py:31
  15.2 8.0 %collective-permute-start.1 = (bf16[4,64,512]{2,1,0:T(8,128)(2,1)S(1)}, bf16[4,64,512]{2,1,0:T(8,128)(2,1)S(1)}, u32[]{:S(2)}, u32[]{:S(2)}) collective-permute-start(bf16[4,64,512]{2,1,0:T(8,128)(2,1)S(1)} %get-tuple-element.10), channel_id=1, source_target_pairs={{0,2},{1,3},{2,0},{3,1},{4,6},{5,7},{6,4},{7,5},{8,10},{9,11},{10,... | collective-permute-start | bytes 786440 | tf_op jit(solution)/shard_map/child_first_leg/ppermute | solution.py:31
  16.4 13.2 %collective-permute-start.2 = (bf16[4,64,512]{2,1,0:T(8,128)(2,1)}, bf16[4,64,512]{2,1,0:T(8,128)(2,1)S(1)}, u32[]{:S(2)}, u32[]{:S(2)}) collective-permute-start(bf16[4,64,512]{2,1,0:T(8,128)(2,1)} %get-tuple-element.9), channel_id=1, source_target_pairs={{0,3},{1,2},{2,1},{3,0},{4,7},{5,6},{6,5},{7,4},{8,11},{9,10},{10,... | collective-permute-start | bytes 786440 | tf_op jit(solution)/shard_map/child_first_leg/ppermute | solution.py:31
  16.8 19.9 %collective-permute-start.3 = (bf16[4,64,512]{2,1,0:T(8,128)(2,1)}, bf16[4,64,512]{2,1,0:T(8,128)(2,1)S(1)}, u32[]{:S(2)}, u32[]{:S(2)}) collective-permute-start(bf16[4,64,512]{2,1,0:T(8,128)(2,1)} %get-tuple-element.8), channel_id=1, source_target_pairs={{0,4},{1,5},{2,6},{3,7},{4,0},{5,1},{6,2},{7,3},{8,12},{9,13},{10,... | collective-permute-start | bytes 786440 | tf_op jit(solution)/shard_map/child_first_leg/ppermute | solution.py:31
  19.5 22.8 %collective-permute-start.4 = (bf16[4,64,512]{2,1,0:T(8,128)(2,1)}, bf16[4,64,512]{2,1,0:T(8,128)(2,1)S(1)}, u32[]{:S(2)}, u32[]{:S(2)}) collective-permute-start(bf16[4,64,512]{2,1,0:T(8,128)(2,1)} %get-tuple-element.7), channel_id=1, source_target_pairs={{0,5},{1,4},{2,7},{3,6},{4,1},{5,0},{6,3},{7,2},{8,13},{9,12},{10,... | collective-permute-start | bytes 786440 | tf_op jit(solution)/shard_map/child_first_leg/ppermute | solution.py:31
  20.2 22.2 %collective-permute-start.5 = (bf16[4,64,512]{2,1,0:T(8,128)(2,1)}, bf16[4,64,512]{2,1,0:T(8,128)(2,1)S(1)}, u32[]{:S(2)}, u32[]{:S(2)}) collective-permute-start(bf16[4,64,512]{2,1,0:T(8,128)(2,1)} %get-tuple-element.6), channel_id=1, source_target_pairs={{0,6},{1,7},{2,4},{3,5},{4,2},{5,3},{6,0},{7,1},{8,14},{9,15},{10,... | collective-permute-start | bytes 786440 | tf_op jit(solution)/shard_map/child_first_leg/ppermute | solution.py:31
  23.2 23.7 %collective-permute-start.6 = (bf16[4,64,512]{2,1,0:T(8,128)(2,1)}, bf16[4,64,512]{2,1,0:T(8,128)(2,1)S(1)}, u32[]{:S(2)}, u32[]{:S(2)}) collective-permute-start(bf16[4,64,512]{2,1,0:T(8,128)(2,1)} %get-tuple-element.5), channel_id=1, source_target_pairs={{0,7},{1,6},{2,5},{3,4},{4,3},{5,2},{6,1},{7,0},{8,15},{9,14},{10,... | collective-permute-start | bytes 786440 | tf_op jit(solution)/shard_map/child_first_leg/ppermute | solution.py:31
  61.4 61.7 %all-to-all-start = ((bf16[128,32,256]{2,1,0:T(8,128)(2,1)}), bf16[128,32,256]{2,1,0:T(8,128)(2,1)S(1)}, u32[]{:S(2)}, u32[]{:S(2)}) async-start(bf16[128,32,256]{2,1,0:T(8,128)(2,1)} %bitcast.44), calls=%async_computation | async-start | bytes 4194304 | tf_op jit(solution)/shard_map/summed_rows/all_to_all | solution.py:259
  77.6 45.5 %collective-permute-start.7 = (bf16[8,512,256]{2,1,0:T(8,128)(2,1)}, bf16[8,512,256]{2,1,0:T(8,128)(2,1)}, u32[]{:S(2)}, u32[]{:S(2)}) collective-permute-start(bf16[8,512,256]{2,1,0:T(8,128)(2,1)} %turn.1.own_ref), channel_id=1, source_target_pairs={{0,1},{1,0},{2,3},{3,2},{4,5},{5,4},{6,7},{7,6},{8,9},{9,8},{10,11... | collective-permute-start | bytes 6291464 | tf_op jit(solution)/shard_map/turn/ppermute | solution.py:31
  144.2 16.1 %all-to-all-start.3 = ((bf16[32,8,256]{2,1,0:T(8,128)(2,1)}), bf16[32,8,256]{2,1,0:T(8,128)(2,1)S(1)}, u32[]{:S(2)}, u32[]{:S(2)}) async-start(bf16[32,8,256]{2,1,0:T(8,128)(2,1)} %broadcast_in_dim.4), calls=%async_computation.3 | async-start | bytes 262144 | tf_op jit(solution)/shard_map/gather_row/all_to_all | solution.py:271
  160.3 8.6 %collective-permute-start.9 = (bf16[32,8,256]{2,1,0:T(8,128)(2,1)S(1)}, bf16[32,8,256]{2,1,0:T(8,128)(2,1)S(1)}, u32[]{:S(2)}, u32[]{:S(2)}) collective-permute-start(bf16[32,8,256]{2,1,0:T(8,128)(2,1)S(1)} %all-to-all-done.3.refs_0_), channel_id=1, source_target_pairs={{0,2},{2,0},{4,6},{6,4},{1,3},{3,1},{5,7},{7,5},{8,10},{10,8},{12,... | collective-permute-start | bytes 393224 | tf_op jit(solution)/shard_map/gather_x/ppermute | solution.py:31
  160.6 8.4 %collective-permute-start.11 = (bf16[32,8,256]{2,1,0:T(8,128)(2,1)S(1)}, bf16[32,8,256]{2,1,0:T(8,128)(2,1)S(1)}, u32[]{:S(2)}, u32[]{:S(2)}) collective-permute-start(bf16[32,8,256]{2,1,0:T(8,128)(2,1)S(1)} %all-to-all-done.3.refs_0_), channel_id=1, source_target_pairs={{0,4},{2,6},{4,0},{6,2},{1,5},{3,7},{5,1},{7,3},{8,12},{10,14},{12... | collective-permute-start | bytes 393224 | tf_op jit(solution)/shard_map/gather_x/ppermute | solution.py:31
  161.9 8.4 %collective-permute-start.13 = (bf16[32,8,256]{2,1,0:T(8,128)(2,1)S(1)}, bf16[32,8,256]{2,1,0:T(8,128)(2,1)S(1)}, u32[]{:S(2)}, u32[]{:S(2)}) collective-permute-start(bf16[32,8,256]{2,1,0:T(8,128)(2,1)S(1)} %all-to-all-done.3.refs_0_), channel_id=1, source_target_pairs={{0,6},{2,4},{4,2},{6,0},{1,7},{3,5},{5,3},{7,1},{8,14},{10,12},{12... | collective-permute-start | bytes 393224 | tf_op jit(solution)/shard_map/gather_x/ppermute | solution.py:31
  164.9 8.2 %collective-permute-start.8 = (bf16[32,8,256]{2,1,0:T(8,128)(2,1)S(1)}, bf16[32,8,256]{2,1,0:T(8,128)(2,1)S(1)}, u32[]{:S(2)}, u32[]{:S(2)}) collective-permute-start(bf16[32,8,256]{2,1,0:T(8,128)(2,1)S(1)} %all-to-all-done.3.refs_0_), channel_id=1, source_target_pairs={{0,1},{1,0},{2,3},{3,2},{4,5},{5,4},{6,7},{7,6},{8,9},{9,8},{10,11... | collective-permute-start | bytes 393224 | tf_op jit(solution)/shard_map/gather_e/ppermute | solution.py:31
  168.9 4.2 %collective-permute-start.10 = (bf16[32,8,256]{2,1,0:T(8,128)(2,1)S(1)}, bf16[32,8,256]{2,1,0:T(8,128)(2,1)S(1)}, u32[]{:S(2)}, u32[]{:S(2)}) collective-permute-start(bf16[32,8,256]{2,1,0:T(8,128)(2,1)S(1)} %collective-permute-done.9.refs_2_), channel_id=1, source_target_pairs={{0,1},{1,0},{2,3},{3,2},{4,5},{5,4},{6,7},{7,6},{8,9},{9,8},{10,11... | collective-permute-start | bytes 393224 | tf_op jit(solution)/shard_map/gather_e/ppermute | solution.py:31
  169.0 4.1 %collective-permute-start.12 = (bf16[32,8,256]{2,1,0:T(8,128)(2,1)S(1)}, bf16[32,8,256]{2,1,0:T(8,128)(2,1)S(1)}, u32[]{:S(2)}, u32[]{:S(2)}) collective-permute-start(bf16[32,8,256]{2,1,0:T(8,128)(2,1)S(1)} %collective-permute-done.11.refs_4_), channel_id=1, source_target_pairs={{0,1},{1,0},{2,3},{3,2},{4,5},{5,4},{6,7},{7,6},{8,9},{9,8},{10,11... | collective-permute-start | bytes 393224 | tf_op jit(solution)/shard_map/gather_e/ppermute | solution.py:31
  170.4 2.8 %collective-permute-start.14 = (bf16[32,8,256]{2,1,0:T(8,128)(2,1)S(1)}, bf16[32,8,256]{2,1,0:T(8,128)(2,1)S(1)}, u32[]{:S(2)}, u32[]{:S(2)}) collective-permute-start(bf16[32,8,256]{2,1,0:T(8,128)(2,1)S(1)} %collective-permute-done.13.refs_6_), channel_id=1, source_target_pairs={{0,1},{1,0},{2,3},{3,2},{4,5},{5,4},{6,7},{7,6},{8,9},{9,8},{10,11... | collective-permute-start | bytes 393224 | tf_op jit(solution)/shard_map/gather_e/ppermute | solution.py:31
